TPU v7x, 512 devices: a whole 4x8x8 slice. The times are simulated.
512 devices in a mesh: section: 8 (over x, core), expert: 64 (over z, y).
Axes of the slice: x: 4, y: 8, z: 8, core: 2. Of those that a mesh axis runs over, the one named last changes fastest.
Arguments:
- histories: bfloat16 [8, 8192, 5120], P('section', 'expert'), may hold values from -6 to 6
- page_map: int32 [8, 2, 2048], P('section', None, 'expert'), may hold values from 0 to 2047, as said below
- user_pages: int32 [8, 64, 4], P('section', 'expert'), may hold values from 1 to 16, 32 in all within a row
- tails: int32 [8, 64, 4], P('section', 'expert'), may hold values from 1 to 4
- routes: int32 [8, 8192, 2], P('section', 'expert'), may hold values from 0 to 31, all different within a row; in each aligned block of 128 rows (0 to 127, 128 to 255, ..., all dimensions but the last counted through in order) at most 16 rows name the same one
- out_proj: bfloat16 [8, 1024, 1024], P('section', 'expert'), may hold values from -0.1875 to 0.1875
- router: bfloat16 [8, 1024, 32], P('section'), may hold values from -0.75 to 0.75
- w_gate: bfloat16 [8, 1024, 32768], P('section', None, 'expert'), may hold values from -0.1875 to 0.1875
- w_up: bfloat16 [8, 1024, 32768], P('section', None, 'expert'), may hold values from -0.1875 to 0.1875
- w_down: bfloat16 [8, 32768, 1024], P('section', 'expert'), may hold values from -0.1875 to 0.1875
Outputs:
- handed: bfloat16 [8, 8192, 1024], P('section', 'expert')
Inputs may be any that keep to these rules, and one draw needn't show every extreme that they name: page_map[0] is a permutation of the pages of a section and page_map[1] its inverse; every device holds exactly 32 pages before and after; no device's pages send more than 1 pages to one device, and some send exactly 1. `user_pages`: the 4 entries of one device sum to 32, and the largest is 16. `routes`: A row names 2 different experts; among the rows of one device, no expert is named more than 16 times, a bound that some block reaches.
All inputs are finite; a program needn't handle non-finite values.
Results may differ from a plain program's by a relative error of at most 0.012.
Values may be sent and summed in bfloat16 or wider, within the bound.
No kernel may reach another device: no remote copies, remote signals or barrier semaphores. Data moves between devices by JAX's collectives and lax.ppermute only.
A program may use at most 64 MiB of HBM per device.

v0:
```python
import jax
import jax.numpy as jnp
from jax import lax
from jax.sharding import PartitionSpec as P

HEADS = 8


def swapped(shard, axis, apart):
    return lax.ppermute(shard, axis, [(i, i ^ 1 << apart) for i in range(lax.axis_size(axis))])


def from_behind(block, axis, distance):
    devices = range(lax.axis_size(axis))
    route = [((i - distance) % len(devices), i) for i in devices]
    return lax.ppermute(block, axis, route)


def layout_rows(counts, tail_rows, page_rows, row_count):
    starting = jnp.cumsum(counts) - counts
    length = (counts - 1) * page_rows + tail_rows
    row_index = jnp.arange(row_count, dtype=jnp.int32)
    page_of = row_index // page_rows
    owner_of = jnp.sum((starting[None, :] <= page_of[:, None]).astype(jnp.int32), axis=1) - 1
    member = owner_of[:, None] == jnp.arange(counts.shape[0], dtype=jnp.int32)[None, :]
    offset = jnp.sum(jnp.where(member, starting[None, :] * page_rows, 0), axis=1)
    spread = jnp.sum(jnp.where(member, length[None, :], 0), axis=1)
    return (owner_of, row_index - offset, spread)


def attend(balanced, counts, tail_rows, page_rows):
    row_count = balanced.shape[0]
    model_width = balanced.shape[1] // 5
    head_dim = model_width // HEADS
    owner_of, position, spread = layout_rows(counts, tail_rows, page_rows, row_count)
    allowed = (
        (owner_of[:, None] == owner_of[None, :])
        & (position[None, :] <= position[:, None])
        & (position[None, :] < spread[None, :])
    )
    queries = balanced[:, :model_width].reshape(row_count, HEADS, head_dim)
    key_rows = balanced[:, model_width : 2 * model_width].reshape(row_count, HEADS, head_dim)
    values = balanced[:, 2 * model_width : 3 * model_width].reshape(row_count, HEADS, head_dim)
    scores = jnp.einsum(
        "qhd,khd->hqk", queries, key_rows, preferred_element_type=jnp.float32
    ) * head_dim ** (-0.5)
    weights = (
        jnp.where(allowed[None], jax.nn.silu(scores), 0.0)
        / spread.astype(jnp.float32)[None, :, None]
    )
    weights = weights.astype(jnp.bfloat16)
    attended = jnp.einsum(
        "hqk,khd->qhd", weights, values, preferred_element_type=jnp.float32
    ).reshape(row_count, model_width)
    average = jnp.mean(attended, axis=1, keepdims=True)
    centered = attended - average
    variance = jnp.mean(centered * centered, axis=1, keepdims=True)
    gating = balanced[:, 3 * model_width : 4 * model_width].astype(jnp.float32)
    return (centered * lax.rsqrt(variance + 1e-05) * gating).astype(jnp.bfloat16)


def gate_share(normed, router, routes):
    logits = jnp.dot(normed, router, preferred_element_type=jnp.float32)
    scores = jax.nn.sigmoid(logits)
    picked = routes[:, :, None] == jnp.arange(router.shape[1], dtype=jnp.int32)[None, None, :]
    chosen = jnp.sum(jnp.where(picked, scores[:, None, :], 0.0), axis=2)
    return chosen / jnp.sum(chosen, axis=1, keepdims=True)


def slot_table(routes, experts, capacity):
    pair_count = routes.shape[0] * routes.shape[1]
    chosen = routes.reshape(-1)
    onehot = (chosen[:, None] == jnp.arange(experts, dtype=jnp.int32)[None, :]).astype(jnp.int32)
    before = jnp.cumsum(onehot, axis=0) - onehot
    ranking = jnp.sum(before * onehot, axis=1)
    slot_of_pair = chosen * capacity + ranking
    matches = slot_of_pair[None, :] == jnp.arange(experts * capacity, dtype=jnp.int32)[:, None]
    source_token = (
        jnp.sum(jnp.where(matches, jnp.arange(pair_count, dtype=jnp.int32)[None, :], 0), axis=1)
        // 2
    )
    return (slot_of_pair, source_token)


def whole_expert(incoming, gate_full, up_full, down_full):
    flat_rows = incoming.reshape(-1, incoming.shape[-1])
    gate_act = jnp.dot(flat_rows, gate_full, preferred_element_type=jnp.float32)
    up_act = jnp.dot(flat_rows, up_full, preferred_element_type=jnp.float32)
    hidden = (jax.nn.silu(gate_act) * up_act).astype(jnp.bfloat16)
    half_units = gate_full.shape[1] // 2
    first_part = jnp.dot(
        hidden[:, :half_units], down_full[:half_units], preferred_element_type=jnp.float32
    ).astype(jnp.bfloat16)
    second_part = jnp.dot(
        hidden[:, half_units:], down_full[half_units:], preferred_element_type=jnp.float32
    ).astype(jnp.bfloat16)
    summed = (first_part.astype(jnp.float32) + second_part.astype(jnp.float32)).astype(jnp.bfloat16)
    return summed.reshape(incoming.shape)


def shards(histories, page_map, user_pages, tails, routes, out_proj, router, w_gate, w_up, w_down):
    devices = lax.axis_size("expert")
    parity = lax.axis_index("expert") % 2
    row_count = histories.shape[1]
    stacked_width = histories.shape[2]
    model_width = stacked_width // 5
    pages_dev = page_map.shape[2]
    page_rows = row_count // pages_dev
    page_slots = (pages_dev + devices - 1) // devices
    page_block = histories[0].reshape(pages_dev, page_rows, stacked_width)
    target = page_map[0, 0]
    target_dev = target // pages_dev
    earlier = (target_dev[None, :] == target_dev[:, None]) & (target[None, :] < target[:, None])
    position = target_dev * page_slots + jnp.sum(earlier.astype(jnp.int32), axis=1)
    matches = position[None, :] == jnp.arange(devices * page_slots, dtype=jnp.int32)[:, None]
    chosen_page = jnp.sum(
        jnp.where(matches, jnp.arange(pages_dev, dtype=jnp.int32)[None, :], 0), axis=1
    )
    outgoing = page_block[chosen_page]
    arrived = lax.all_to_all(outgoing, "expert", split_axis=0, concat_axis=0, tiled=True)
    anchor = page_map[0, 1]
    anchor_dev = anchor // pages_dev
    ordering = jnp.arange(pages_dev, dtype=jnp.int32)
    sooner = (anchor_dev[None, :] == anchor_dev[:, None]) & (ordering[None, :] < ordering[:, None])
    where_from = anchor_dev * page_slots + jnp.sum(sooner.astype(jnp.int32), axis=1)
    balanced = arrived[where_from].reshape(row_count, stacked_width)
    mixed_in = attend(balanced, user_pages[0, 0], tails[0, 0], page_rows)
    projected = jnp.dot(
        mixed_in,
        lax.all_gather(out_proj, "expert", axis=1, tiled=True)[0],
        preferred_element_type=jnp.float32,
    )
    resid = (balanced[:, 4 * model_width :].astype(jnp.float32) + projected).astype(jnp.bfloat16)
    resid_wide = resid.astype(jnp.float32)
    normed = (
        resid_wide * lax.rsqrt(jnp.mean(resid_wide * resid_wide, axis=1, keepdims=True) + 1e-06)
    ).astype(jnp.bfloat16)
    experts = router.shape[2]
    capacity = 4 * row_count // experts
    share = gate_share(normed, router[0], routes[0])
    slot_of_pair, source_token = slot_table(routes[0], experts, capacity)
    packed = normed[source_token].reshape(experts, capacity, model_width)
    is_odd = parity == 1
    half_units = w_gate.shape[2]
    gate_up = jnp.concatenate([w_gate[0], w_up[0]], axis=1)
    other_gate_up = swapped(gate_up, "expert", 0)
    other_down = swapped(w_down[0], "expert", 0)
    own_gate = gate_up[:, :half_units]
    own_up = gate_up[:, half_units:]
    other_gate = other_gate_up[:, :half_units]
    other_up = other_gate_up[:, half_units:]
    gate_full = jnp.where(
        is_odd,
        jnp.concatenate([other_gate, own_gate], axis=1),
        jnp.concatenate([own_gate, other_gate], axis=1),
    )
    up_full = jnp.where(
        is_odd,
        jnp.concatenate([other_up, own_up], axis=1),
        jnp.concatenate([own_up, other_up], axis=1),
    )
    down_full = jnp.where(
        is_odd,
        jnp.concatenate([other_down, w_down[0]], axis=0),
        jnp.concatenate([w_down[0], other_down], axis=0),
    )
    half_cap = capacity // 2
    sent_rows = packed.reshape(experts * 2, half_cap, model_width)
    own_rows = lax.all_to_all(sent_rows, "expert", split_axis=0, concat_axis=0, tiled=True)
    served = whole_expert(own_rows, gate_full, up_full, down_full)
    came_back = lax.all_to_all(served, "expert", split_axis=0, concat_axis=0, tiled=True)
    result = came_back.reshape(experts, capacity, model_width)
    picked = result.reshape(experts * capacity, model_width)[slot_of_pair]
    picked = picked.reshape(row_count, 2, model_width).astype(jnp.float32)
    mixture = jnp.sum(picked * share[:, :, None], axis=1)
    output_rows = (resid_wide + mixture).astype(jnp.bfloat16)
    return from_behind(output_rows[None], "section", 1)


def solution(mesh):
    in_specs = (
        P("section", "expert", None),
        P("section", None, "expert"),
        P("section", "expert", None),
        P("section", "expert", None),
        P("section", "expert", None),
        P("section", "expert", None),
        P("section", None, None),
        P("section", None, "expert"),
        P("section", None, "expert"),
        P("section", "expert", None),
    )
    out_specs = P("section", "expert", None)
    return jax.shard_map(shards, mesh=mesh, in_specs=in_specs, out_specs=out_specs, check_vma=False)
```

profile of v0, /device:TPU:8, one launch (start us, length us, event | category | flops | bytes accessed | tf_op | source)
XLA Modules:
  0.0 288.9 jit_solution(12892616485323434839)
XLA Ops:
  8.3 2.6 reshape_squeeze.6
  10.9 4.2 %gather_fusion = bf16[64,4,5120]{2,1,0:T(4,128)(2,1)} fusion(bf16[32,4,5120]{2,1,0:T(4,128)(2,1)S(1)} %reshape_squeeze.6, s32[1024]{0:T(1024)S(1)} %pad_clamp_fusion.3), kind=kCustom, calls=%fused_computation | custom fusion | bytes 5243136 | tf_op jit(solution)/shard_map/gather | solution.py:119
  15.1 16.6 %all-to-all-start = ((bf16[64,4,5120]{2,1,0:T(4,128)(2,1)}), bf16[64,4,5120]{2,1,0:T(4,128)(2,1)S(1)}, u32[]{:S(2)}, u32[]{:S(2)}) async-start(bf16[64,4,5120]{2,1,0:T(4,128)(2,1)} %gather_fusion), calls=%async_computation | async-start | bytes 5242880 | tf_op jit(solution)/shard_map/all_to_all | solution.py:120
  32.5 3.1 %pad_maximum_fusion.1 = bf16[1024,1024]{1,0:T(8,128)(2,1)} fusion(bf16[1024,512]{1,0:T(8,128)(2,1)} %bitcast.121, bf16[1024,512]{1,0:T(8,128)(2,1)} %bitcast.119), kind=kLoop, calls=%fused_computation.5 | loop fusion | flops 4194304 | bytes 4194304 | tf_op jit(solution)/shard_map/concatenate | solution.py:145
  35.6 2.4 collective-permute-start
  40.0 57.6 %all-to-all-done = bf16[64,4,5120]{2,1,0:T(4,128)(2,1)S(1)} async-done(((bf16[64,4,5120]{2,1,0:T(4,128)(2,1)}), bf16[64,4,5120]{2,1,0:T(4,128)(2,1)S(1)}, u32[]{:S(2)}, u32[]{:S(2)}) %all-to-all-start) | async-done | bytes 2621472 | tf_op jit(solution)/shard_map/all_to_all | solution.py:120
  97.6 2.7 gather_fusion.1
  100.3 2.5 reshape.543
  104.4 52.7 %all-gather.2.cloned.1.call-done = bf16[1,1024,1024]{2,1,0:T(8,128)(2,1)} async-done(((bf16[1,16,1024]{2,1,0:T(8,128)(2,1)}), bf16[1,1024,1024]{2,1,0:T(8,128)(2,1)}) %all-gather.2.cloned.1.call-update) | async-done | bytes 2097168 | tf_op jit(solution)/shard_map/all_gather | solution.py:130
  157.1 2.2 multiply_reduce_fusion.1
  159.3 2.8 gather_fusion.2
  162.1 10.0 %all-to-all-start.1 = ((bf16[64,8,1024]{2,1,0:T(8,128)(2,1)}), bf16[64,8,1024]{2,1,0:T(8,128)(2,1)}, u32[]{:S(2)}, u32[]{:S(2)}) async-start(bf16[64,8,1024]{2,1,0:T(8,128)(2,1)} %bitcast.20), calls=%async_computation.1 | async-start | bytes 2097152 | tf_op jit(solution)/shard_map/all_to_all | solution.py:169
  172.1 2.6 collective-permute-start.1
  174.8 39.3 %collective-permute-done.1 = bf16[512,1024]{1,0:T(8,128)(2,1)} collective-permute-done((bf16[512,1024]{1,0:T(8,128)(2,1)S(1)}, bf16[512,1024]{1,0:T(8,128)(2,1)}, u32[]{:S(2)}, u32[]{:S(2)}) %collective-permute-start.1) | collective-permute-done | bytes 1048608 | tf_op jit(solution)/shard_map/ppermute | solution.py:10
  214.0 4.1 %maximum_select_fusion = bf16[1024,1024]{1,0:T(8,128)(2,1)} fusion(bf16[512,1024]{1,0:T(8,128)(2,1)S(1)} %bitcast.118, bf16[512,1024]{1,0:T(8,128)(2,1)} %collective-permute-done.1, pred[]{:T(512)S(6)} %eq.150), kind=kLoop, calls=%fused_computation.19 | loop fusion | flops 9437184 | bytes 4194305 | tf_op jit(solution)/shard_map/jit(_where)/select_n | solution.py:162
  218.1 3.1 %fusion.68 = (bf16[1024,512]{1,0:T(8,128)(2,1)}, bf16[1024,512]{1,0:T(8,128)(2,1)}) fusion(bf16[1024,1024]{1,0:T(8,128)(2,1)} %collective-permute-done), kind=kLoop, calls=%fused_computation.141 | loop fusion | bytes 4194304 | tf_op jit(solution)/shard_map/slice | solution.py:151
  221.2 3.3 %fusion.1 = f32[512,1024]{1,0:T(8,128)S(1)} fusion(bf16[1024,512]{1,0:T(8,128)(2,1)S(1)} %bitcast.120, bf16[1024,512]{1,0:T(8,128)(2,1)} %get-tuple-element.12, pred[]{:T(512)S(6)} %eq.150, bf16[64,8,1024]{2,1,0:T(8,128)(2,1)} %all-to-all-done.1), kind=kOutput, calls=%fused_computation.8 | convolution fusion | flops 1083179008 | bytes 5242881 | tf_op jit(solution)/shard_map/dot_general | solution.py:87
  224.6 3.8 %multiply_convert_fusion = bf16[512,1024]{1,0:T(8,128)(2,1)S(1)} fusion(f32[512,1024]{1,0:T(8,128)S(1)} %fusion.1, bf16[1024,512]{1,0:T(8,128)(2,1)S(1)} %bitcast.122, bf16[1024,512]{1,0:T(8,128)(2,1)S(1)} %copy-done.5, pred[]{:T(512)S(6)} %eq.150, bf16[64,8,1024]{2,1,0:T(8,128)(2,1)} %all-to-all-done.1), kind=kOutput, calls=%fused_computation.23 | convolution fusion | flops 1086324736 | bytes 6291457 | tf_op jit(solution)/shard_map/dot_general | solution.py:88
  229.1 1.7 fusion.18
  230.8 12.6 %all-to-all-start.2 = ((bf16[64,8,1024]{2,1,0:T(8,128)(2,1)}), bf16[64,8,1024]{2,1,0:T(8,128)(2,1)S(1)}, u32[]{:S(2)}, u32[]{:S(2)}) async-start(bf16[64,8,1024]{2,1,0:T(8,128)(2,1)} %fusion.18), calls=%async_computation.2 | async-start | bytes 2097152 | tf_op jit(solution)/shard_map/all_to_all | solution.py:171
  244.1 27.0 %all-to-all-done.2 = bf16[64,8,1024]{2,1,0:T(8,128)(2,1)S(1)} async-done(((bf16[64,8,1024]{2,1,0:T(8,128)(2,1)}), bf16[64,8,1024]{2,1,0:T(8,128)(2,1)S(1)}, u32[]{:S(2)}, u32[]{:S(2)}) %all-to-all-start.2) | async-done | bytes 1048608 | tf_op jit(solution)/shard_map/all_to_all | solution.py:171
  271.1 1.2 gather_fusion.3
  273.0 1.3 multiply_reduce_fusion
  274.4 7.0 %collective-permute-done.2 = bf16[1,128,1024]{2,1,0:T(8,128)(2,1)S(1)} collective-permute-done((bf16[1,128,1024]{2,1,0:T(8,128)(2,1)S(1)}, bf16[1,128,1024]{2,1,0:T(8,128)(2,1)S(1)}, u32[]{:S(2)}, u32[]{:S(2)}) %collective-permute-start.2) | collective-permute-done | bytes 262176 | tf_op jit(solution)/shard_map/ppermute | solution.py:16
  (81 shorter events, 9.0 us)
Async XLA Ops:
  6.5 237.2 %copy-start = (bf16[1,1024,32]{1,2,0:T(8,128)(2,1)S(1)}, bf16[1,1024,32]{1,2,0:T(8,128)(2,1)}, u32[]{:S(2)}) copy-start(bf16[1,1024,32]{1,2,0:T(8,128)(2,1)} %param.16) | copy-start | bytes 196612
  15.1 82.5 %all-to-all-start = ((bf16[64,4,5120]{2,1,0:T(4,128)(2,1)}), bf16[64,4,5120]{2,1,0:T(4,128)(2,1)S(1)}, u32[]{:S(2)}, u32[]{:S(2)}) async-start(bf16[64,4,5120]{2,1,0:T(4,128)(2,1)} %gather_fusion), calls=%async_computation | async-start | bytes 5242880 | tf_op jit(solution)/shard_map/all_to_all | solution.py:120
  31.7 125.4 %all-gather.2.cloned.1.call-start = ((), (), s32[]{:S(2)}) async-start(), calls=%async_computation.3 | async-start | bytes 2129920 | tf_op jit(solution)/shard_map/all_gather | solution.py:130
  32.4 5.5 %copy-start.6 = (s32[1,128,2]{1,2,0:T(2,128)S(1)}, s32[1,128,2]{1,2,0:T(2,128)}, u32[]{:S(2)}) copy-start(s32[1,128,2]{1,2,0:T(2,128)} %param.14) | copy-start | bytes 3076
  32.4 5.9 %copy-start.8 = (s32[1,1,4]{2,1,0:T(1,128)S(1)}, s32[1,1,4]{2,1,0:T(1,128)}, u32[]{:S(2)}) copy-start(s32[1,1,4]{2,1,0:T(1,128)} %param.12) | copy-start | bytes 52
  32.4 6.1 %copy-start.9 = (s32[1,1,4]{2,1,0:T(1,128)S(1)}, s32[1,1,4]{2,1,0:T(1,128)}, u32[]{:S(2)}) copy-start(s32[1,1,4]{2,1,0:T(1,128)} %param.13) | copy-start | bytes 52
  32.5 7.1 %copy-start.7 = (s32[1,2,32]{2,1,0:T(2,128)S(1)}, s32[1,2,32]{2,1,0:T(2,128)}, u32[]{:S(2)}) copy-start(s32[1,2,32]{2,1,0:T(2,128)} %param.11) | copy-start | bytes 772
  35.6 182.6 %collective-permute-start = (bf16[1024,1024]{1,0:T(8,128)(2,1)}, bf16[1024,1024]{1,0:T(8,128)(2,1)}, u32[]{:S(2)}, u32[]{:S(2)}) collective-permute-start(bf16[1024,1024]{1,0:T(8,128)(2,1)} %pad_maximum_fusion.1), channel_id=1, source_target_pairs={{0,1},{1,0},{2,3},{3,2},{4,5},{5,4},{6,7},{7,6},{8,9},{9,8},{10,11... | collective-permute-start | bytes 6291464 | tf_op jit(solution)/shard_map/ppermute | solution.py:10
  162.1 10.0 %copy-start.2 = (bf16[1,512,1024]{2,1,0:T(8,128)(2,1)S(1)}, bf16[1,512,1024]{2,1,0:T(8,128)(2,1)}, u32[]{:S(2)}) copy-start(bf16[1,512,1024]{2,1,0:T(8,128)(2,1)} %param.19) | copy-start | bytes 3145732
  162.1 59.1 %all-to-all-start.1 = ((bf16[64,8,1024]{2,1,0:T(8,128)(2,1)}), bf16[64,8,1024]{2,1,0:T(8,128)(2,1)}, u32[]{:S(2)}, u32[]{:S(2)}) async-start(bf16[64,8,1024]{2,1,0:T(8,128)(2,1)} %bitcast.20), calls=%async_computation.1 | async-start | bytes 2097152 | tf_op jit(solution)/shard_map/all_to_all | solution.py:169
  172.1 41.9 %collective-permute-start.1 = (bf16[512,1024]{1,0:T(8,128)(2,1)S(1)}, bf16[512,1024]{1,0:T(8,128)(2,1)}, u32[]{:S(2)}, u32[]{:S(2)}) collective-permute-start(bf16[512,1024]{1,0:T(8,128)(2,1)S(1)} %bitcast.117), channel_id=1, source_target_pairs={{0,1},{1,0},{2,3},{3,2},{4,5},{5,4},{6,7},{7,6},{8,9},{9,8},{10,11... | collective-permute-start | bytes 3145736 | tf_op jit(solution)/shard_map/ppermute | solution.py:10
  218.1 3.1 %copy-start.3 = (bf16[1,1024,512]{2,1,0:T(8,128)(2,1)S(1)}, bf16[1,1024,512]{2,1,0:T(8,128)(2,1)}, u32[]{:S(2)}) copy-start(bf16[1,1024,512]{2,1,0:T(8,128)(2,1)} %param.17) | copy-start | bytes 3145732
  221.2 3.3 %copy-start.4 = (bf16[1,1024,512]{2,1,0:T(8,128)(2,1)S(1)}, bf16[1,1024,512]{2,1,0:T(8,128)(2,1)}, u32[]{:S(2)}) copy-start(bf16[1,1024,512]{2,1,0:T(8,128)(2,1)} %param.18) | copy-start | bytes 3145732
  221.2 3.3 %copy-start.5 = (bf16[1024,512]{1,0:T(8,128)(2,1)S(1)}, bf16[1024,512]{1,0:T(8,128)(2,1)}, u32[]{:S(2)}) copy-start(bf16[1024,512]{1,0:T(8,128)(2,1)} %get-tuple-element.11) | copy-start | bytes 3145732
  224.5 3.8 %copy-start.1 = (bf16[1024,1024]{1,0:T(8,128)(2,1)S(1)}, bf16[1024,1024]{1,0:T(8,128)(2,1)}, u32[]{:S(2)}) copy-start(bf16[1024,1024]{1,0:T(8,128)(2,1)} %maximum_select_fusion) | copy-start | bytes 6291460
  230.8 40.3 %all-to-all-start.2 = ((bf16[64,8,1024]{2,1,0:T(8,128)(2,1)}), bf16[64,8,1024]{2,1,0:T(8,128)(2,1)S(1)}, u32[]{:S(2)}, u32[]{:S(2)}) async-start(bf16[64,8,1024]{2,1,0:T(8,128)(2,1)} %fusion.18), calls=%async_computation.2 | async-start | bytes 2097152 | tf_op jit(solution)/shard_map/all_to_all | solution.py:171
  274.4 7.0 %collective-permute-start.2 = (bf16[1,128,1024]{2,1,0:T(8,128)(2,1)S(1)}, bf16[1,128,1024]{2,1,0:T(8,128)(2,1)S(1)}, u32[]{:S(2)}, u32[]{:S(2)}) collective-permute-start(bf16[1,128,1024]{2,1,0:T(8,128)(2,1)S(1)} %fusion.44), channel_id=1, source_target_pairs={{448,0},{0,64},{64,128},{128,192},{192,256},{256,320},{320,384},{3... | collective-permute-start | bytes 786440 | tf_op jit(solution)/shard_map/ppermute | solution.py:16
Sparse Core Ops, SparseCore 0:
  35.6 121.4 all-gather.1
where the time goes:
time: 290 us; the launch traced here: 289 us
  waiting for transfers between devices  184 us (63%)
  starting transfers between devices  44.2 us (15%)
  local copies, waits for them, and re-layouts  22.7 us (8%)
  between operations  13.8 us (5%)
  matrix products  12.5 us (4%)
  other arithmetic  11.4 us (4%)
    all_to_all x1, waiting for transfers between devices, shards(): lax.all_to_all(outgoing, 'expert', split_axis=0, concat_axis=0, tiled=True)  57.6 us
    all_gather x1, waiting for transfers between devices, shards(): lax.all_gather(out_proj, 'expert', axis=1, tiled=True)[0]  52.7 us
    ppermute x2, waiting for transfers between devices, swapped(): lax.ppermute(shard, axis, [(i, i ^ 1 << apart) for i in range(lax.axis_si...  39.3 us
    all_to_all x1, waiting for transfers between devices, shards(): lax.all_to_all(served, 'expert', split_axis=0, concat_axis=0, tiled=True)  27 us
    all_to_all x1, starting transfers between devices, shards(): lax.all_to_all(outgoing, 'expert', split_axis=0, concat_axis=0, tiled=True)  16.6 us
    all_to_all x1, starting transfers between devices, shards(): lax.all_to_all(served, 'expert', split_axis=0, concat_axis=0, tiled=True)  12.6 us
    all_to_all x1, starting transfers between devices, shards(): lax.all_to_all(sent_rows, 'expert', split_axis=0, concat_axis=0, tiled=True)  9.98 us
    ppermute x1, waiting for transfers between devices, from_behind(): return lax.ppermute(block, axis, route)  6.99 us
  transfers between devices with their start and end apart: 7, of which 5 were waited for; matrix products, arithmetic and copies ran while one was open for 9% of the time, Pallas kernels for 0%

commit v1 on v0

v1 whole, which is shorter than its diff:
```python
import functools

import jax
import jax.numpy as jnp
from jax import lax
from jax.experimental import pallas as pl
from jax.experimental.pallas import tpu as pltpu
from jax.sharding import PartitionSpec as P


HEADS = 8
SIDE = 8
F32 = jnp.float32
BF16 = jnp.bfloat16
VMEM = pltpu.VMEM
SMEM = pltpu.SMEM


def iota(shape, axis):
    return lax.broadcasted_iota(jnp.int32, shape, axis)


def dot(a, b):
    return jnp.dot(a, b, preferred_element_type=F32)


def dot_t(a, b):
    return lax.dot_general(a, b, (((1,), (1,)), ((), ())), preferred_element_type=F32)


def flag(mask):
    return jnp.where(mask, 1.0, 0.0).astype(BF16)


def whole(space=VMEM):
    return pl.BlockSpec(memory_space=space)


def pack_pages_body(map_ref, rows_ref, out_ref, pick_ref):
    @pl.when(pl.program_id(0) == 0)
    def _():
        device = lax.shift_right_logical(map_ref[0, 0:1, :], 5).astype(F32)
        pages = device.shape[1]
        rows = pages * 4
        spread = flag(iota((pages, rows), 0) == lax.shift_right_logical(iota((pages, rows), 1), 2))
        target = dot(jnp.broadcast_to(device, (8, pages)).astype(BF16), spread)[0:1]
        slot = iota((pick_ref.shape[0], rows), 0)
        row = iota((pick_ref.shape[0], rows), 1)
        hit = (lax.shift_right_logical(slot, 3) == target.astype(jnp.int32)) & ((slot & 3) == (row & 3))
        pick_ref[:, :rows] = flag(hit & ((slot & 4) == 0))
        pick_ref[:, rows:] = flag(hit & ((slot & 4) == 4))

    half = rows_ref.shape[1] // 2
    both = jnp.concatenate([rows_ref[:, :half], rows_ref[:, half:]], axis=0)
    out_ref[...] = dot(pick_ref[...], both).astype(BF16)


def pack_pages(page_map, rows, devices):
    count, width = rows.shape
    block = width // 5
    slots = devices * 8
    return pl.pallas_call(
        pack_pages_body,
        name="pack_pages",
        grid=(5,),
        in_specs=[
            whole(),
            pl.BlockSpec((count, block), lambda b: (0, b)),
        ],
        out_specs=pl.BlockSpec((slots, block // 2), lambda b: (0, b)),
        out_shape=jax.ShapeDtypeStruct((slots, width // 2), BF16),
        scratch_shapes=[pltpu.VMEM((slots, 2 * count), BF16)],
        cost_estimate=pl.CostEstimate(flops=1 << 30, bytes_accessed=4 << 20, transcendentals=0),
    )(page_map, rows)


def user_layout(index, pages_ref, tails_ref):
    users = pages_ref.shape[2]
    owner = jnp.zeros_like(index)
    offset = jnp.zeros_like(index)
    length = jnp.zeros_like(index) + ((pages_ref[0, 0, 0] - 1) * 4 + tails_ref[0, 0, 0])
    start = 0
    for user in range(1, users):
        start = start + pages_ref[0, 0, user - 1] * 4
        inside = index >= start
        owner = jnp.where(inside, user, owner)
        offset = jnp.where(inside, start, offset)
        length = jnp.where(inside, (pages_ref[0, 0, user] - 1) * 4 + tails_ref[0, 0, user], length)
    return owner, offset, length


def token_body(
    place_ref, pages_ref, tails_ref, map_ref, routes_ref, arrived_ref, router_ref, *refs
):
    proj_refs = refs[:SIDE]
    normed_ref, resid_ref, share_ref, mixed_ref = refs[SIDE:]
    count = resid_ref.shape[0]
    slots = arrived_ref.shape[0]
    half = arrived_ref.shape[1] // 5
    pages = map_ref.shape[2]
    model_width = 2 * half
    head_dim = model_width // HEADS

    source = lax.shift_right_logical(map_ref[0, 1:2, :], 5).astype(F32)
    mine = lax.shift_right_logical(iota((count, pages), 0), 2) == iota((count, pages), 1)
    source = jnp.sum(jnp.where(mine, source, 0.0), axis=1, keepdims=True).astype(jnp.int32)
    slot = iota((count, slots), 1)
    near = lax.shift_right_logical(slot, 3) == source
    row = iota((count, slots), 0) & 3
    picks = [flag(near & ((slot & 7) == row + 4 * side)) for side in range(2)]

    def block(index, side):
        return dot(picks[side], arrived_ref[:, index * half : (index + 1) * half])

    rows = iota((count, count), 0)
    keys = iota((count, count), 1)
    row_owner, _, row_length = user_layout(rows, pages_ref, tails_ref)
    key_owner, key_offset, key_length = user_layout(keys, pages_ref, tails_ref)
    allowed = (row_owner == key_owner) & (keys <= rows) & (keys - key_offset < key_length)
    factor = jnp.where(allowed, 1.0 / row_length.astype(F32), 0.0)
    attended = []
    for side in range(2):
        queries = block(0, side).astype(BF16)
        key_rows = block(1, side).astype(BF16)
        values = block(2, side).astype(BF16)
        for head in range(HEADS // 2):
            part = slice(head * head_dim, (head + 1) * head_dim)
            scores = dot_t(queries[:, part], key_rows[:, part]) * head_dim ** (-0.5)
            weights = (scores * jax.nn.sigmoid(scores) * factor).astype(BF16)
            attended.append(dot(weights, values[:, part]))
    total = functools.reduce(jnp.add, attended)
    average = jnp.sum(total, axis=1, keepdims=True) * (1.0 / model_width)
    attended = [part - average for part in attended]
    squares = functools.reduce(jnp.add, [part * part for part in attended])
    variance = jnp.sum(squares, axis=1, keepdims=True) * (1.0 / model_width)
    scale = lax.rsqrt(variance + 1e-05)
    for side in range(2):
        gating = block(3, side)
        for head in range(HEADS // 2):
            part = slice(head * head_dim, (head + 1) * head_dim)
            index = side * (HEADS // 2) + head
            mixed_ref[index] = (attended[index] * scale * gating[:, part]).astype(BF16)

    place = place_ref[0]
    order = [0, 1, 2, 3, 4, -1, -2, -3]
    mixed = [mixed_ref[(place - shift) & (SIDE - 1)] for shift in order]
    squares = jnp.zeros((count, 1), F32)
    chunk = half // 2
    for side in range(2):
        inputs = block(4, side)
        for quarter in range(2):
            part = slice(side * half + quarter * chunk, side * half + (quarter + 1) * chunk)
            projected = dot(mixed[0], proj_refs[0][:, part])
            for index in range(1, SIDE):
                projected += dot(mixed[index], proj_refs[index][:, part])
            resid = (inputs[:, quarter * chunk : (quarter + 1) * chunk] + projected).astype(BF16)
            resid_ref[:, part] = resid
            wide = resid.astype(F32)
            squares += jnp.sum(wide * wide, axis=1, keepdims=True)
    scale = lax.rsqrt(squares * (1.0 / model_width) + 1e-06)
    for quarter in range(4):
        part = slice(quarter * chunk, (quarter + 1) * chunk)
        normed_ref[:, part] = (resid_ref[:, part].astype(F32) * scale).astype(BF16)

    experts = router_ref.shape[0]
    scores = jax.nn.sigmoid(dot_t(router_ref[...], normed_ref[...]))
    expert = iota((experts, count), 0)
    chosen = [
        jnp.sum(jnp.where(expert == routes_ref[k : k + 1, :], scores, 0.0), axis=0, keepdims=True)
        for k in range(2)
    ]
    share_ref[...] = jnp.zeros(share_ref.shape, F32)
    for k in range(2):
        share_ref[k : k + 1, :] = chosen[k] / (chosen[0] + chosen[1])


def token_stage(place, user_pages, tails, page_map, routes, arrived, router, proj, count):
    width = arrived.shape[1] // 5 * 2
    return pl.pallas_call(
        token_body,
        name="token_stage",
        in_specs=[whole(SMEM)] * 3 + [whole()] * (4 + SIDE),
        out_specs=[whole()] * 3,
        out_shape=[
            jax.ShapeDtypeStruct((count, width), BF16),
            jax.ShapeDtypeStruct((count, width), BF16),
            jax.ShapeDtypeStruct((8, count), F32),
        ],
        scratch_shapes=[pltpu.VMEM((HEADS, count, width // HEADS), BF16)],
        cost_estimate=pl.CostEstimate(flops=2 << 30, bytes_accessed=6 << 20, transcendentals=0),
    )(place, user_pages, tails, page_map, routes, arrived, router, *proj)


def slots_body(experts, core_ref, mine_ref, theirs_ref, pick_ref, lanes_ref):
    count = mine_ref.shape[1]
    core = core_ref[0]
    capacity = 4 * count // experts
    expert = iota((experts, count), 0)
    earlier = flag(iota((count, count), 0) < iota((count, count), 1))
    row = iota((pick_ref.shape[0], count), 0)
    lanes_ref[...] = jnp.zeros(lanes_ref.shape, F32)
    for side, routes_ref in enumerate((mine_ref, theirs_ref)):
        chosen = [routes_ref[k : k + 1, :] for k in range(2)]
        named = [expert == chosen[k] for k in range(2)]
        before = dot(flag(named[0] | named[1]), earlier)
        lanes = []
        for k in range(2):
            rank = jnp.sum(jnp.where(named[k], before, 0.0), axis=0, keepdims=True)
            slot = chosen[k] * capacity + rank.astype(jnp.int32)
            half = lax.shift_right_logical(slot, 3) & 1
            lanes.append(jnp.where(half == core, slot ^ (8 * side), -1))
            lanes_ref[2 * side + k : 2 * side + k + 1, :] = lanes[k].astype(F32)
        pick_ref[:, side * count : (side + 1) * count] = flag((row == lanes[0]) | (row == lanes[1]))


def slot_tables(core, mine, theirs, experts):
    count = mine.shape[1]
    rows = 4 * count
    return pl.pallas_call(
        functools.partial(slots_body, experts),
        name="slot_tables",
        in_specs=[whole(SMEM), whole(), whole()],
        out_specs=[whole()] * 2,
        out_shape=[
            jax.ShapeDtypeStruct((rows, 2 * count), BF16),
            jax.ShapeDtypeStruct((8, count), F32),
        ],
        cost_estimate=pl.CostEstimate(flops=1 << 24, bytes_accessed=1 << 18, transcendentals=0),
    )(core, mine, theirs)


def pack_rows_body(pick_ref, mine_ref, theirs_ref, out_ref):
    _, width = mine_ref.shape
    chunk = width // 4
    for quarter in range(4):
        part = slice(quarter * chunk, (quarter + 1) * chunk)
        rows = jnp.concatenate([mine_ref[:, part], theirs_ref[:, part]], axis=0)
        out_ref[:, part] = dot(pick_ref[...], rows).astype(BF16)


def pack_rows(pick, mine, theirs):
    return pl.pallas_call(
        pack_rows_body,
        name="pack_rows",
        in_specs=[whole()] * 3,
        out_specs=whole(),
        out_shape=jax.ShapeDtypeStruct((pick.shape[0], mine.shape[1]), BF16),
        cost_estimate=pl.CostEstimate(flops=1 << 28, bytes_accessed=2 << 20, transcendentals=0),
    )(pick, mine, theirs)


def expert_body(added, rows_ref, gate_ref, up_ref, down_ref, *refs):
    out_ref, total_ref = refs[-2:]
    step = pl.program_id(0)
    tile = 256
    for index in range(rows_ref.shape[0] // tile):
        part = slice(index * tile, (index + 1) * tile)
        rows = rows_ref[part, :]
        gate = dot(rows, gate_ref[...])
        hidden = (gate * jax.nn.sigmoid(gate) * dot(rows, up_ref[...])).astype(BF16)
        result = dot(hidden, down_ref[...])

        @pl.when(step == 0)
        def _():
            total_ref[part, :] = result

        @pl.when(step == 1)
        def _():
            half = (total_ref[part, :] + result).astype(BF16)
            if added:
                half = (half.astype(F32) + refs[0][part, :].astype(F32)).astype(BF16)
            out_ref[part, :] = half


def expert_half(rows, gate, up, down, earlier=None):
    count, width = rows.shape
    chunk = gate.shape[1] // 2
    added = earlier is not None
    extra = (earlier,) if added else ()
    return pl.pallas_call(
        functools.partial(expert_body, added),
        name="expert_half",
        grid=(2,),
        in_specs=[
            pl.BlockSpec((count, width), lambda c: (0, 0)),
            pl.BlockSpec((width, chunk), lambda c: (0, c)),
            pl.BlockSpec((width, chunk), lambda c: (0, c)),
            pl.BlockSpec((chunk, width), lambda c: (c, 0)),
        ]
        + [pl.BlockSpec((count, width), lambda c: (0, 0))] * len(extra),
        out_specs=pl.BlockSpec((count, width), lambda c: (0, 0)),
        out_shape=jax.ShapeDtypeStruct((count, width), BF16),
        scratch_shapes=[pltpu.VMEM((count, width), F32)],
        cost_estimate=pl.CostEstimate(flops=2 << 30, bytes_accessed=5 << 20, transcendentals=0),
    )(rows, gate, up, down, *extra)


def combine_body(lanes_ref, mine_ref, theirs_ref, resid_ref, rows_ref, own_ref, other_ref):
    count, width = resid_ref.shape
    slots = rows_ref.shape[0]
    table = jnp.concatenate([lanes_ref[0:4, :], mine_ref[0:2, :], theirs_ref[0:2, :]], axis=0)
    table = jnp.transpose(table)
    slot = iota((count, slots), 1).astype(F32)
    shares = []
    for side in range(2):
        share = jnp.zeros((count, slots), F32)
        for k in range(2):
            lane = 2 * side + k
            share += jnp.where(slot == table[:, lane : lane + 1], table[:, 4 + lane : 5 + lane], 0.0)
        high = share.astype(BF16)
        shares.append((high, (share - high.astype(F32)).astype(BF16)))
    chunk = width // 4
    for quarter in range(4):
        part = slice(quarter * chunk, (quarter + 1) * chunk)
        rows = rows_ref[:, part]
        own, other = [dot(high, rows) + dot(low, rows) for high, low in shares]
        own_ref[:, part] = (resid_ref[:, part].astype(F32) + own).astype(BF16)
        other_ref[:, part] = other.astype(BF16)


def combine(lanes, mine, theirs, resid, rows):
    return pl.pallas_call(
        combine_body,
        name="combine",
        in_specs=[whole()] * 5,
        out_specs=[whole()] * 2,
        out_shape=[jax.ShapeDtypeStruct(resid.shape, BF16)] * 2,
        cost_estimate=pl.CostEstimate(flops=1 << 29, bytes_accessed=2 << 20, transcendentals=0),
    )(lanes, mine, theirs, resid, rows)


def moved(shard, where):
    sections, devices = lax.axis_size("section"), lax.axis_size("expert")
    route = []
    for s in range(sections):
        for i in range(devices):
            to_s, to_i = where(s, i)
            route.append((s * devices + i, to_s % sections * devices + to_i))
    return lax.ppermute(shard, ("section", "expert"), route)


def across_cores(shard):
    return moved(shard, lambda s, i: (s ^ 1, i))


def swapped(shard, apart):
    return lax.ppermute(shard, "expert", [(i, i ^ apart) for i in range(lax.axis_size("expert"))])


def shifted(shard, apart):
    size = lax.axis_size("expert")
    return lax.ppermute(shard, "expert", [(i, (i + apart) % size) for i in range(size)])


def gathered_proj(piece, index):
    block = piece
    for apart in (4, 2, 1):
        other = swapped(block, apart)
        upper = (index & apart) != 0
        low = jnp.where(upper, other, block)
        high = jnp.where(upper, block, other)
        rows = piece.shape[0]
        shape = (block.shape[0] // rows, 1, rows, piece.shape[1])
        block = jnp.concatenate([low.reshape(shape), high.reshape(shape)], axis=1)
        block = block.reshape(-1, piece.shape[1])
    onward, backward = [block], [block]
    for step in range(4):
        onward.append(shifted(onward[-1], SIDE))
        if step < 3:
            backward.append(shifted(backward[-1], -SIDE))
    return onward + backward[1:]


def exchanged(blocks, devices):
    rows, width = blocks.shape
    sent = blocks.reshape(devices, rows // devices, width)
    return lax.all_to_all(sent, "expert", split_axis=0, concat_axis=0, tiled=True).reshape(rows, width)


def shards(histories, page_map, user_pages, tails, routes, out_proj, router, w_gate, w_up, w_down):
    devices = lax.axis_size("expert")
    index = lax.axis_index("expert")
    count = histories.shape[1]
    experts = router.shape[2]
    weights = dict(gate=w_gate[0], up=w_up[0], down=w_down[0])
    mine = routes[0].T
    first = {}

    def trade(name):
        first[name] = moved(
            weights[name], lambda s, i: (s, i) if s % 2 == i % 2 else (s ^ 1, i ^ 1)
        )

    trade("gate")
    outgoing = pack_pages(page_map, histories[0], devices)
    arrived = exchanged(outgoing, devices)
    arrived, weights["up"], weights["down"] = lax.optimization_barrier(
        (arrived, weights["up"], weights["down"])
    )
    trade("up")
    trade("down")
    theirs = across_cores(mine)
    core = (lax.axis_index("section") & 1).astype(jnp.int32).reshape(1)
    pick, lanes = slot_tables(core, mine, theirs, experts)
    proj = gathered_proj(out_proj[0], index)
    place = lax.shift_right_logical(index, 3).astype(jnp.int32).reshape(1)
    normed, resid, share = token_stage(
        place, user_pages, tails, page_map, mine, arrived, router[0].T, proj, count
    )
    other_rows = across_cores(normed)
    other_share = across_cores(share)
    packed = pack_rows(pick, normed, other_rows)
    rows = exchanged(packed, devices)
    second = {}
    for name in weights:
        second[name] = across_cores(first[name])
    served = expert_half(rows, first["gate"], first["up"], first["down"])
    served = expert_half(rows, second["gate"], second["up"], second["down"], served)
    result = exchanged(served, devices)
    own, other = combine(lanes, share, other_share, resid, result)
    own = moved(own, lambda s, i: (s + 1, i))
    other = moved(other, lambda s, i: (s, i) if s % 2 else (s + 2, i))
    return (own.astype(F32) + other.astype(F32)).astype(BF16)[None]


def solution(mesh):
    in_specs = (
        P("section", "expert", None),
        P("section", None, "expert"),
        P("section", "expert", None),
        P("section", "expert", None),
        P("section", "expert", None),
        P("section", "expert", None),
        P("section", None, None),
        P("section", None, "expert"),
        P("section", None, "expert"),
        P("section", "expert", None),
    )
    out_specs = P("section", "expert", None)
    return jax.shard_map(
        shards, mesh=mesh, in_specs=in_specs, out_specs=out_specs, check_vma=False
    )
```

time: 290 us -> 312 us (1.076)
  starting transfers between devices: 44.2 us -> 117 us
  Pallas kernels: 0 us -> 30.6 us
  waiting for transfers between devices: 184 us -> 157 us
  local copies, waits for them, and re-layouts: 22.7 us -> 4.66 us
  between operations: 13.8 us -> 0.44 us
  matrix products: 12.5 us -> 0 us
  other arithmetic: 11.4 us -> 0.88 us
    ppermute x3 -> x21, waiting for transfers between devices: 46.3 us -> 130 us  [the longest x3 61.3 us: swapped(): lax.ppermute(shard, 'expert', [(i, i ^ apart) for i in range(lax.axis_siz...]
    ppermute x3 -> x21, starting transfers between devices: 4.99 us -> 66.6 us  [the longest x7 24.4 us: shifted(): lax.ppermute(shard, 'expert', [(i, (i + apart) % size) for i in range(siz...]
    all_to_all x3, waiting for transfers between devices: 84.6 us -> 26.9 us  [exchanged(): lax.all_to_all(sent, 'expert', split_axis=0, concat_axis=0, tiled=True)]
    all_gather x1 -> x0, waiting for transfers between devices: 52.7 us -> none  [shards(): lax.all_gather(out_proj, 'expert', axis=1, tiled=True)[0]]
    pallas_call x0 -> x7, Pallas kernels: none -> 30.6 us  [the longest x2 12 us: expert_half(): pl.pallas_call(functools.partial(expert_body, added), name='expert_half',...]
    dot_general x7 -> x0, matrix products: 12.5 us -> none  [the longest x1 3.76 us: whole_expert(): up_act = jnp.dot(flat_rows, up_full, preferred_element_type=jnp.float32)]
    all_to_all x3, starting transfers between devices: 39.2 us -> 50.1 us  [exchanged(): lax.all_to_all(sent, 'expert', split_axis=0, concat_axis=0, tiled=True)]
    gather x4 -> x0, local copies, waits for them, and re-layouts: 10.9 us -> none  [the longest x1 4.22 us: shards(): outgoing = page_block[chosen_page]]
  transfers between devices with their start and end apart: 7 -> 24, of which waited for: 5 -> 16; matrix products, arithmetic and copies ran while one was open for 9% -> 0% of each run, Pallas kernels for 0% -> 2%
where the time goes in v1:
time: 312 us; the launch traced here: 310 us
  waiting for transfers between devices  157 us (50%)
  starting transfers between devices  117 us (38%)
  Pallas kernels  30.6 us (10%)
  local copies, waits for them, and re-layouts  4.66 us (1%)
    ppermute x3, waiting for transfers between devices, swapped(): lax.ppermute(shard, 'expert', [(i, i ^ apart) for i in range(lax.axis_siz...  61.3 us
    ppermute x11, waiting for transfers between devices, moved(): return lax.ppermute(shard, ('section', 'expert'), route)  54.5 us
    all_to_all x3, starting transfers between devices, exchanged(): lax.all_to_all(sent, 'expert', split_axis=0, concat_axis=0, tiled=True)  50.1 us
    all_to_all x3, waiting for transfers between devices, exchanged(): lax.all_to_all(sent, 'expert', split_axis=0, concat_axis=0, tiled=True)  26.9 us
    ppermute x7, starting transfers between devices, shifted(): lax.ppermute(shard, 'expert', [(i, (i + apart) % size) for i in range(siz...  24.4 us
    ppermute x11, starting transfers between devices, moved(): return lax.ppermute(shard, ('section', 'expert'), route)  23.1 us
    ppermute x3, starting transfers between devices, swapped(): lax.ppermute(shard, 'expert', [(i, i ^ apart) for i in range(lax.axis_siz...  19.1 us
    ppermute x7, waiting for transfers between devices, shifted(): lax.ppermute(shard, 'expert', [(i, (i + apart) % size) for i in range(siz...  14.4 us
  transfers between devices with their start and end apart: 24, of which 16 were waited for; matrix products, arithmetic and copies ran while one was open for 0% of the time, Pallas kernels for 2%

profile of v1, /device:TPU:8, one launch (start us, length us, event | category | flops | bytes accessed | tf_op | source)
XLA Modules:
  0.0 310.3 jit_solution(17369547874335567081)
XLA Ops:
  0.0 5.2 %pack_pages.1 = bf16[512,2560]{1,0:T(8,128)(2,1)} custom-call(s32[1,2,32]{2,1,0:T(2,128)} %map_ref.3, bf16[128,5120]{1,0:T(8,128)(2,1)} %bitcast.55), custom_call_target="tpu_custom_call" | custom-call | flops 1073741824 | bytes 4194304 | tf_op jit(solution)/shard_map/pack_pages/pallas_call | solution.py:62
  5.2 16.7 %all-to-all-start = ((bf16[64,8,2560]{2,1,0:T(8,128)(2,1)}), bf16[64,8,2560]{2,1,0:T(8,128)(2,1)S(1)}, u32[]{:S(2)}, u32[]{:S(2)}) async-start(bf16[64,8,2560]{2,1,0:T(8,128)(2,1)} %bitcast.40), calls=%async_computation | async-start | bytes 5242880 | tf_op jit(solution)/shard_map/all_to_all | solution.py:377
  22.0 6.4 %collective-permute-start.1 = (bf16[16,1024]{1,0:T(8,128)(2,1)S(1)}, bf16[16,1024]{1,0:T(8,128)(2,1)S(1)}, u32[]{:S(2)}, u32[]{:S(2)}) collective-permute-start(bf16[16,1024]{1,0:T(8,128)(2,1)S(1)} %bitcast.54), channel_id=1, source_target_pairs={{0,4},{1,5},{2,6},{3,7},{4,0},{5,1},{6,2},{7,3},{8,12},{9,13},{10,... | collective-permute-start | bytes 98312 | tf_op jit(solution)/shard_map/ppermute | solution.py:347
  28.4 54.9 %collective-permute-done.1 = bf16[16,1024]{1,0:T(8,128)(2,1)S(1)} collective-permute-done((bf16[16,1024]{1,0:T(8,128)(2,1)S(1)}, bf16[16,1024]{1,0:T(8,128)(2,1)S(1)}, u32[]{:S(2)}, u32[]{:S(2)}) %collective-permute-start.1) | collective-permute-done | bytes 32800 | tf_op jit(solution)/shard_map/ppermute | solution.py:347
  83.4 3.6 %collective-permute-start.2 = (bf16[32,1024]{1,0:T(8,128)(2,1)S(1)}, bf16[32,1024]{1,0:T(8,128)(2,1)S(1)}, u32[]{:S(2)}, u32[]{:S(2)}) collective-permute-start(bf16[32,1024]{1,0:T(8,128)(2,1)S(1)} %bitcast.51), channel_id=1, source_target_pairs={{0,2},{1,3},{2,0},{3,1},{4,6},{5,7},{6,4},{7,5},{8,10},{9,11},{10,... | collective-permute-start | bytes 196616 | tf_op jit(solution)/shard_map/ppermute | solution.py:347
  87.0 3.4 %collective-permute-done.2 = bf16[32,1024]{1,0:T(8,128)(2,1)S(1)} collective-permute-done((bf16[32,1024]{1,0:T(8,128)(2,1)S(1)}, bf16[32,1024]{1,0:T(8,128)(2,1)S(1)}, u32[]{:S(2)}, u32[]{:S(2)}) %collective-permute-start.2) | collective-permute-done | bytes 65568 | tf_op jit(solution)/shard_map/ppermute | solution.py:347
  90.5 9.1 %collective-permute-start.3 = (bf16[64,1024]{1,0:T(8,128)(2,1)S(1)}, bf16[64,1024]{1,0:T(8,128)(2,1)S(1)}, u32[]{:S(2)}, u32[]{:S(2)}) collective-permute-start(bf16[64,1024]{1,0:T(8,128)(2,1)S(1)} %bitcast.45), channel_id=1, source_target_pairs={{0,1},{1,0},{2,3},{3,2},{4,5},{5,4},{6,7},{7,6},{8,9},{9,8},{10,11... | collective-permute-start | bytes 393224 | tf_op jit(solution)/shard_map/ppermute | solution.py:347
  104.5 5.1 %collective-permute-start.8 = (bf16[128,1024]{1,0:T(8,128)(2,1)S(1)}, bf16[128,1024]{1,0:T(8,128)(2,1)S(1)}, u32[]{:S(2)}, u32[]{:S(2)}) collective-permute-start(bf16[128,1024]{1,0:T(8,128)(2,1)S(1)} %bitcast.49), channel_id=1, source_target_pairs={{0,56},{1,57},{2,58},{3,59},{4,60},{5,61},{6,62},{7,63},{8,0},{9,1... | collective-permute-start | bytes 786440 | tf_op jit(solution)/shard_map/ppermute | solution.py:352
  114.0 5.8 %collective-permute-start.9 = (bf16[128,1024]{1,0:T(8,128)(2,1)S(1)}, bf16[128,1024]{1,0:T(8,128)(2,1)}, u32[]{:S(2)}, u32[]{:S(2)}) collective-permute-start(bf16[128,1024]{1,0:T(8,128)(2,1)S(1)} %collective-permute-done.8.refs_5_), channel_id=1, source_target_pairs={{0,56},{1,57},{2,58},{3,59},{4,60},{5,61},{6,62},{7,63},{8,0},{9,1... | collective-permute-start | bytes 786440 | tf_op jit(solution)/shard_map/ppermute | solution.py:352
  124.1 5.2 %collective-permute-start.10 = (bf16[128,1024]{1,0:T(8,128)(2,1)}, bf16[128,1024]{1,0:T(8,128)(2,1)}, u32[]{:S(2)}, u32[]{:S(2)}) collective-permute-start(bf16[128,1024]{1,0:T(8,128)(2,1)} %collective-permute-done.9.refs_6_), channel_id=1, source_target_pairs={{0,56},{1,57},{2,58},{3,59},{4,60},{5,61},{6,62},{7,63},{8,0},{9,1... | collective-permute-start | bytes 786440 | tf_op jit(solution)/shard_map/ppermute | solution.py:352
  136.1 5.4 %collective-permute-done.7.refs_4_ = bf16[128,1024]{1,0:T(8,128)(2,1)} collective-permute-done((bf16[128,1024]{1,0:T(8,128)(2,1)}, bf16[128,1024]{1,0:T(8,128)(2,1)}, u32[]{:S(2)}, u32[]{:S(2)}) %collective-permute-start.7) | collective-permute-done | bytes 262176 | tf_op jit(solution)/shard_map/ppermute | solution.py:352
  141.6 6.0 %token_stage.1 = (bf16[128,1024]{1,0:T(8,128)(2,1)}, bf16[128,1024]{1,0:T(8,128)(2,1)}, f32[8,128]{1,0:T(8,128)}) custom-call(s32[1]{0:T(128)} %bitcast.4.place_ref, s32[1,1,4]{2,1,0:T(1,128)} %pages_ref.1, s32[1,1,4]{2,1,0:T(1,128)} %tails_ref.1, s32[1,2,32]{2,1,0:T(2,128)} %map_ref.3, s32[2,128]{1,0:T(2,128)} %bitcast.60, bf16[512,2560]{1,0:T(8,128)(2,1)} %bitcast.39, ...), custom_call_target="tpu_custom_call" | custom-call | flops 2147483648 | bytes 6291456 | tf_op jit(solution)/shard_map/token_stage/pallas_call | solution.py:179
  158.4 20.7 %all-to-all-start.1 = ((bf16[64,8,1024]{2,1,0:T(8,128)(2,1)}), bf16[64,8,1024]{2,1,0:T(8,128)(2,1)S(1)}, u32[]{:S(2)}, u32[]{:S(2)}) async-start(bf16[64,8,1024]{2,1,0:T(8,128)(2,1)} %bitcast.38), calls=%async_computation.1 | async-start | bytes 2097152 | tf_op jit(solution)/shard_map/all_to_all | solution.py:377
  181.2 3.5 %collective-permute-start.15 = (bf16[1024,512]{1,0:T(8,128)(2,1)S(1)}, bf16[1024,512]{1,0:T(8,128)(2,1)}, u32[]{:S(2)}, u32[]{:S(2)}) collective-permute-start(bf16[1024,512]{1,0:T(8,128)(2,1)S(1)} %bitcast.57), channel_id=1, source_target_pairs={{0,0},{1,64},{2,2},{3,66},{4,4},{5,68},{6,6},{7,70},{8,8},{9,72},{... | collective-permute-start | bytes 3145736 | tf_op jit(solution)/shard_map/ppermute | solution.py:339
  186.7 27.3 %collective-permute-done.13.gate_ref = bf16[1024,512]{1,0:T(8,128)(2,1)} collective-permute-done((bf16[1024,512]{1,0:T(8,128)(2,1)S(1)}, bf16[1024,512]{1,0:T(8,128)(2,1)}, u32[]{:S(2)}, u32[]{:S(2)}) %collective-permute-start.13) | collective-permute-done | bytes 1048608 | tf_op jit(solution)/shard_map/ppermute | solution.py:339
  215.9 9.3 %collective-permute-done.15.up_ref = bf16[1024,512]{1,0:T(8,128)(2,1)} collective-permute-done((bf16[1024,512]{1,0:T(8,128)(2,1)S(1)}, bf16[1024,512]{1,0:T(8,128)(2,1)}, u32[]{:S(2)}, u32[]{:S(2)}) %collective-permute-start.15) | collective-permute-done | bytes 1048608 | tf_op jit(solution)/shard_map/ppermute | solution.py:339
  227.2 9.3 %collective-permute-done.17.down_ref = bf16[512,1024]{1,0:T(8,128)(2,1)} collective-permute-done((bf16[512,1024]{1,0:T(8,128)(2,1)}, bf16[512,1024]{1,0:T(8,128)(2,1)}, u32[]{:S(2)}, u32[]{:S(2)}) %collective-permute-start.17) | collective-permute-done | bytes 1048608 | tf_op jit(solution)/shard_map/ppermute | solution.py:339
  239.4 5.7 %expert_half.2.refs_0_ = bf16[512,1024]{1,0:T(8,128)(2,1)} custom-call(bf16[512,1024]{1,0:T(8,128)(2,1)} %bitcast.41, bf16[1024,512]{1,0:T(8,128)(2,1)} %collective-permute-done.13.gate_ref, bf16[1024,512]{1,0:T(8,128)(2,1)} %collective-permute-done.15.up_ref, bf16[512,1024]{1,0:T(8,128)(2,1)} %collective-permute-done.17.down_ref), custom_call_target="tpu_custom_call" | custom-call | flops 2147483648 | bytes 5242880 | tf_op jit(solution)/shard_map/expert_half/pallas_call | solution.py:280
  246.5 6.2 %expert_half.3 = bf16[512,1024]{1,0:T(8,128)(2,1)} custom-call(bf16[512,1024]{1,0:T(8,128)(2,1)} %bitcast.42, bf16[1024,512]{1,0:T(8,128)(2,1)} %copy-done.8, bf16[1024,512]{1,0:T(8,128)(2,1)} %copy-done.9, bf16[512,1024]{1,0:T(8,128)(2,1)} %collective-permute-done.18.down_ref, bf16[512,1024]{1,0:T(8,128)(2,1)} %expert_half.2.refs_0_), custom_call_target="tpu_custom_call" | custom-call | flops 2147483648 | bytes 5242880 | tf_op jit(solution)/shard_map/expert_half/pallas_call | solution.py:280
  252.7 12.6 %all-to-all-start.2 = ((bf16[64,8,1024]{2,1,0:T(8,128)(2,1)}), bf16[64,8,1024]{2,1,0:T(8,128)(2,1)S(1)}, u32[]{:S(2)}, u32[]{:S(2)}) async-start(bf16[64,8,1024]{2,1,0:T(8,128)(2,1)} %bitcast.44), calls=%async_computation.2 | async-start | bytes 2097152 | tf_op jit(solution)/shard_map/all_to_all | solution.py:377
  268.5 26.9 %all-to-all-done.2 = bf16[64,8,1024]{2,1,0:T(8,128)(2,1)S(1)} async-done(((bf16[64,8,1024]{2,1,0:T(8,128)(2,1)}), bf16[64,8,1024]{2,1,0:T(8,128)(2,1)S(1)}, u32[]{:S(2)}, u32[]{:S(2)}) %all-to-all-start.2) | async-done | bytes 1048608 | tf_op jit(solution)/shard_map/all_to_all | solution.py:377
  296.3 3.1 %combine.1 = (bf16[128,1024]{1,0:T(8,128)(2,1)}, bf16[128,1024]{1,0:T(8,128)(2,1)}) custom-call(f32[8,128]{1,0:T(8,128)} %get-tuple-element.15.lanes_ref, f32[8,128]{1,0:T(8,128)} %get-tuple-element.17.mine_ref, f32[8,128]{1,0:T(8,128)} %copy-done.14, bf16[128,1024]{1,0:T(8,128)(2,1)} %get-tuple-element.18.resid_ref, bf16[512,1024]{1,0:T(8,128)(2,1)} %bitcast.43), custom_call_target="tpu_custom_call" | custom-call | flops 536870912 | bytes 2097152 | tf_op jit(solution)/shard_map/combine/pallas_call | solution.py:322
  299.5 3.4 %collective-permute-start.20 = (bf16[128,1024]{1,0:T(8,128)(2,1)}, bf16[128,1024]{1,0:T(8,128)(2,1)S(1)}, u32[]{:S(2)}, u32[]{:S(2)}) collective-permute-start(bf16[128,1024]{1,0:T(8,128)(2,1)} %get-tuple-element.24), channel_id=1, source_target_pairs={{0,128},{1,129},{2,130},{3,131},{4,132},{5,133},{6,134},{7,135},{8... | collective-permute-start | bytes 786440 | tf_op jit(solution)/shard_map/ppermute | solution.py:339
  302.9 4.2 %collective-permute-done.19 = bf16[128,1024]{1,0:T(8,128)(2,1)S(1)} collective-permute-done((bf16[128,1024]{1,0:T(8,128)(2,1)}, bf16[128,1024]{1,0:T(8,128)(2,1)S(1)}, u32[]{:S(2)}, u32[]{:S(2)}) %collective-permute-start.19) | collective-permute-done | bytes 262176 | tf_op jit(solution)/shard_map/ppermute | solution.py:339
  (73 shorter events, 50.6 us)
Async XLA Ops:
  5.2 129.1 %all-to-all-start = ((bf16[64,8,2560]{2,1,0:T(8,128)(2,1)}), bf16[64,8,2560]{2,1,0:T(8,128)(2,1)S(1)}, u32[]{:S(2)}, u32[]{:S(2)}) async-start(bf16[64,8,2560]{2,1,0:T(8,128)(2,1)} %bitcast.40), calls=%async_computation | async-start | bytes 5242880 | tf_op jit(solution)/shard_map/all_to_all | solution.py:377
  22.0 61.3 %collective-permute-start.1 = (bf16[16,1024]{1,0:T(8,128)(2,1)S(1)}, bf16[16,1024]{1,0:T(8,128)(2,1)S(1)}, u32[]{:S(2)}, u32[]{:S(2)}) collective-permute-start(bf16[16,1024]{1,0:T(8,128)(2,1)S(1)} %bitcast.54), channel_id=1, source_target_pairs={{0,4},{1,5},{2,6},{3,7},{4,0},{5,1},{6,2},{7,3},{8,12},{9,13},{10,... | collective-permute-start | bytes 98312 | tf_op jit(solution)/shard_map/ppermute | solution.py:347
  83.4 7.1 %collective-permute-start.2 = (bf16[32,1024]{1,0:T(8,128)(2,1)S(1)}, bf16[32,1024]{1,0:T(8,128)(2,1)S(1)}, u32[]{:S(2)}, u32[]{:S(2)}) collective-permute-start(bf16[32,1024]{1,0:T(8,128)(2,1)S(1)} %bitcast.51), channel_id=1, source_target_pairs={{0,2},{1,3},{2,0},{3,1},{4,6},{5,7},{6,4},{7,5},{8,10},{9,11},{10,... | collective-permute-start | bytes 196616 | tf_op jit(solution)/shard_map/ppermute | solution.py:347
  90.5 12.0 %collective-permute-start.3 = (bf16[64,1024]{1,0:T(8,128)(2,1)S(1)}, bf16[64,1024]{1,0:T(8,128)(2,1)S(1)}, u32[]{:S(2)}, u32[]{:S(2)}) collective-permute-start(bf16[64,1024]{1,0:T(8,128)(2,1)S(1)} %bitcast.45), channel_id=1, source_target_pairs={{0,1},{1,0},{2,3},{3,2},{4,5},{5,4},{6,7},{7,6},{8,9},{9,8},{10,11... | collective-permute-start | bytes 393224 | tf_op jit(solution)/shard_map/ppermute | solution.py:347
  102.6 9.5 %collective-permute-start.4 = (bf16[128,1024]{1,0:T(8,128)(2,1)S(1)}, bf16[128,1024]{1,0:T(8,128)(2,1)S(1)}, u32[]{:S(2)}, u32[]{:S(2)}) collective-permute-start(bf16[128,1024]{1,0:T(8,128)(2,1)S(1)} %bitcast.48), channel_id=1, source_target_pairs={{0,8},{1,9},{2,10},{3,11},{4,12},{5,13},{6,14},{7,15},{8,16},{9,17... | collective-permute-start | bytes 786440 | tf_op jit(solution)/shard_map/ppermute | solution.py:352
  104.5 9.5 %collective-permute-start.8 = (bf16[128,1024]{1,0:T(8,128)(2,1)S(1)}, bf16[128,1024]{1,0:T(8,128)(2,1)S(1)}, u32[]{:S(2)}, u32[]{:S(2)}) collective-permute-start(bf16[128,1024]{1,0:T(8,128)(2,1)S(1)} %bitcast.49), channel_id=1, source_target_pairs={{0,56},{1,57},{2,58},{3,59},{4,60},{5,61},{6,62},{7,63},{8,0},{9,1... | collective-permute-start | bytes 786440 | tf_op jit(solution)/shard_map/ppermute | solution.py:352
  112.1 10.1 %collective-permute-start.5 = (bf16[128,1024]{1,0:T(8,128)(2,1)S(1)}, bf16[128,1024]{1,0:T(8,128)(2,1)S(1)}, u32[]{:S(2)}, u32[]{:S(2)}) collective-permute-start(bf16[128,1024]{1,0:T(8,128)(2,1)S(1)} %collective-permute-done.4.refs_1_), channel_id=1, source_target_pairs={{0,8},{1,9},{2,10},{3,11},{4,12},{5,13},{6,14},{7,15},{8,16},{9,17... | collective-permute-start | bytes 786440 | tf_op jit(solution)/shard_map/ppermute | solution.py:352
  114.0 10.1 %collective-permute-start.9 = (bf16[128,1024]{1,0:T(8,128)(2,1)S(1)}, bf16[128,1024]{1,0:T(8,128)(2,1)}, u32[]{:S(2)}, u32[]{:S(2)}) collective-permute-start(bf16[128,1024]{1,0:T(8,128)(2,1)S(1)} %collective-permute-done.8.refs_5_), channel_id=1, source_target_pairs={{0,56},{1,57},{2,58},{3,59},{4,60},{5,61},{6,62},{7,63},{8,0},{9,1... | collective-permute-start | bytes 786440 | tf_op jit(solution)/shard_map/ppermute | solution.py:352
  122.2 9.6 %collective-permute-start.6 = (bf16[128,1024]{1,0:T(8,128)(2,1)S(1)}, bf16[128,1024]{1,0:T(8,128)(2,1)}, u32[]{:S(2)}, u32[]{:S(2)}) collective-permute-start(bf16[128,1024]{1,0:T(8,128)(2,1)S(1)} %collective-permute-done.5.refs_2_), channel_id=1, source_target_pairs={{0,8},{1,9},{2,10},{3,11},{4,12},{5,13},{6,14},{7,15},{8,16},{9,17... | collective-permute-start | bytes 786440 | tf_op jit(solution)/shard_map/ppermute | solution.py:352
  124.1 12.0 %collective-permute-start.10 = (bf16[128,1024]{1,0:T(8,128)(2,1)}, bf16[128,1024]{1,0:T(8,128)(2,1)}, u32[]{:S(2)}, u32[]{:S(2)}) collective-permute-start(bf16[128,1024]{1,0:T(8,128)(2,1)} %collective-permute-done.9.refs_6_), channel_id=1, source_target_pairs={{0,56},{1,57},{2,58},{3,59},{4,60},{5,61},{6,62},{7,63},{8,0},{9,1... | collective-permute-start | bytes 786440 | tf_op jit(solution)/shard_map/ppermute | solution.py:352
  131.8 9.8 %collective-permute-start.7 = (bf16[128,1024]{1,0:T(8,128)(2,1)}, bf16[128,1024]{1,0:T(8,128)(2,1)}, u32[]{:S(2)}, u32[]{:S(2)}) collective-permute-start(bf16[128,1024]{1,0:T(8,128)(2,1)} %collective-permute-done.6.refs_3_), channel_id=1, source_target_pairs={{0,8},{1,9},{2,10},{3,11},{4,12},{5,13},{6,14},{7,15},{8,16},{9,17... | collective-permute-start | bytes 786440 | tf_op jit(solution)/shard_map/ppermute | solution.py:352
  147.6 7.5 %collective-permute-start.12 = (bf16[128,1024]{1,0:T(8,128)(2,1)}, bf16[128,1024]{1,0:T(8,128)(2,1)S(1)}, u32[]{:S(2)}, u32[]{:S(2)}) collective-permute-start(bf16[128,1024]{1,0:T(8,128)(2,1)} %get-tuple-element.20.mine_ref), channel_id=1, source_target_pairs={{0,64},{1,65},{2,66},{3,67},{4,68},{5,69},{6,70},{7,71},{8,72},{9,... | collective-permute-start | bytes 786440 | tf_op jit(solution)/shard_map/ppermute | solution.py:339
  149.6 3.2 %collective-permute-start = (s32[2,128]{1,0:T(2,128)S(1)}, s32[2,128]{1,0:T(2,128)S(1)}, u32[]{:S(2)}, u32[]{:S(2)}) collective-permute-start(s32[2,128]{1,0:T(2,128)S(1)} %bitcast.62), channel_id=1, source_target_pairs={{0,64},{1,65},{2,66},{3,67},{4,68},{5,69},{6,70},{7,71},{8,72},{9,... | collective-permute-start | bytes 3080 | tf_op jit(solution)/shard_map/ppermute | solution.py:339
  158.4 80.0 %all-to-all-start.1 = ((bf16[64,8,1024]{2,1,0:T(8,128)(2,1)}), bf16[64,8,1024]{2,1,0:T(8,128)(2,1)S(1)}, u32[]{:S(2)}, u32[]{:S(2)}) async-start(bf16[64,8,1024]{2,1,0:T(8,128)(2,1)} %bitcast.38), calls=%async_computation.1 | async-start | bytes 2097152 | tf_op jit(solution)/shard_map/all_to_all | solution.py:377
  179.1 34.9 %collective-permute-start.13 = (bf16[1024,512]{1,0:T(8,128)(2,1)S(1)}, bf16[1024,512]{1,0:T(8,128)(2,1)}, u32[]{:S(2)}, u32[]{:S(2)}) collective-permute-start(bf16[1024,512]{1,0:T(8,128)(2,1)S(1)} %bitcast.56), channel_id=1, source_target_pairs={{0,0},{1,64},{2,2},{3,66},{4,4},{5,68},{6,6},{7,70},{8,8},{9,72},{... | collective-permute-start | bytes 3145736 | tf_op jit(solution)/shard_map/ppermute | solution.py:339
  181.2 44.1 %collective-permute-start.15 = (bf16[1024,512]{1,0:T(8,128)(2,1)S(1)}, bf16[1024,512]{1,0:T(8,128)(2,1)}, u32[]{:S(2)}, u32[]{:S(2)}) collective-permute-start(bf16[1024,512]{1,0:T(8,128)(2,1)S(1)} %bitcast.57), channel_id=1, source_target_pairs={{0,0},{1,64},{2,2},{3,66},{4,4},{5,68},{6,6},{7,70},{8,8},{9,72},{... | collective-permute-start | bytes 3145736 | tf_op jit(solution)/shard_map/ppermute | solution.py:339
  184.7 51.8 %collective-permute-start.17 = (bf16[512,1024]{1,0:T(8,128)(2,1)}, bf16[512,1024]{1,0:T(8,128)(2,1)}, u32[]{:S(2)}, u32[]{:S(2)}) collective-permute-start(bf16[512,1024]{1,0:T(8,128)(2,1)} %bitcast.58), channel_id=1, source_target_pairs={{0,0},{1,64},{2,2},{3,66},{4,4},{5,68},{6,6},{7,70},{8,8},{9,72},{... | collective-permute-start | bytes 3145736 | tf_op jit(solution)/shard_map/ppermute | solution.py:339
  214.0 31.1 %collective-permute-start.14 = (bf16[1024,512]{1,0:T(8,128)(2,1)}, bf16[1024,512]{1,0:T(8,128)(2,1)S(1)}, u32[]{:S(2)}, u32[]{:S(2)}) collective-permute-start(bf16[1024,512]{1,0:T(8,128)(2,1)} %collective-permute-done.13.gate_ref), channel_id=1, source_target_pairs={{0,64},{1,65},{2,66},{3,67},{4,68},{5,69},{6,70},{7,71},{8,72},{9,... | collective-permute-start | bytes 3145736 | tf_op jit(solution)/shard_map/ppermute | solution.py:339
  225.2 19.9 %collective-permute-start.16 = (bf16[1024,512]{1,0:T(8,128)(2,1)}, bf16[1024,512]{1,0:T(8,128)(2,1)S(1)}, u32[]{:S(2)}, u32[]{:S(2)}) collective-permute-start(bf16[1024,512]{1,0:T(8,128)(2,1)} %collective-permute-done.15.up_ref), channel_id=1, source_target_pairs={{0,64},{1,65},{2,66},{3,67},{4,68},{5,69},{6,70},{7,71},{8,72},{9,... | collective-permute-start | bytes 3145736 | tf_op jit(solution)/shard_map/ppermute | solution.py:339
  236.5 8.7 %collective-permute-start.18 = (bf16[512,1024]{1,0:T(8,128)(2,1)}, bf16[512,1024]{1,0:T(8,128)(2,1)}, u32[]{:S(2)}, u32[]{:S(2)}) collective-permute-start(bf16[512,1024]{1,0:T(8,128)(2,1)} %collective-permute-done.17.down_ref), channel_id=1, source_target_pairs={{0,64},{1,65},{2,66},{3,67},{4,68},{5,69},{6,70},{7,71},{8,72},{9,... | collective-permute-start | bytes 3145736 | tf_op jit(solution)/shard_map/ppermute | solution.py:339
  252.7 42.6 %all-to-all-start.2 = ((bf16[64,8,1024]{2,1,0:T(8,128)(2,1)}), bf16[64,8,1024]{2,1,0:T(8,128)(2,1)S(1)}, u32[]{:S(2)}, u32[]{:S(2)}) async-start(bf16[64,8,1024]{2,1,0:T(8,128)(2,1)} %bitcast.44), calls=%async_computation.2 | async-start | bytes 2097152 | tf_op jit(solution)/shard_map/all_to_all | solution.py:377
  265.4 3.1 collective-permute-start.11
  299.5 7.6 %collective-permute-start.19 = (bf16[128,1024]{1,0:T(8,128)(2,1)}, bf16[128,1024]{1,0:T(8,128)(2,1)S(1)}, u32[]{:S(2)}, u32[]{:S(2)}) collective-permute-start(bf16[128,1024]{1,0:T(8,128)(2,1)} %get-tuple-element.23), channel_id=1, source_target_pairs={{0,64},{1,65},{2,66},{3,67},{4,68},{5,69},{6,70},{7,71},{8,72},{9,... | collective-permute-start | bytes 786440 | tf_op jit(solution)/shard_map/ppermute | solution.py:339
  299.5 10.0 %collective-permute-start.20 = (bf16[128,1024]{1,0:T(8,128)(2,1)}, bf16[128,1024]{1,0:T(8,128)(2,1)S(1)}, u32[]{:S(2)}, u32[]{:S(2)}) collective-permute-start(bf16[128,1024]{1,0:T(8,128)(2,1)} %get-tuple-element.24), channel_id=1, source_target_pairs={{0,128},{1,129},{2,130},{3,131},{4,132},{5,133},{6,134},{7,135},{8... | collective-permute-start | bytes 786440 | tf_op jit(solution)/shard_map/ppermute | solution.py:339
  (17 other events, 247.8 us)

commit v2 on v1

--- a/solution.py
+++ b/solution.py
@@ -9,7 +9,6 @@
 
 
 HEADS = 8
-SIDE = 8
 F32 = jnp.float32
 BF16 = jnp.bfloat16
 VMEM = pltpu.VMEM
@@ -90,16 +89,35 @@
 
 
 def token_body(
-    place_ref, pages_ref, tails_ref, map_ref, routes_ref, arrived_ref, router_ref, *refs
+    pages_ref,
+    tails_ref,
+    map_ref,
+    routes_ref,
+    router_ref,
+    arrived_hbm,
+    proj_hbm,
+    normed_ref,
+    resid_ref,
+    share_ref,
+    arrived_ref,
+    proj_ref,
+    mixed_ref,
+    sems,
 ):
-    proj_refs = refs[:SIDE]
-    normed_ref, resid_ref, share_ref, mixed_ref = refs[SIDE:]
-    count = resid_ref.shape[0]
+    count, model_width = resid_ref.shape
     slots = arrived_ref.shape[0]
     half = arrived_ref.shape[1] // 5
     pages = map_ref.shape[2]
-    model_width = 2 * half
     head_dim = model_width // HEADS
+    copies = []
+    for index in range(5):
+        part = pl.ds(index * half, half)
+        copies.append(
+            pltpu.make_async_copy(arrived_hbm.at[:, part], arrived_ref.at[:, part], sems.at[index])
+        )
+    copies.append(pltpu.make_async_copy(proj_hbm, proj_ref, sems.at[5]))
+    for copy in copies:
+        copy.start()
 
     source = lax.shift_right_logical(map_ref[0, 1:2, :], 5).astype(F32)
     mine = lax.shift_right_logical(iota((count, pages), 0), 2) == iota((count, pages), 1)
@@ -110,6 +128,8 @@
     picks = [flag(near & ((slot & 7) == row + 4 * side)) for side in range(2)]
 
     def block(index, side):
+        if side == 0:
+            copies[index].wait()
         return dot(picks[side], arrived_ref[:, index * half : (index + 1) * half])
 
     rows = iota((count, count), 0)
@@ -119,10 +139,9 @@
     allowed = (row_owner == key_owner) & (keys <= rows) & (keys - key_offset < key_length)
     factor = jnp.where(allowed, 1.0 / row_length.astype(F32), 0.0)
     attended = []
+    blocks = [[block(index, side).astype(BF16) for side in range(2)] for index in range(3)]
     for side in range(2):
-        queries = block(0, side).astype(BF16)
-        key_rows = block(1, side).astype(BF16)
-        values = block(2, side).astype(BF16)
+        queries, key_rows, values = [blocks[index][side] for index in range(3)]
         for head in range(HEADS // 2):
             part = slice(head * head_dim, (head + 1) * head_dim)
             scores = dot_t(queries[:, part], key_rows[:, part]) * head_dim ** (-0.5)
@@ -139,20 +158,18 @@
         for head in range(HEADS // 2):
             part = slice(head * head_dim, (head + 1) * head_dim)
             index = side * (HEADS // 2) + head
-            mixed_ref[index] = (attended[index] * scale * gating[:, part]).astype(BF16)
-
-    place = place_ref[0]
-    order = [0, 1, 2, 3, 4, -1, -2, -3]
-    mixed = [mixed_ref[(place - shift) & (SIDE - 1)] for shift in order]
+            mixed = attended[index] * scale * gating[:, part]
+            mixed_ref[:, index * head_dim : (index + 1) * head_dim] = mixed.astype(BF16)
+
     squares = jnp.zeros((count, 1), F32)
     chunk = half // 2
     for side in range(2):
         inputs = block(4, side)
+        if side == 0:
+            copies[5].wait()
         for quarter in range(2):
             part = slice(side * half + quarter * chunk, side * half + (quarter + 1) * chunk)
-            projected = dot(mixed[0], proj_refs[0][:, part])
-            for index in range(1, SIDE):
-                projected += dot(mixed[index], proj_refs[index][:, part])
+            projected = dot(mixed_ref[...], proj_ref[:, part])
             resid = (inputs[:, quarter * chunk : (quarter + 1) * chunk] + projected).astype(BF16)
             resid_ref[:, part] = resid
             wide = resid.astype(F32)
@@ -174,21 +191,27 @@
         share_ref[k : k + 1, :] = chosen[k] / (chosen[0] + chosen[1])
 
 
-def token_stage(place, user_pages, tails, page_map, routes, arrived, router, proj, count):
-    width = arrived.shape[1] // 5 * 2
+def token_stage(user_pages, tails, page_map, routes, router, arrived, proj, count):
+    width = proj.shape[1]
     return pl.pallas_call(
         token_body,
         name="token_stage",
-        in_specs=[whole(SMEM)] * 3 + [whole()] * (4 + SIDE),
+        in_specs=[whole(SMEM)] * 2 + [whole()] * 3 + [whole(pl.ANY)] * 2,
         out_specs=[whole()] * 3,
         out_shape=[
             jax.ShapeDtypeStruct((count, width), BF16),
             jax.ShapeDtypeStruct((count, width), BF16),
             jax.ShapeDtypeStruct((8, count), F32),
         ],
-        scratch_shapes=[pltpu.VMEM((HEADS, count, width // HEADS), BF16)],
+        scratch_shapes=[
+            pltpu.VMEM(arrived.shape, BF16),
+            pltpu.VMEM(proj.shape, BF16),
+            pltpu.VMEM((count, width), BF16),
+            pltpu.SemaphoreType.DMA((6,)),
+        ],
+        compiler_params=pltpu.CompilerParams(vmem_limit_bytes=40 << 20),
         cost_estimate=pl.CostEstimate(flops=2 << 30, bytes_accessed=6 << 20, transcendentals=0),
-    )(place, user_pages, tails, page_map, routes, arrived, router, *proj)
+    )(user_pages, tails, page_map, routes, router, arrived, proj)
 
 
 def slots_body(experts, core_ref, mine_ref, theirs_ref, pick_ref, lanes_ref):
@@ -225,11 +248,15 @@
             jax.ShapeDtypeStruct((rows, 2 * count), BF16),
             jax.ShapeDtypeStruct((8, count), F32),
         ],
+        compiler_params=pltpu.CompilerParams(vmem_limit_bytes=4 << 20),
         cost_estimate=pl.CostEstimate(flops=1 << 24, bytes_accessed=1 << 18, transcendentals=0),
     )(core, mine, theirs)
 
 
-def pack_rows_body(pick_ref, mine_ref, theirs_ref, out_ref):
+def pack_rows_body(pick_ref, mine_ref, theirs_hbm, out_ref, theirs_ref, sem):
+    copy = pltpu.make_async_copy(theirs_hbm, theirs_ref, sem)
+    copy.start()
+    copy.wait()
     _, width = mine_ref.shape
     chunk = width // 4
     for quarter in range(4):
@@ -242,60 +269,94 @@
     return pl.pallas_call(
         pack_rows_body,
         name="pack_rows",
-        in_specs=[whole()] * 3,
+        in_specs=[whole(), whole(), whole(pl.ANY)],
         out_specs=whole(),
         out_shape=jax.ShapeDtypeStruct((pick.shape[0], mine.shape[1]), BF16),
+        scratch_shapes=[pltpu.VMEM(theirs.shape, BF16), pltpu.SemaphoreType.DMA],
+        compiler_params=pltpu.CompilerParams(vmem_limit_bytes=4 << 20),
         cost_estimate=pl.CostEstimate(flops=1 << 28, bytes_accessed=2 << 20, transcendentals=0),
     )(pick, mine, theirs)
 
 
-def expert_body(added, rows_ref, gate_ref, up_ref, down_ref, *refs):
-    out_ref, total_ref = refs[-2:]
-    step = pl.program_id(0)
-    tile = 256
-    for index in range(rows_ref.shape[0] // tile):
-        part = slice(index * tile, (index + 1) * tile)
-        rows = rows_ref[part, :]
-        gate = dot(rows, gate_ref[...])
-        hidden = (gate * jax.nn.sigmoid(gate) * dot(rows, up_ref[...])).astype(BF16)
-        result = dot(hidden, down_ref[...])
-
-        @pl.when(step == 0)
-        def _():
-            total_ref[part, :] = result
-
-        @pl.when(step == 1)
-        def _():
-            half = (total_ref[part, :] + result).astype(BF16)
-            if added:
-                half = (half.astype(F32) + refs[0][part, :].astype(F32)).astype(BF16)
-            out_ref[part, :] = half
-
-
-def expert_half(rows, gate, up, down, earlier=None):
+def expert_body(
+    rows_hbm,
+    gate_hbm,
+    up_hbm,
+    down_hbm,
+    out_ref,
+    rows_ref,
+    gate_ref,
+    up_ref,
+    down_ref,
+    hidden_ref,
+    sems,
+):
+    units = hidden_ref.shape[1]
+    chunk = units // 2
+    width = out_ref.shape[1]
+    rows_copy = pltpu.make_async_copy(rows_hbm, rows_ref, sems.at[0])
+    rows_copy.start()
+    copies = []
+    for half in range(2):
+        for piece in range(2):
+            part = pl.ds(piece * chunk, chunk)
+            for hbm, ref in ((gate_hbm, gate_ref), (up_hbm, up_ref)):
+                copies.append(
+                    pltpu.make_async_copy(
+                        hbm.at[half, :, part], ref.at[half, :, part], sems.at[1 + len(copies)]
+                    )
+                )
+        copies.append(
+            pltpu.make_async_copy(down_hbm.at[half], down_ref.at[half], sems.at[1 + len(copies)])
+        )
+    for copy in copies:
+        copy.start()
+    rows_copy.wait()
+    pending = iter(copies)
+    for half in range(2):
+        for piece in range(2):
+            part = slice(piece * chunk, (piece + 1) * chunk)
+            next(pending).wait()
+            gate = dot(rows_ref[...], gate_ref[half, :, part])
+            next(pending).wait()
+            hidden = gate * jax.nn.sigmoid(gate) * dot(rows_ref[...], up_ref[half, :, part])
+            hidden_ref[:, part] = hidden.astype(BF16)
+        next(pending).wait()
+        for quarter in range(4):
+            part = slice(quarter * width // 4, (quarter + 1) * width // 4)
+            result = dot(hidden_ref[...], down_ref[half, :, part]).astype(BF16)
+            if half == 1:
+                result = (out_ref[:, part].astype(F32) + result.astype(F32)).astype(BF16)
+            out_ref[:, part] = result
+
+
+def expert_stage(rows, gate, up, down):
     count, width = rows.shape
-    chunk = gate.shape[1] // 2
-    added = earlier is not None
-    extra = (earlier,) if added else ()
-    return pl.pallas_call(
-        functools.partial(expert_body, added),
-        name="expert_half",
-        grid=(2,),
-        in_specs=[
-            pl.BlockSpec((count, width), lambda c: (0, 0)),
-            pl.BlockSpec((width, chunk), lambda c: (0, c)),
-            pl.BlockSpec((width, chunk), lambda c: (0, c)),
-            pl.BlockSpec((chunk, width), lambda c: (c, 0)),
-        ]
-        + [pl.BlockSpec((count, width), lambda c: (0, 0))] * len(extra),
-        out_specs=pl.BlockSpec((count, width), lambda c: (0, 0)),
+    units = gate.shape[2]
+    return pl.pallas_call(
+        expert_body,
+        name="expert_stage",
+        in_specs=[whole(pl.ANY)] * 4,
+        out_specs=whole(),
         out_shape=jax.ShapeDtypeStruct((count, width), BF16),
-        scratch_shapes=[pltpu.VMEM((count, width), F32)],
-        cost_estimate=pl.CostEstimate(flops=2 << 30, bytes_accessed=5 << 20, transcendentals=0),
-    )(rows, gate, up, down, *extra)
-
-
-def combine_body(lanes_ref, mine_ref, theirs_ref, resid_ref, rows_ref, own_ref, other_ref):
+        scratch_shapes=[
+            pltpu.VMEM((count, width), BF16),
+            pltpu.VMEM(gate.shape, BF16),
+            pltpu.VMEM(up.shape, BF16),
+            pltpu.VMEM(down.shape, BF16),
+            pltpu.VMEM((count, units), BF16),
+            pltpu.SemaphoreType.DMA((11,)),
+        ],
+        compiler_params=pltpu.CompilerParams(vmem_limit_bytes=50 << 20),
+        cost_estimate=pl.CostEstimate(flops=4 << 30, bytes_accessed=8 << 20, transcendentals=0),
+    )(rows, gate, up, down)
+
+
+def combine_body(
+    lanes_ref, mine_ref, theirs_ref, resid_ref, rows_hbm, own_ref, other_ref, rows_ref, sem
+):
+    copy = pltpu.make_async_copy(rows_hbm, rows_ref, sem)
+    copy.start()
     count, width = resid_ref.shape
     slots = rows_ref.shape[0]
     table = jnp.concatenate([lanes_ref[0:4, :], mine_ref[0:2, :], theirs_ref[0:2, :]], axis=0)
@@ -310,6 +371,7 @@
         high = share.astype(BF16)
         shares.append((high, (share - high.astype(F32)).astype(BF16)))
     chunk = width // 4
+    copy.wait()
     for quarter in range(4):
         part = slice(quarter * chunk, (quarter + 1) * chunk)
         rows = rows_ref[:, part]
@@ -322,9 +384,11 @@
     return pl.pallas_call(
         combine_body,
         name="combine",
-        in_specs=[whole()] * 5,
+        in_specs=[whole()] * 4 + [whole(pl.ANY)],
         out_specs=[whole()] * 2,
         out_shape=[jax.ShapeDtypeStruct(resid.shape, BF16)] * 2,
+        scratch_shapes=[pltpu.VMEM(rows.shape, BF16), pltpu.SemaphoreType.DMA],
+        compiler_params=pltpu.CompilerParams(vmem_limit_bytes=10 << 20),
         cost_estimate=pl.CostEstimate(flops=1 << 29, bytes_accessed=2 << 20, transcendentals=0),
     )(lanes, mine, theirs, resid, rows)
 
@@ -343,79 +407,53 @@
     return moved(shard, lambda s, i: (s ^ 1, i))
 
 
-def swapped(shard, apart):
-    return lax.ppermute(shard, "expert", [(i, i ^ apart) for i in range(lax.axis_size("expert"))])
-
-
-def shifted(shard, apart):
-    size = lax.axis_size("expert")
-    return lax.ppermute(shard, "expert", [(i, (i + apart) % size) for i in range(size)])
-
-
-def gathered_proj(piece, index):
-    block = piece
-    for apart in (4, 2, 1):
-        other = swapped(block, apart)
-        upper = (index & apart) != 0
-        low = jnp.where(upper, other, block)
-        high = jnp.where(upper, block, other)
-        rows = piece.shape[0]
-        shape = (block.shape[0] // rows, 1, rows, piece.shape[1])
-        block = jnp.concatenate([low.reshape(shape), high.reshape(shape)], axis=1)
-        block = block.reshape(-1, piece.shape[1])
-    onward, backward = [block], [block]
-    for step in range(4):
-        onward.append(shifted(onward[-1], SIDE))
-        if step < 3:
-            backward.append(shifted(backward[-1], -SIDE))
-    return onward + backward[1:]
-
-
 def exchanged(blocks, devices):
     rows, width = blocks.shape
     sent = blocks.reshape(devices, rows // devices, width)
     return lax.all_to_all(sent, "expert", split_axis=0, concat_axis=0, tiled=True).reshape(rows, width)
 
 
+def traded(weight):
+    sections, devices = lax.axis_size("section"), lax.axis_size("expert")
+    groups = []
+    for s in range(sections):
+        for i in range(devices):
+            partner = ((s ^ 1), (i ^ 1)) if s % 2 != i % 2 else (s ^ 2 if sections > 2 else s, i ^ 2 * (sections == 2))
+            me, other = s * devices + i, partner[0] * devices + partner[1]
+            if me < other:
+                groups.append([me, other])
+    pair = lax.all_gather(weight, ("section", "expert"), axis_index_groups=groups)
+    section, index = lax.axis_index("section"), lax.axis_index("expert")
+    core = section & 1
+    spot = (section >> 1) & 1 if sections > 2 else (index >> 1) & 1
+    return lax.dynamic_index_in_dim(pair, jnp.where(core != (index & 1), 1 - core, spot), keepdims=False)
+
+
 def shards(histories, page_map, user_pages, tails, routes, out_proj, router, w_gate, w_up, w_down):
     devices = lax.axis_size("expert")
-    index = lax.axis_index("expert")
     count = histories.shape[1]
     experts = router.shape[2]
     weights = dict(gate=w_gate[0], up=w_up[0], down=w_down[0])
     mine = routes[0].T
-    first = {}
-
-    def trade(name):
-        first[name] = moved(
-            weights[name], lambda s, i: (s, i) if s % 2 == i % 2 else (s ^ 1, i ^ 1)
-        )
-
-    trade("gate")
+    pairs = [[s, s + 1] for s in range(0, lax.axis_size("section"), 2)]
+    proj = lax.all_gather(out_proj[0], "expert", axis=0, tiled=True)
+    theirs = across_cores(mine)
     outgoing = pack_pages(page_map, histories[0], devices)
     arrived = exchanged(outgoing, devices)
-    arrived, weights["up"], weights["down"] = lax.optimization_barrier(
-        (arrived, weights["up"], weights["down"])
-    )
-    trade("up")
-    trade("down")
-    theirs = across_cores(mine)
+    both = {}
+    for name, weight in weights.items():
+        first = traded(weight)
+        both[name] = lax.all_gather(first, "section", axis_index_groups=pairs)
     core = (lax.axis_index("section") & 1).astype(jnp.int32).reshape(1)
     pick, lanes = slot_tables(core, mine, theirs, experts)
-    proj = gathered_proj(out_proj[0], index)
-    place = lax.shift_right_logical(index, 3).astype(jnp.int32).reshape(1)
     normed, resid, share = token_stage(
-        place, user_pages, tails, page_map, mine, arrived, router[0].T, proj, count
+        user_pages, tails, page_map, mine, router[0].T, arrived, proj, count
     )
     other_rows = across_cores(normed)
-    other_share = across_cores(share)
     packed = pack_rows(pick, normed, other_rows)
     rows = exchanged(packed, devices)
-    second = {}
-    for name in weights:
-        second[name] = across_cores(first[name])
-    served = expert_half(rows, first["gate"], first["up"], first["down"])
-    served = expert_half(rows, second["gate"], second["up"], second["down"], served)
+    other_share = across_cores(share)
+    served = expert_stage(rows, both["gate"], both["up"], both["down"])
     result = exchanged(served, devices)
     own, other = combine(lanes, share, other_share, resid, result)
     own = moved(own, lambda s, i: (s + 1, i))

time: 312 us -> 384 us (1.23)
  waiting for transfers between devices: 157 us -> 283 us
  starting transfers between devices: 117 us -> 54.7 us
  between operations: 0.44 us -> 13.7 us
  Pallas kernels: 30.6 us -> 22.1 us
    all_gather x0 -> x7, waiting for transfers between devices: none -> 243 us  [the longest x3 111 us: traded(): lax.all_gather(weight, ('section', 'expert'), axis_index_groups=groups)]
    ppermute x10 -> x0, waiting for transfers between devices: 75.7 us -> none  [the longest x3 61.3 us: swapped(): lax.ppermute(shard, 'expert', [(i, i ^ apart) for i in range(lax.axis_siz...]
    ppermute x11 -> x5, waiting for transfers between devices: 54.5 us -> 10.8 us  [moved(): return lax.ppermute(shard, ('section', 'expert'), route)]
    ppermute x10 -> x0, starting transfers between devices: 43.5 us -> none  [the longest x7 24.4 us: shifted(): lax.ppermute(shard, 'expert', [(i, (i + apart) % size) for i in range(siz...]
    ppermute x11 -> x5, starting transfers between devices: 23.1 us -> 10.1 us  [moved(): return lax.ppermute(shard, ('section', 'expert'), route)]
    pallas_call x5 -> x4, Pallas kernels: 23.6 us -> 16.5 us  [the longest x1 9.18 us: expert_stage(): pl.pallas_call(expert_body, name='expert_stage', in_specs=[whole(pl.ANY)]...]
    dynamic_slice x0 -> x3, local copies, waits for them, and re-layouts: none -> 6.86 us  [traded(): lax.dynamic_index_in_dim(pair, jnp.where(core != index & 1, 1 - core, spo...]
    all_to_all x3, starting transfers between devices: 50.1 us -> 44.4 us  [exchanged(): lax.all_to_all(sent, 'expert', split_axis=0, concat_axis=0, tiled=True)]
  transfers between devices with their start and end apart: 24 -> 15, of which waited for: 16 -> 12; matrix products, arithmetic and copies ran while one was open for 0% -> 2% of each run, Pallas kernels for 2% -> 3%
where the time goes in v2:
time: 384 us; the launch traced here: 383 us
  waiting for transfers between devices  283 us (74%)
  starting transfers between devices  54.7 us (14%)
  Pallas kernels  22.1 us (6%)
  between operations  13.7 us (4%)
  local copies, waits for them, and re-layouts  8.46 us (2%)
    all_gather x3, waiting for transfers between devices, traded(): lax.all_gather(weight, ('section', 'expert'), axis_index_groups=groups)  111 us
    all_gather x1, waiting for transfers between devices, shards(): proj = lax.all_gather(out_proj[0], 'expert', axis=0, tiled=True)  86.4 us
    all_gather x3, waiting for transfers between devices, shards(): both[name] = lax.all_gather(first, 'section', axis_index_groups=pairs)  45.3 us
    all_to_all x3, starting transfers between devices, exchanged(): lax.all_to_all(sent, 'expert', split_axis=0, concat_axis=0, tiled=True)  44.4 us
    all_to_all x3, waiting for transfers between devices, exchanged(): lax.all_to_all(sent, 'expert', split_axis=0, concat_axis=0, tiled=True)  26.7 us
    ppermute x5, waiting for transfers between devices, moved(): return lax.ppermute(shard, ('section', 'expert'), route)  10.8 us
    ppermute x5, starting transfers between devices, moved(): return lax.ppermute(shard, ('section', 'expert'), route)  10.1 us
    pallas_call x1, Pallas kernels, expert_stage(): pl.pallas_call(expert_body, name='expert_stage', in_specs=[whole(pl.ANY)]...  9.18 us
  transfers between devices with their start and end apart: 15, of which 12 were waited for; matrix products, arithmetic and copies ran while one was open for 2% of the time, Pallas kernels for 3%

profile of v2, /device:TPU:8, one launch (start us, length us, event | category | flops | bytes accessed | tf_op | source)
XLA Modules:
  0.0 383.0 jit_solution(2776428957147131145)
XLA Ops:
  9.3 5.2 %pack_pages.1 = bf16[512,2560]{1,0:T(8,128)(2,1)} custom-call(s32[1,2,32]{2,1,0:T(2,128)} %map_ref.3, bf16[128,5120]{1,0:T(8,128)(2,1)} %bitcast.26), custom_call_target="tpu_custom_call" | custom-call | flops 1073741824 | bytes 4194304 | tf_op jit(solution)/shard_map/pack_pages/pallas_call | solution.py:61
  14.6 16.6 %all-to-all-start = ((bf16[64,8,2560]{2,1,0:T(8,128)(2,1)}), bf16[64,8,2560]{2,1,0:T(8,128)(2,1)S(1)}, u32[]{:S(2)}, u32[]{:S(2)}) async-start(bf16[64,8,2560]{2,1,0:T(8,128)(2,1)} %bitcast.25), calls=%async_computation | async-start | bytes 5242880 | tf_op jit(solution)/shard_map/all_to_all | solution.py:413
  31.2 57.4 %all-gather.9.cloned.1.call-done = bf16[2,1024,512]{2,1,0:T(8,128)(2,1)} async-done(((bf16[1,1024,512]{2,1,0:T(8,128)(2,1)}), bf16[2,1024,512]{2,1,0:T(8,128)(2,1)}) %all-gather.9.cloned.1.call-update) | async-done | bytes 2097168 | tf_op jit(solution)/shard_map/all_gather | solution.py:425
  88.6 2.3 constant_dynamic-slice_fusion.2
  91.0 34.7 %all-gather.13.cloned.1.call-done = bf16[2,1024,512]{2,1,0:T(8,128)(2,1)} async-done(((bf16[1,1024,512]{2,1,0:T(8,128)(2,1)}), bf16[2,1024,512]{2,1,0:T(8,128)(2,1)}) %all-gather.13.cloned.1.call-update) | async-done | bytes 2097168 | tf_op jit(solution)/shard_map/all_gather | solution.py:425
  125.6 2.3 constant_dynamic-slice_fusion.1
  128.0 86.4 %all-gather.21.cloned.1.call-done = bf16[1,1024,1024]{2,1,0:T(8,128)(2,1)} async-done(((bf16[1,16,1024]{2,1,0:T(8,128)(2,1)}), bf16[1,1024,1024]{2,1,0:T(8,128)(2,1)}) %all-gather.21.cloned.1.call-update) | async-done | bytes 2097168 | tf_op jit(solution)/shard_map/all_gather | solution.py:439
  214.5 1.6 copy-done
  216.1 4.7 %token_stage.1 = (bf16[128,1024]{1,0:T(8,128)(2,1)S(1)}, bf16[128,1024]{1,0:T(8,128)(2,1)S(1)}, f32[8,128]{1,0:T(8,128)S(1)}) custom-call(s32[1,1,4]{2,1,0:T(1,128)S(1)} %copy-done.4, s32[1,1,4]{2,1,0:T(1,128)S(1)} %copy-done.5, s32[1,2,32]{2,1,0:T(2,128)S(1)} %copy-done.2, s32[2,128]{1,0:T(2,128)S(1)} %bitcast.22, bf16[32,1024]{1,0:T(8,128)(2,1)S(1)} %bitcast.21, ...), custom_call_target="tpu_custom_call" | custom-call | flops 2147483648 | bytes 6291456 | tf_op jit(solution)/shard_map/token_stage/pallas_call | solution.py:196
  220.8 1.9 collective-permute-start.2
  222.7 19.4 %all-gather.17.cloned.1.call-done = bf16[2,512,1024]{2,1,0:T(8,128)(2,1)} async-done(((bf16[1,512,1024]{2,1,0:T(8,128)(2,1)}), bf16[2,512,1024]{2,1,0:T(8,128)(2,1)}) %all-gather.17.cloned.1.call-update) | async-done | bytes 2097168 | tf_op jit(solution)/shard_map/all_gather | solution.py:425
  242.1 2.2 constant_dynamic-slice_fusion
  244.4 2.9 collective-permute-start
  248.4 1.5 pack_rows.1
  249.9 14.4 %all-to-all-start.1 = ((bf16[64,8,1024]{2,1,0:T(8,128)(2,1)}), bf16[64,8,1024]{2,1,0:T(8,128)(2,1)S(1)}, u32[]{:S(2)}, u32[]{:S(2)}) async-start(bf16[64,8,1024]{2,1,0:T(8,128)(2,1)} %bitcast.10), calls=%async_computation.1 | async-start | bytes 2097152 | tf_op jit(solution)/shard_map/all_to_all | solution.py:413
  264.3 1.2 all-gather.11.cloned.1.call-done.gate_hbm
  265.5 22.0 %all-gather.15.cloned.1.call-done.up_hbm = bf16[2,1024,512]{2,1,0:T(8,128)(2,1)} async-done(((bf16[1,1024,512]{2,1,0:T(8,128)(2,1)}), bf16[2,1024,512]{2,1,0:T(8,128)(2,1)}) %all-gather.15.cloned.1.call-update) | async-done | bytes 2097168 | tf_op jit(solution)/shard_map/all_gather | solution.py:446
  287.5 22.1 %all-gather.19.cloned.1.call-done.down_hbm = bf16[2,512,1024]{2,1,0:T(8,128)(2,1)} async-done(((bf16[1,512,1024]{2,1,0:T(8,128)(2,1)}), bf16[2,512,1024]{2,1,0:T(8,128)(2,1)}) %all-gather.19.cloned.1.call-update) | async-done | bytes 2097168 | tf_op jit(solution)/shard_map/all_gather | solution.py:446
  309.6 9.2 %expert_stage.1 = bf16[512,1024]{1,0:T(8,128)(2,1)} custom-call(bf16[512,1024]{1,0:T(8,128)(2,1)S(1)} %bitcast.18, bf16[2,1024,512]{2,1,0:T(8,128)(2,1)} %all-gather.11.cloned.1.call-done.gate_hbm, bf16[2,1024,512]{2,1,0:T(8,128)(2,1)} %all-gather.15.cloned.1.call-done.up_hbm, bf16[2,512,1024]{2,1,0:T(8,128)(2,1)} %all-gather.19.cloned.1.call-done.down_hbm), custom_call_target="tpu_custom_call" | custom-call | flops 4294967296 | bytes 8388608 | tf_op jit(solution)/shard_map/expert_stage/pallas_call | solution.py:336
  318.8 13.4 %all-to-all-start.2 = ((bf16[64,8,1024]{2,1,0:T(8,128)(2,1)}), bf16[64,8,1024]{2,1,0:T(8,128)(2,1)S(1)}, u32[]{:S(2)}, u32[]{:S(2)}) async-start(bf16[64,8,1024]{2,1,0:T(8,128)(2,1)} %bitcast.12), calls=%async_computation.2 | async-start | bytes 2097152 | tf_op jit(solution)/shard_map/all_to_all | solution.py:413
  332.2 1.9 collective-permute-start.1
  335.3 26.6 %all-to-all-done.2 = bf16[64,8,1024]{2,1,0:T(8,128)(2,1)S(1)} async-done(((bf16[64,8,1024]{2,1,0:T(8,128)(2,1)}), bf16[64,8,1024]{2,1,0:T(8,128)(2,1)S(1)}, u32[]{:S(2)}, u32[]{:S(2)}) %all-to-all-start.2) | async-done | bytes 1048608 | tf_op jit(solution)/shard_map/all_to_all | solution.py:413
  363.1 3.4 collective-permute-start.4
  366.5 7.9 %collective-permute-done.4 = bf16[128,1024]{1,0:T(8,128)(2,1)S(1)} collective-permute-done((bf16[128,1024]{1,0:T(8,128)(2,1)S(1)}, bf16[128,1024]{1,0:T(8,128)(2,1)S(1)}, u32[]{:S(2)}, u32[]{:S(2)}) %collective-permute-start.4) | collective-permute-done | bytes 262176 | tf_op jit(solution)/shard_map/ppermute | solution.py:403
  (35 shorter events, 8.1 us)
Async XLA Ops:
  6.5 82.1 %all-gather.9.cloned.1.call-start = ((), (), s32[]{:S(2)}) async-start(), calls=%async_computation.3 | async-start | bytes 3145728 | tf_op jit(solution)/shard_map/all_gather | solution.py:425
  7.3 118.4 %all-gather.13.cloned.1.call-start = ((), (), s32[]{:S(2)}) async-start(), calls=%async_computation.5 | async-start | bytes 3145728 | tf_op jit(solution)/shard_map/all_gather | solution.py:425
  8.0 206.4 %all-gather.21.cloned.1.call-start = ((), (), s32[]{:S(2)}) async-start(), calls=%async_computation.9 | async-start | bytes 2129920 | tf_op jit(solution)/shard_map/all_gather | solution.py:439
  8.7 233.4 %all-gather.17.cloned.1.call-start = ((), (), s32[]{:S(2)}) async-start(), calls=%async_computation.7 | async-start | bytes 3145728 | tf_op jit(solution)/shard_map/all_gather | solution.py:425
  14.6 199.9 %all-to-all-start = ((bf16[64,8,2560]{2,1,0:T(8,128)(2,1)}), bf16[64,8,2560]{2,1,0:T(8,128)(2,1)S(1)}, u32[]{:S(2)}, u32[]{:S(2)}) async-start(bf16[64,8,2560]{2,1,0:T(8,128)(2,1)} %bitcast.25), calls=%async_computation | async-start | bytes 5242880 | tf_op jit(solution)/shard_map/all_to_all | solution.py:413
  31.1 234.4 %all-gather.11.cloned.1.call-start = ((), (), s32[]{:S(2)}) async-start(), calls=%async_computation.4 | async-start | bytes 3145728 | tf_op jit(solution)/shard_map/all_gather | solution.py:446
  90.9 123.6 %copy-start.1 = (bf16[1,1024,32]{1,2,0:T(8,128)(2,1)S(1)}, bf16[1,1024,32]{1,2,0:T(8,128)(2,1)}, u32[]{:S(2)}) copy-start(bf16[1,1024,32]{1,2,0:T(8,128)(2,1)} %param.16) | copy-start | bytes 196612
  90.9 123.6 %copy-start.2 = (s32[1,2,32]{2,1,0:T(2,128)S(1)}, s32[1,2,32]{2,1,0:T(2,128)}, u32[]{:S(2)}) copy-start(s32[1,2,32]{2,1,0:T(2,128)} %map_ref.3) | copy-start | bytes 772
  90.9 123.6 %copy-start.3 = (s32[1,128,2]{1,2,0:T(2,128)S(1)}, s32[1,128,2]{1,2,0:T(2,128)}, u32[]{:S(2)}) copy-start(s32[1,128,2]{1,2,0:T(2,128)} %param.14) | copy-start | bytes 3076
  90.9 123.6 %copy-start.4 = (s32[1,1,4]{2,1,0:T(1,128)S(1)}, s32[1,1,4]{2,1,0:T(1,128)}, u32[]{:S(2)}) copy-start(s32[1,1,4]{2,1,0:T(1,128)} %pages_ref.1) | copy-start | bytes 52
  90.9 123.6 %copy-start.5 = (s32[1,1,4]{2,1,0:T(1,128)S(1)}, s32[1,1,4]{2,1,0:T(1,128)}, u32[]{:S(2)}) copy-start(s32[1,1,4]{2,1,0:T(1,128)} %tails_ref.1) | copy-start | bytes 52
  90.9 196.6 %all-gather.15.cloned.1.call-start = ((), (), s32[]{:S(2)}) async-start(), calls=%async_computation.6 | async-start | bytes 3145728 | tf_op jit(solution)/shard_map/all_gather | solution.py:446
  128.0 181.6 %all-gather.19.cloned.1.call-start = ((), (), s32[]{:S(2)}) async-start(), calls=%async_computation.8 | async-start | bytes 3145728 | tf_op jit(solution)/shard_map/all_gather | solution.py:446
  214.5 1.6 copy-start
  220.8 27.7 %collective-permute-start.2 = (bf16[128,1024]{1,0:T(8,128)(2,1)S(1)}, bf16[128,1024]{1,0:T(8,128)(2,1)S(1)}, u32[]{:S(2)}, u32[]{:S(2)}) collective-permute-start(bf16[128,1024]{1,0:T(8,128)(2,1)S(1)} %get-tuple-element.16.mine_ref), channel_id=1, source_target_pairs={{0,64},{1,65},{2,66},{3,67},{4,68},{5,69},{6,70},{7,71},{8,72},{9,... | collective-permute-start | bytes 786440 | tf_op jit(solution)/shard_map/ppermute | solution.py:403
  244.4 3.7 collective-permute-start
  249.9 59.8 %all-to-all-start.1 = ((bf16[64,8,1024]{2,1,0:T(8,128)(2,1)}), bf16[64,8,1024]{2,1,0:T(8,128)(2,1)S(1)}, u32[]{:S(2)}, u32[]{:S(2)}) async-start(bf16[64,8,1024]{2,1,0:T(8,128)(2,1)} %bitcast.10), calls=%async_computation.1 | async-start | bytes 2097152 | tf_op jit(solution)/shard_map/all_to_all | solution.py:413
  318.8 43.1 %all-to-all-start.2 = ((bf16[64,8,1024]{2,1,0:T(8,128)(2,1)}), bf16[64,8,1024]{2,1,0:T(8,128)(2,1)S(1)}, u32[]{:S(2)}, u32[]{:S(2)}) async-start(bf16[64,8,1024]{2,1,0:T(8,128)(2,1)} %bitcast.12), calls=%async_computation.2 | async-start | bytes 2097152 | tf_op jit(solution)/shard_map/all_to_all | solution.py:413
  332.2 3.1 collective-permute-start.1
  363.1 11.4 %collective-permute-start.4 = (bf16[128,1024]{1,0:T(8,128)(2,1)S(1)}, bf16[128,1024]{1,0:T(8,128)(2,1)S(1)}, u32[]{:S(2)}, u32[]{:S(2)}) collective-permute-start(bf16[128,1024]{1,0:T(8,128)(2,1)S(1)} %get-tuple-element.18), channel_id=1, source_target_pairs={{0,128},{1,129},{2,130},{3,131},{4,132},{5,133},{6,134},{7,135},{8... | collective-permute-start | bytes 786440 | tf_op jit(solution)/shard_map/ppermute | solution.py:403
  366.5 8.9 %collective-permute-start.3 = (bf16[128,1024]{1,0:T(8,128)(2,1)S(1)}, bf16[128,1024]{1,0:T(8,128)(2,1)S(1)}, u32[]{:S(2)}, u32[]{:S(2)}) collective-permute-start(bf16[128,1024]{1,0:T(8,128)(2,1)S(1)} %get-tuple-element.17), channel_id=1, source_target_pairs={{0,64},{1,65},{2,66},{3,67},{4,68},{5,69},{6,70},{7,71},{8,72},{9,... | collective-permute-start | bytes 786440 | tf_op jit(solution)/shard_map/ppermute | solution.py:403
Sparse Core Ops, SparseCore 0:
  9.4 79.1 all-gather.8
  90.7 34.9 all-gather.12
  128.7 85.6 all-gather.20
  216.4 25.7 all-gather.16
  244.1 21.3 all-gather.10
  267.4 20.0 all-gather.14
  289.6 20.0 all-gather.18

commit v3 on v2

--- a/solution.py
+++ b/solution.py
@@ -9,6 +9,7 @@
 
 
 HEADS = 8
+RING = (0, 1, 2, 3, 4, -1, -2, -3)
 F32 = jnp.float32
 BF16 = jnp.bfloat16
 VMEM = pltpu.VMEM
@@ -94,16 +95,12 @@
     map_ref,
     routes_ref,
     router_ref,
+    place_ref,
     arrived_hbm,
-    proj_hbm,
-    normed_ref,
-    resid_ref,
-    share_ref,
-    arrived_ref,
-    proj_ref,
-    mixed_ref,
-    sems,
+    *refs,
 ):
+    proj_hbm = refs[: len(RING)]
+    normed_ref, resid_ref, share_ref, arrived_ref, proj_ref, mixed_ref, sems = refs[len(RING) :]
     count, model_width = resid_ref.shape
     slots = arrived_ref.shape[0]
     half = arrived_ref.shape[1] // 5
@@ -115,7 +112,11 @@
         copies.append(
             pltpu.make_async_copy(arrived_hbm.at[:, part], arrived_ref.at[:, part], sems.at[index])
         )
-    copies.append(pltpu.make_async_copy(proj_hbm, proj_ref, sems.at[5]))
+    for index, shift in enumerate(RING):
+        rows = proj_hbm[index].shape[0]
+        start = pl.multiple_of(((place_ref[0] - shift) & (len(RING) - 1)) * rows, rows)
+        target = proj_ref.at[pl.ds(start, rows)]
+        copies.append(pltpu.make_async_copy(proj_hbm[index], target, sems.at[5 + index]))
     for copy in copies:
         copy.start()
 
@@ -166,7 +167,8 @@
     for side in range(2):
         inputs = block(4, side)
         if side == 0:
-            copies[5].wait()
+            for copy in copies[5:]:
+                copy.wait()
         for quarter in range(2):
             part = slice(side * half + quarter * chunk, side * half + (quarter + 1) * chunk)
             projected = dot(mixed_ref[...], proj_ref[:, part])
@@ -191,12 +193,12 @@
         share_ref[k : k + 1, :] = chosen[k] / (chosen[0] + chosen[1])
 
 
-def token_stage(user_pages, tails, page_map, routes, router, arrived, proj, count):
-    width = proj.shape[1]
+def token_stage(user_pages, tails, page_map, routes, router, place, arrived, proj, count):
+    depth, width = proj[0].shape
     return pl.pallas_call(
         token_body,
         name="token_stage",
-        in_specs=[whole(SMEM)] * 2 + [whole()] * 3 + [whole(pl.ANY)] * 2,
+        in_specs=[whole(SMEM)] * 2 + [whole()] * 3 + [whole(SMEM)] + [whole(pl.ANY)] * (1 + len(RING)),
         out_specs=[whole()] * 3,
         out_shape=[
             jax.ShapeDtypeStruct((count, width), BF16),
@@ -205,13 +207,13 @@
         ],
         scratch_shapes=[
             pltpu.VMEM(arrived.shape, BF16),
-            pltpu.VMEM(proj.shape, BF16),
+            pltpu.VMEM((depth * len(RING), width), BF16),
             pltpu.VMEM((count, width), BF16),
-            pltpu.SemaphoreType.DMA((6,)),
+            pltpu.SemaphoreType.DMA((5 + len(RING),)),
         ],
         compiler_params=pltpu.CompilerParams(vmem_limit_bytes=40 << 20),
         cost_estimate=pl.CostEstimate(flops=2 << 30, bytes_accessed=6 << 20, transcendentals=0),
-    )(user_pages, tails, page_map, routes, router, arrived, proj)
+    )(user_pages, tails, page_map, routes, router, place, arrived, *proj)
 
 
 def slots_body(experts, core_ref, mine_ref, theirs_ref, pick_ref, lanes_ref):
@@ -278,19 +280,9 @@
     )(pick, mine, theirs)
 
 
-def expert_body(
-    rows_hbm,
-    gate_hbm,
-    up_hbm,
-    down_hbm,
-    out_ref,
-    rows_ref,
-    gate_ref,
-    up_ref,
-    down_ref,
-    hidden_ref,
-    sems,
-):
+def expert_body(rows_hbm, *refs):
+    weights_hbm = (refs[0:3], refs[3:6])
+    out_ref, rows_ref, gate_ref, up_ref, down_ref, hidden_ref, sems = refs[6:]
     units = hidden_ref.shape[1]
     chunk = units // 2
     width = out_ref.shape[1]
@@ -298,17 +290,14 @@
     rows_copy.start()
     copies = []
     for half in range(2):
+        gate_hbm, up_hbm, down_hbm = weights_hbm[half]
         for piece in range(2):
             part = pl.ds(piece * chunk, chunk)
             for hbm, ref in ((gate_hbm, gate_ref), (up_hbm, up_ref)):
-                copies.append(
-                    pltpu.make_async_copy(
-                        hbm.at[half, :, part], ref.at[half, :, part], sems.at[1 + len(copies)]
-                    )
-                )
-        copies.append(
-            pltpu.make_async_copy(down_hbm.at[half], down_ref.at[half], sems.at[1 + len(copies)])
-        )
+                sem = sems.at[1 + len(copies)]
+                copies.append(pltpu.make_async_copy(hbm.at[:, part], ref.at[half, :, part], sem))
+        sem = sems.at[1 + len(copies)]
+        copies.append(pltpu.make_async_copy(down_hbm, down_ref.at[half], sem))
     for copy in copies:
         copy.start()
     rows_copy.wait()
@@ -330,26 +319,26 @@
             out_ref[:, part] = result
 
 
-def expert_stage(rows, gate, up, down):
+def expert_stage(rows, first, second):
     count, width = rows.shape
-    units = gate.shape[2]
+    units = first[0].shape[1]
     return pl.pallas_call(
         expert_body,
         name="expert_stage",
-        in_specs=[whole(pl.ANY)] * 4,
+        in_specs=[whole(pl.ANY)] * 7,
         out_specs=whole(),
         out_shape=jax.ShapeDtypeStruct((count, width), BF16),
         scratch_shapes=[
             pltpu.VMEM((count, width), BF16),
-            pltpu.VMEM(gate.shape, BF16),
-            pltpu.VMEM(up.shape, BF16),
-            pltpu.VMEM(down.shape, BF16),
+            pltpu.VMEM((2, width, units), BF16),
+            pltpu.VMEM((2, width, units), BF16),
+            pltpu.VMEM((2, units, width), BF16),
             pltpu.VMEM((count, units), BF16),
             pltpu.SemaphoreType.DMA((11,)),
         ],
         compiler_params=pltpu.CompilerParams(vmem_limit_bytes=50 << 20),
         cost_estimate=pl.CostEstimate(flops=4 << 30, bytes_accessed=8 << 20, transcendentals=0),
-    )(rows, gate, up, down)
+    )(rows, *first, *second)
 
 
 def combine_body(
@@ -413,20 +402,26 @@
     return lax.all_to_all(sent, "expert", split_axis=0, concat_axis=0, tiled=True).reshape(rows, width)
 
 
-def traded(weight):
-    sections, devices = lax.axis_size("section"), lax.axis_size("expert")
-    groups = []
-    for s in range(sections):
-        for i in range(devices):
-            partner = ((s ^ 1), (i ^ 1)) if s % 2 != i % 2 else (s ^ 2 if sections > 2 else s, i ^ 2 * (sections == 2))
-            me, other = s * devices + i, partner[0] * devices + partner[1]
-            if me < other:
-                groups.append([me, other])
-    pair = lax.all_gather(weight, ("section", "expert"), axis_index_groups=groups)
-    section, index = lax.axis_index("section"), lax.axis_index("expert")
-    core = section & 1
-    spot = (section >> 1) & 1 if sections > 2 else (index >> 1) & 1
-    return lax.dynamic_index_in_dim(pair, jnp.where(core != (index & 1), 1 - core, spot), keepdims=False)
+def shifted(shard, apart):
+    size = lax.axis_size("expert")
+    return lax.ppermute(shard, "expert", [(i, (i + apart) % size) for i in range(size)])
+
+
+def gathered_proj(piece):
+    side = len(RING)
+    devices = lax.axis_size("expert")
+    groups = [list(range(start, start + side)) for start in range(0, devices, side)]
+    copies = jnp.broadcast_to(piece[None], (side,) + piece.shape)
+    block = lax.all_to_all(
+        copies, "expert", split_axis=0, concat_axis=0, tiled=True, axis_index_groups=groups
+    )
+    block = block.reshape(-1, piece.shape[1])
+    blocks = {0: block}
+    for step in range(1, side // 2 + 1):
+        blocks[step] = shifted(blocks[step - 1], side)
+        if step < side // 2:
+            blocks[-step] = shifted(blocks[1 - step], -side)
+    return [blocks[shift] for shift in RING]
 
 
 def shards(histories, page_map, user_pages, tails, routes, out_proj, router, w_gate, w_up, w_down):
@@ -435,25 +430,25 @@
     experts = router.shape[2]
     weights = dict(gate=w_gate[0], up=w_up[0], down=w_down[0])
     mine = routes[0].T
-    pairs = [[s, s + 1] for s in range(0, lax.axis_size("section"), 2)]
-    proj = lax.all_gather(out_proj[0], "expert", axis=0, tiled=True)
-    theirs = across_cores(mine)
+    proj = gathered_proj(out_proj[0])
+    first, second = [], []
+    for weight in weights.values():
+        first.append(moved(weight, lambda s, i: (s, i) if s % 2 == i % 2 else (s ^ 1, i ^ 1)))
+        second.append(across_cores(first[-1]))
     outgoing = pack_pages(page_map, histories[0], devices)
     arrived = exchanged(outgoing, devices)
-    both = {}
-    for name, weight in weights.items():
-        first = traded(weight)
-        both[name] = lax.all_gather(first, "section", axis_index_groups=pairs)
+    theirs = across_cores(mine)
     core = (lax.axis_index("section") & 1).astype(jnp.int32).reshape(1)
+    place = lax.shift_right_logical(lax.axis_index("expert"), 3).astype(jnp.int32).reshape(1)
     pick, lanes = slot_tables(core, mine, theirs, experts)
     normed, resid, share = token_stage(
-        user_pages, tails, page_map, mine, router[0].T, arrived, proj, count
+        user_pages, tails, page_map, mine, router[0].T, place, arrived, proj, count
     )
     other_rows = across_cores(normed)
     packed = pack_rows(pick, normed, other_rows)
     rows = exchanged(packed, devices)
     other_share = across_cores(share)
-    served = expert_stage(rows, both["gate"], both["up"], both["down"])
+    served = expert_stage(rows, first, second)
     result = exchanged(served, devices)
     own, other = combine(lanes, share, other_share, resid, result)
     own = moved(own, lambda s, i: (s + 1, i))

time: 384 us -> 267 us (0.70)
  waiting for transfers between devices: 283 us -> 128 us
  starting transfers between devices: 54.7 us -> 106 us
  between operations: 13.7 us -> 0.36 us
    all_gather x7 -> x0, waiting for transfers between devices: 243 us -> none  [the longest x3 111 us: traded(): lax.all_gather(weight, ('section', 'expert'), axis_index_groups=groups)]
    ppermute x0 -> x7, waiting for transfers between devices: none -> 67.9 us  [shifted(): lax.ppermute(shard, 'expert', [(i, (i + apart) % size) for i in range(siz...]
    ppermute x5 -> x11, starting transfers between devices: 10.1 us -> 36.6 us  [moved(): return lax.ppermute(shard, ('section', 'expert'), route)]
    ppermute x0 -> x7, starting transfers between devices: none -> 23 us  [shifted(): lax.ppermute(shard, 'expert', [(i, (i + apart) % size) for i in range(siz...]
    all_to_all x3, waiting for transfers between devices: 26.7 us -> 46 us  [exchanged(): lax.all_to_all(sent, 'expert', split_axis=0, concat_axis=0, tiled=True)]
    all_to_all x0 -> x1, starting transfers between devices: none -> 9.11 us  [gathered_proj(): lax.all_to_all(copies, 'expert', split_axis=0, concat_axis=0, tiled=True,...]
    all_to_all x3, starting transfers between devices: 44.4 us -> 37.1 us  [exchanged(): lax.all_to_all(sent, 'expert', split_axis=0, concat_axis=0, tiled=True)]
    dynamic_slice x3 -> x0, local copies, waits for them, and re-layouts: 6.86 us -> none  [traded(): lax.dynamic_index_in_dim(pair, jnp.where(core != index & 1, 1 - core, spo...]
  transfers between devices with their start and end apart: 15 -> 22, of which waited for: 12 -> 14; matrix products, arithmetic and copies ran while one was open for 2% -> 0% of each run, Pallas kernels for 3% -> 3%
where the time goes in v3:
time: 267 us; the launch traced here: 265 us
  waiting for transfers between devices  128 us (48%)
  starting transfers between devices  106 us (40%)
  Pallas kernels  21.4 us (8%)
  local copies, waits for them, and re-layouts  8.13 us (3%)
    ppermute x7, waiting for transfers between devices, shifted(): lax.ppermute(shard, 'expert', [(i, (i + apart) % size) for i in range(siz...  67.9 us
    all_to_all x3, waiting for transfers between devices, exchanged(): lax.all_to_all(sent, 'expert', split_axis=0, concat_axis=0, tiled=True)  46 us
    all_to_all x3, starting transfers between devices, exchanged(): lax.all_to_all(sent, 'expert', split_axis=0, concat_axis=0, tiled=True)  37.1 us
    ppermute x11, starting transfers between devices, moved(): return lax.ppermute(shard, ('section', 'expert'), route)  36.6 us
    ppermute x7, starting transfers between devices, shifted(): lax.ppermute(shard, 'expert', [(i, (i + apart) % size) for i in range(siz...  23 us
    ppermute x11, waiting for transfers between devices, moved(): return lax.ppermute(shard, ('section', 'expert'), route)  10.3 us
    all_to_all x1, starting transfers between devices, gathered_proj(): lax.all_to_all(copies, 'expert', split_axis=0, concat_axis=0, tiled=True,...  9.11 us
    pallas_call x1, Pallas kernels, expert_stage(): pl.pallas_call(expert_body, name='expert_stage', in_specs=[whole(pl.ANY)]...  8.52 us
  transfers between devices with their start and end apart: 22, of which 14 were waited for; matrix products, arithmetic and copies ran while one was open for 0% of the time, Pallas kernels for 3%

profile of v3, /device:TPU:8, one launch (start us, length us, event | category | flops | bytes accessed | tf_op | source)
XLA Modules:
  0.0 264.6 jit_solution(14595182733163604304)
XLA Ops:
  1.5 9.1 %all-to-all-start.1 = ((bf16[8,16,1024]{2,1,0:T(8,128)(2,1)}), bf16[8,16,1024]{2,1,0:T(8,128)(2,1)S(1)}, u32[]{:S(2)}, u32[]{:S(2)}) async-start(bf16[8,16,1024]{2,1,0:T(8,128)(2,1)} %broadcast_in_dim.11), calls=%async_computation.1 | async-start | bytes 524288 | tf_op jit(solution)/shard_map/all_to_all | solution.py:415
  10.6 5.2 %pack_pages.1 = bf16[512,2560]{1,0:T(8,128)(2,1)} custom-call(s32[1,2,32]{2,1,0:T(2,128)} %map_ref.3, bf16[128,5120]{1,0:T(8,128)(2,1)} %bitcast.34), custom_call_target="tpu_custom_call" | custom-call | flops 1073741824 | bytes 4194304 | tf_op jit(solution)/shard_map/pack_pages/pallas_call | solution.py:62
  15.8 3.8 %all-to-all-done.1 = bf16[8,16,1024]{2,1,0:T(8,128)(2,1)S(1)} async-done(((bf16[8,16,1024]{2,1,0:T(8,128)(2,1)}), bf16[8,16,1024]{2,1,0:T(8,128)(2,1)S(1)}, u32[]{:S(2)}, u32[]{:S(2)}) %all-to-all-start.1) | async-done | bytes 262176 | tf_op jit(solution)/shard_map/all_to_all | solution.py:415
  19.7 12.3 %all-to-all-start = ((bf16[64,8,2560]{2,1,0:T(8,128)(2,1)}), bf16[64,8,2560]{2,1,0:T(8,128)(2,1)S(1)}, u32[]{:S(2)}, u32[]{:S(2)}) async-start(bf16[64,8,2560]{2,1,0:T(8,128)(2,1)} %bitcast.32), calls=%async_computation | async-start | bytes 5242880 | tf_op jit(solution)/shard_map/all_to_all | solution.py:402
  32.0 3.4 %collective-permute-start.1 = (bf16[128,1024]{1,0:T(8,128)(2,1)S(1)}, bf16[128,1024]{1,0:T(8,128)(2,1)S(1)}, u32[]{:S(2)}, u32[]{:S(2)}) collective-permute-start(bf16[128,1024]{1,0:T(8,128)(2,1)S(1)} %bitcast.25), channel_id=1, source_target_pairs={{0,8},{1,9},{2,10},{3,11},{4,12},{5,13},{6,14},{7,15},{8,16},{9,17... | collective-permute-start | bytes 786440 | tf_op jit(solution)/shard_map/ppermute | solution.py:407
  35.3 3.7 %collective-permute-start.5 = (bf16[128,1024]{1,0:T(8,128)(2,1)S(1)}, bf16[128,1024]{1,0:T(8,128)(2,1)S(1)}, u32[]{:S(2)}, u32[]{:S(2)}) collective-permute-start(bf16[128,1024]{1,0:T(8,128)(2,1)S(1)} %bitcast.26), channel_id=1, source_target_pairs={{0,56},{1,57},{2,58},{3,59},{4,60},{5,61},{6,62},{7,63},{8,0},{9,1... | collective-permute-start | bytes 786440 | tf_op jit(solution)/shard_map/ppermute | solution.py:407
  39.0 57.2 %collective-permute-done.1.refs_1_ = bf16[128,1024]{1,0:T(8,128)(2,1)S(1)} collective-permute-done((bf16[128,1024]{1,0:T(8,128)(2,1)S(1)}, bf16[128,1024]{1,0:T(8,128)(2,1)S(1)}, u32[]{:S(2)}, u32[]{:S(2)}) %collective-permute-start.1) | collective-permute-done | bytes 262176 | tf_op jit(solution)/shard_map/ppermute | solution.py:407
  98.2 5.1 %collective-permute-start.6 = (bf16[128,1024]{1,0:T(8,128)(2,1)S(1)}, bf16[128,1024]{1,0:T(8,128)(2,1)}, u32[]{:S(2)}, u32[]{:S(2)}) collective-permute-start(bf16[128,1024]{1,0:T(8,128)(2,1)S(1)} %collective-permute-done.5.refs_5_), channel_id=1, source_target_pairs={{0,56},{1,57},{2,58},{3,59},{4,60},{5,61},{6,62},{7,63},{8,0},{9,1... | collective-permute-start | bytes 786440 | tf_op jit(solution)/shard_map/ppermute | solution.py:407
  108.4 5.1 %collective-permute-start.7 = (bf16[128,1024]{1,0:T(8,128)(2,1)}, bf16[128,1024]{1,0:T(8,128)(2,1)S(1)}, u32[]{:S(2)}, u32[]{:S(2)}) collective-permute-start(bf16[128,1024]{1,0:T(8,128)(2,1)} %collective-permute-done.6.refs_6_), channel_id=1, source_target_pairs={{0,56},{1,57},{2,58},{3,59},{4,60},{5,61},{6,62},{7,63},{8,0},{9,1... | collective-permute-start | bytes 786440 | tf_op jit(solution)/shard_map/ppermute | solution.py:407
  118.4 6.7 %collective-permute-done.4.refs_4_ = bf16[128,1024]{1,0:T(8,128)(2,1)} collective-permute-done((bf16[128,1024]{1,0:T(8,128)(2,1)}, bf16[128,1024]{1,0:T(8,128)(2,1)}, u32[]{:S(2)}, u32[]{:S(2)}) %collective-permute-start.4) | collective-permute-done | bytes 262176 | tf_op jit(solution)/shard_map/ppermute | solution.py:407
  128.0 4.7 %token_stage.1 = (bf16[128,1024]{1,0:T(8,128)(2,1)S(1)}, bf16[128,1024]{1,0:T(8,128)(2,1)S(1)}, f32[8,128]{1,0:T(8,128)S(1)}) custom-call(s32[1,1,4]{2,1,0:T(1,128)S(1)} %copy-done.9, s32[1,1,4]{2,1,0:T(1,128)S(1)} %copy-done.10, s32[1,2,32]{2,1,0:T(2,128)S(1)} %copy-done.7, s32[2,128]{1,0:T(2,128)S(1)} %bitcast.29, bf16[32,1024]{1,0:T(8,128)(2,1)S(1)} %bitcast.28, ...), custom_call_target="tpu_custom_call" | custom-call | flops 2147483648 | bytes 6291456 | tf_op jit(solution)/shard_map/token_stage/pallas_call | solution.py:198
  135.4 6.1 %collective-permute-start.10 = (bf16[1024,512]{1,0:T(8,128)(2,1)}, bf16[1024,512]{1,0:T(8,128)(2,1)S(1)}, u32[]{:S(2)}, u32[]{:S(2)}) collective-permute-start(bf16[1024,512]{1,0:T(8,128)(2,1)} %bitcast.14), channel_id=1, source_target_pairs={{0,0},{1,64},{2,2},{3,66},{4,4},{5,68},{6,6},{7,70},{8,8},{9,72},{... | collective-permute-start | bytes 3145736 | tf_op jit(solution)/shard_map/ppermute | solution.py:392
  141.5 1.9 collective-permute-start.11
  143.4 3.6 %collective-permute-start.12 = (bf16[512,1024]{1,0:T(8,128)(2,1)}, bf16[512,1024]{1,0:T(8,128)(2,1)}, u32[]{:S(2)}, u32[]{:S(2)}) collective-permute-start(bf16[512,1024]{1,0:T(8,128)(2,1)} %bitcast.16), channel_id=1, source_target_pairs={{0,0},{1,64},{2,2},{3,66},{4,4},{5,68},{6,6},{7,70},{8,8},{9,72},{... | collective-permute-start | bytes 3145736 | tf_op jit(solution)/shard_map/ppermute | solution.py:392
  147.1 11.4 %collective-permute-start = (s32[2,128]{1,0:T(2,128)S(1)}, s32[2,128]{1,0:T(2,128)S(1)}, u32[]{:S(2)}, u32[]{:S(2)}) collective-permute-start(s32[2,128]{1,0:T(2,128)S(1)} %bitcast.30), channel_id=1, source_target_pairs={{0,64},{1,65},{2,66},{3,67},{4,68},{5,69},{6,70},{7,71},{8,72},{9,... | collective-permute-start | bytes 3080 | tf_op jit(solution)/shard_map/ppermute | solution.py:392
  161.1 14.4 %all-to-all-start.2 = ((bf16[64,8,1024]{2,1,0:T(8,128)(2,1)}), bf16[64,8,1024]{2,1,0:T(8,128)(2,1)S(1)}, u32[]{:S(2)}, u32[]{:S(2)}) async-start(bf16[64,8,1024]{2,1,0:T(8,128)(2,1)} %bitcast.12), calls=%async_computation.2 | async-start | bytes 2097152 | tf_op jit(solution)/shard_map/all_to_all | solution.py:402
  177.5 2.4 collective-permute-start.14
  184.9 20.4 %all-to-all-done.2 = bf16[64,8,1024]{2,1,0:T(8,128)(2,1)S(1)} async-done(((bf16[64,8,1024]{2,1,0:T(8,128)(2,1)}), bf16[64,8,1024]{2,1,0:T(8,128)(2,1)S(1)}, u32[]{:S(2)}, u32[]{:S(2)}) %all-to-all-start.2) | async-done | bytes 1048608 | tf_op jit(solution)/shard_map/all_to_all | solution.py:402
  205.3 8.5 %expert_stage.1 = bf16[512,1024]{1,0:T(8,128)(2,1)} custom-call(bf16[512,1024]{1,0:T(8,128)(2,1)S(1)} %bitcast.23, bf16[1024,512]{1,0:T(8,128)(2,1)S(1)} %collective-permute-done.10.refs_0_, bf16[1024,512]{1,0:T(8,128)(2,1)} %collective-permute-done.11.refs_1_, bf16[512,1024]{1,0:T(8,128)(2,1)} %collective-permute-done.12.refs_2_, ...), custom_call_target="tpu_custom_call" | custom-call | flops 4294967296 | bytes 8388608 | tf_op jit(solution)/shard_map/expert_stage/pallas_call | solution.py:325
  213.8 10.4 %all-to-all-start.3 = ((bf16[64,8,1024]{2,1,0:T(8,128)(2,1)}), bf16[64,8,1024]{2,1,0:T(8,128)(2,1)S(1)}, u32[]{:S(2)}, u32[]{:S(2)}) async-start(bf16[64,8,1024]{2,1,0:T(8,128)(2,1)} %bitcast.17), calls=%async_computation.3 | async-start | bytes 2097152 | tf_op jit(solution)/shard_map/all_to_all | solution.py:402
  227.3 25.6 %all-to-all-done.3 = bf16[64,8,1024]{2,1,0:T(8,128)(2,1)S(1)} async-done(((bf16[64,8,1024]{2,1,0:T(8,128)(2,1)}), bf16[64,8,1024]{2,1,0:T(8,128)(2,1)S(1)}, u32[]{:S(2)}, u32[]{:S(2)}) %all-to-all-start.3) | async-done | bytes 1048608 | tf_op jit(solution)/shard_map/all_to_all | solution.py:402
  254.0 3.4 %collective-permute-start.17 = (bf16[128,1024]{1,0:T(8,128)(2,1)S(1)}, bf16[128,1024]{1,0:T(8,128)(2,1)S(1)}, u32[]{:S(2)}, u32[]{:S(2)}) collective-permute-start(bf16[128,1024]{1,0:T(8,128)(2,1)S(1)} %get-tuple-element.18), channel_id=1, source_target_pairs={{0,128},{1,129},{2,130},{3,131},{4,132},{5,133},{6,134},{7,135},{8... | collective-permute-start | bytes 786440 | tf_op jit(solution)/shard_map/ppermute | solution.py:392
  257.4 3.9 %collective-permute-done.16 = bf16[128,1024]{1,0:T(8,128)(2,1)S(1)} collective-permute-done((bf16[128,1024]{1,0:T(8,128)(2,1)S(1)}, bf16[128,1024]{1,0:T(8,128)(2,1)S(1)}, u32[]{:S(2)}, u32[]{:S(2)}) %collective-permute-start.16) | collective-permute-done | bytes 262176 | tf_op jit(solution)/shard_map/ppermute | solution.py:392
  261.3 2.5 collective-permute-done.17
  (58 shorter events, 33.1 us)
Async XLA Ops:
  1.5 18.2 %all-to-all-start.1 = ((bf16[8,16,1024]{2,1,0:T(8,128)(2,1)}), bf16[8,16,1024]{2,1,0:T(8,128)(2,1)S(1)}, u32[]{:S(2)}, u32[]{:S(2)}) async-start(bf16[8,16,1024]{2,1,0:T(8,128)(2,1)} %broadcast_in_dim.11), calls=%async_computation.1 | async-start | bytes 524288 | tf_op jit(solution)/shard_map/all_to_all | solution.py:415
  19.7 105.5 %copy-start.9 = (s32[1,1,4]{2,1,0:T(1,128)S(1)}, s32[1,1,4]{2,1,0:T(1,128)}, u32[]{:S(2)}) copy-start(s32[1,1,4]{2,1,0:T(1,128)} %pages_ref.1) | copy-start | bytes 52
  19.7 105.5 %copy-start.10 = (s32[1,1,4]{2,1,0:T(1,128)S(1)}, s32[1,1,4]{2,1,0:T(1,128)}, u32[]{:S(2)}) copy-start(s32[1,1,4]{2,1,0:T(1,128)} %tails_ref.1) | copy-start | bytes 52
  19.7 105.4 %all-to-all-start = ((bf16[64,8,2560]{2,1,0:T(8,128)(2,1)}), bf16[64,8,2560]{2,1,0:T(8,128)(2,1)S(1)}, u32[]{:S(2)}, u32[]{:S(2)}) async-start(bf16[64,8,2560]{2,1,0:T(8,128)(2,1)} %bitcast.32), calls=%async_computation | async-start | bytes 5242880 | tf_op jit(solution)/shard_map/all_to_all | solution.py:402
  32.0 64.3 %collective-permute-start.1 = (bf16[128,1024]{1,0:T(8,128)(2,1)S(1)}, bf16[128,1024]{1,0:T(8,128)(2,1)S(1)}, u32[]{:S(2)}, u32[]{:S(2)}) collective-permute-start(bf16[128,1024]{1,0:T(8,128)(2,1)S(1)} %bitcast.25), channel_id=1, source_target_pairs={{0,8},{1,9},{2,10},{3,11},{4,12},{5,13},{6,14},{7,15},{8,16},{9,17... | collective-permute-start | bytes 786440 | tf_op jit(solution)/shard_map/ppermute | solution.py:407
  35.3 62.8 %collective-permute-start.5 = (bf16[128,1024]{1,0:T(8,128)(2,1)S(1)}, bf16[128,1024]{1,0:T(8,128)(2,1)S(1)}, u32[]{:S(2)}, u32[]{:S(2)}) collective-permute-start(bf16[128,1024]{1,0:T(8,128)(2,1)S(1)} %bitcast.26), channel_id=1, source_target_pairs={{0,56},{1,57},{2,58},{3,59},{4,60},{5,61},{6,62},{7,63},{8,0},{9,1... | collective-permute-start | bytes 786440 | tf_op jit(solution)/shard_map/ppermute | solution.py:407
  96.3 9.5 %collective-permute-start.2 = (bf16[128,1024]{1,0:T(8,128)(2,1)S(1)}, bf16[128,1024]{1,0:T(8,128)(2,1)S(1)}, u32[]{:S(2)}, u32[]{:S(2)}) collective-permute-start(bf16[128,1024]{1,0:T(8,128)(2,1)S(1)} %collective-permute-done.1.refs_1_), channel_id=1, source_target_pairs={{0,8},{1,9},{2,10},{3,11},{4,12},{5,13},{6,14},{7,15},{8,16},{9,17... | collective-permute-start | bytes 786440 | tf_op jit(solution)/shard_map/ppermute | solution.py:407
  98.2 10.2 %collective-permute-start.6 = (bf16[128,1024]{1,0:T(8,128)(2,1)S(1)}, bf16[128,1024]{1,0:T(8,128)(2,1)}, u32[]{:S(2)}, u32[]{:S(2)}) collective-permute-start(bf16[128,1024]{1,0:T(8,128)(2,1)S(1)} %collective-permute-done.5.refs_5_), channel_id=1, source_target_pairs={{0,56},{1,57},{2,58},{3,59},{4,60},{5,61},{6,62},{7,63},{8,0},{9,1... | collective-permute-start | bytes 786440 | tf_op jit(solution)/shard_map/ppermute | solution.py:407
  105.7 9.6 %collective-permute-start.3 = (bf16[128,1024]{1,0:T(8,128)(2,1)S(1)}, bf16[128,1024]{1,0:T(8,128)(2,1)}, u32[]{:S(2)}, u32[]{:S(2)}) collective-permute-start(bf16[128,1024]{1,0:T(8,128)(2,1)S(1)} %collective-permute-done.2.refs_2_), channel_id=1, source_target_pairs={{0,8},{1,9},{2,10},{3,11},{4,12},{5,13},{6,14},{7,15},{8,16},{9,17... | collective-permute-start | bytes 786440 | tf_op jit(solution)/shard_map/ppermute | solution.py:407
  108.4 9.3 %collective-permute-start.7 = (bf16[128,1024]{1,0:T(8,128)(2,1)}, bf16[128,1024]{1,0:T(8,128)(2,1)S(1)}, u32[]{:S(2)}, u32[]{:S(2)}) collective-permute-start(bf16[128,1024]{1,0:T(8,128)(2,1)} %collective-permute-done.6.refs_6_), channel_id=1, source_target_pairs={{0,56},{1,57},{2,58},{3,59},{4,60},{5,61},{6,62},{7,63},{8,0},{9,1... | collective-permute-start | bytes 786440 | tf_op jit(solution)/shard_map/ppermute | solution.py:407
  115.3 9.8 %collective-permute-start.4 = (bf16[128,1024]{1,0:T(8,128)(2,1)}, bf16[128,1024]{1,0:T(8,128)(2,1)}, u32[]{:S(2)}, u32[]{:S(2)}) collective-permute-start(bf16[128,1024]{1,0:T(8,128)(2,1)} %collective-permute-done.3.refs_3_), channel_id=1, source_target_pairs={{0,8},{1,9},{2,10},{3,11},{4,12},{5,13},{6,14},{7,15},{8,16},{9,17... | collective-permute-start | bytes 786440 | tf_op jit(solution)/shard_map/ppermute | solution.py:407
  133.4 26.2 %collective-permute-start.9 = (bf16[128,1024]{1,0:T(8,128)(2,1)S(1)}, bf16[128,1024]{1,0:T(8,128)(2,1)S(1)}, u32[]{:S(2)}, u32[]{:S(2)}) collective-permute-start(bf16[128,1024]{1,0:T(8,128)(2,1)S(1)} %get-tuple-element.16.mine_ref), channel_id=1, source_target_pairs={{0,64},{1,65},{2,66},{3,67},{4,68},{5,69},{6,70},{7,71},{8,72},{9,... | collective-permute-start | bytes 786440 | tf_op jit(solution)/shard_map/ppermute | solution.py:392
  135.4 40.2 %collective-permute-start.10 = (bf16[1024,512]{1,0:T(8,128)(2,1)}, bf16[1024,512]{1,0:T(8,128)(2,1)S(1)}, u32[]{:S(2)}, u32[]{:S(2)}) collective-permute-start(bf16[1024,512]{1,0:T(8,128)(2,1)} %bitcast.14), channel_id=1, source_target_pairs={{0,0},{1,64},{2,2},{3,66},{4,4},{5,68},{6,6},{7,70},{8,8},{9,72},{... | collective-permute-start | bytes 3145736 | tf_op jit(solution)/shard_map/ppermute | solution.py:392
  141.5 36.0 %collective-permute-start.11 = (bf16[1024,512]{1,0:T(8,128)(2,1)}, bf16[1024,512]{1,0:T(8,128)(2,1)}, u32[]{:S(2)}, u32[]{:S(2)}) collective-permute-start(bf16[1024,512]{1,0:T(8,128)(2,1)} %bitcast.15), channel_id=1, source_target_pairs={{0,0},{1,64},{2,2},{3,66},{4,4},{5,68},{6,6},{7,70},{8,8},{9,72},{... | collective-permute-start | bytes 3145736 | tf_op jit(solution)/shard_map/ppermute | solution.py:392
  143.4 36.5 %collective-permute-start.12 = (bf16[512,1024]{1,0:T(8,128)(2,1)}, bf16[512,1024]{1,0:T(8,128)(2,1)}, u32[]{:S(2)}, u32[]{:S(2)}) collective-permute-start(bf16[512,1024]{1,0:T(8,128)(2,1)} %bitcast.16), channel_id=1, source_target_pairs={{0,0},{1,64},{2,2},{3,66},{4,4},{5,68},{6,6},{7,70},{8,8},{9,72},{... | collective-permute-start | bytes 3145736 | tf_op jit(solution)/shard_map/ppermute | solution.py:392
  147.1 12.2 %collective-permute-start = (s32[2,128]{1,0:T(2,128)S(1)}, s32[2,128]{1,0:T(2,128)S(1)}, u32[]{:S(2)}, u32[]{:S(2)}) collective-permute-start(s32[2,128]{1,0:T(2,128)S(1)} %bitcast.30), channel_id=1, source_target_pairs={{0,64},{1,65},{2,66},{3,67},{4,68},{5,69},{6,70},{7,71},{8,72},{9,... | collective-permute-start | bytes 3080 | tf_op jit(solution)/shard_map/ppermute | solution.py:392
  161.1 44.1 %all-to-all-start.2 = ((bf16[64,8,1024]{2,1,0:T(8,128)(2,1)}), bf16[64,8,1024]{2,1,0:T(8,128)(2,1)S(1)}, u32[]{:S(2)}, u32[]{:S(2)}) async-start(bf16[64,8,1024]{2,1,0:T(8,128)(2,1)} %bitcast.12), calls=%async_computation.2 | async-start | bytes 2097152 | tf_op jit(solution)/shard_map/all_to_all | solution.py:402
  175.6 6.3 %collective-permute-start.13 = (bf16[1024,512]{1,0:T(8,128)(2,1)S(1)}, bf16[1024,512]{1,0:T(8,128)(2,1)S(1)}, u32[]{:S(2)}, u32[]{:S(2)}) collective-permute-start(bf16[1024,512]{1,0:T(8,128)(2,1)S(1)} %collective-permute-done.10.refs_0_), channel_id=1, source_target_pairs={{0,64},{1,65},{2,66},{3,67},{4,68},{5,69},{6,70},{7,71},{8,72},{9,... | collective-permute-start | bytes 3145736 | tf_op jit(solution)/shard_map/ppermute | solution.py:392
  177.5 4.9 %collective-permute-start.14 = (bf16[1024,512]{1,0:T(8,128)(2,1)}, bf16[1024,512]{1,0:T(8,128)(2,1)S(1)}, u32[]{:S(2)}, u32[]{:S(2)}) collective-permute-start(bf16[1024,512]{1,0:T(8,128)(2,1)} %collective-permute-done.11.refs_1_), channel_id=1, source_target_pairs={{0,64},{1,65},{2,66},{3,67},{4,68},{5,69},{6,70},{7,71},{8,72},{9,... | collective-permute-start | bytes 3145736 | tf_op jit(solution)/shard_map/ppermute | solution.py:392
  180.0 4.9 %collective-permute-start.15 = (bf16[512,1024]{1,0:T(8,128)(2,1)}, bf16[512,1024]{1,0:T(8,128)(2,1)}, u32[]{:S(2)}, u32[]{:S(2)}) collective-permute-start(bf16[512,1024]{1,0:T(8,128)(2,1)} %collective-permute-done.12.refs_2_), channel_id=1, source_target_pairs={{0,64},{1,65},{2,66},{3,67},{4,68},{5,69},{6,70},{7,71},{8,72},{9,... | collective-permute-start | bytes 3145736 | tf_op jit(solution)/shard_map/ppermute | solution.py:392
  213.8 39.0 %all-to-all-start.3 = ((bf16[64,8,1024]{2,1,0:T(8,128)(2,1)}), bf16[64,8,1024]{2,1,0:T(8,128)(2,1)S(1)}, u32[]{:S(2)}, u32[]{:S(2)}) async-start(bf16[64,8,1024]{2,1,0:T(8,128)(2,1)} %bitcast.17), calls=%async_computation.3 | async-start | bytes 2097152 | tf_op jit(solution)/shard_map/all_to_all | solution.py:402
  224.2 3.1 %collective-permute-start.8 = (f32[8,128]{1,0:T(8,128)S(1)}, f32[8,128]{1,0:T(8,128)S(1)}, u32[]{:S(2)}, u32[]{:S(2)}) collective-permute-start(f32[8,128]{1,0:T(8,128)S(1)} %get-tuple-element.13.mine_ref), channel_id=1, source_target_pairs={{0,64},{1,65},{2,66},{3,67},{4,68},{5,69},{6,70},{7,71},{8,72},{9,... | collective-permute-start | bytes 12296 | tf_op jit(solution)/shard_map/ppermute | solution.py:392
  254.0 7.3 %collective-permute-start.16 = (bf16[128,1024]{1,0:T(8,128)(2,1)S(1)}, bf16[128,1024]{1,0:T(8,128)(2,1)S(1)}, u32[]{:S(2)}, u32[]{:S(2)}) collective-permute-start(bf16[128,1024]{1,0:T(8,128)(2,1)S(1)} %get-tuple-element.17), channel_id=1, source_target_pairs={{0,64},{1,65},{2,66},{3,67},{4,68},{5,69},{6,70},{7,71},{8,72},{9,... | collective-permute-start | bytes 786440 | tf_op jit(solution)/shard_map/ppermute | solution.py:392
  254.0 9.8 %collective-permute-start.17 = (bf16[128,1024]{1,0:T(8,128)(2,1)S(1)}, bf16[128,1024]{1,0:T(8,128)(2,1)S(1)}, u32[]{:S(2)}, u32[]{:S(2)}) collective-permute-start(bf16[128,1024]{1,0:T(8,128)(2,1)S(1)} %get-tuple-element.18), channel_id=1, source_target_pairs={{0,128},{1,129},{2,130},{3,131},{4,132},{5,133},{6,134},{7,135},{8... | collective-permute-start | bytes 786440 | tf_op jit(solution)/shard_map/ppermute | solution.py:392
  (13 other events, 393.9 us)

commit v4 on v3

--- a/solution.py
+++ b/solution.py
@@ -388,7 +388,8 @@
     for s in range(sections):
         for i in range(devices):
             to_s, to_i = where(s, i)
-            route.append((s * devices + i, to_s % sections * devices + to_i))
+            if (to_s, to_i) != (s, i):
+                route.append((s * devices + i, to_s % sections * devices + to_i))
     return lax.ppermute(shard, ("section", "expert"), route)
 
 
@@ -407,7 +408,7 @@
     return lax.ppermute(shard, "expert", [(i, (i + apart) % size) for i in range(size)])
 
 
-def gathered_proj(piece):
+def column_block(piece):
     side = len(RING)
     devices = lax.axis_size("expert")
     groups = [list(range(start, start + side)) for start in range(0, devices, side)]
@@ -415,7 +416,11 @@
     block = lax.all_to_all(
         copies, "expert", split_axis=0, concat_axis=0, tiled=True, axis_index_groups=groups
     )
-    block = block.reshape(-1, piece.shape[1])
+    return block.reshape(-1, piece.shape[1])
+
+
+def ringed(block):
+    side = len(RING)
     blocks = {0: block}
     for step in range(1, side // 2 + 1):
         blocks[step] = shifted(blocks[step - 1], side)
@@ -430,11 +435,16 @@
     experts = router.shape[2]
     weights = dict(gate=w_gate[0], up=w_up[0], down=w_down[0])
     mine = routes[0].T
-    proj = gathered_proj(out_proj[0])
+    block = column_block(out_proj[0])
+    weights = dict(zip(weights, lax.optimization_barrier((*weights.values(), block))))
     first, second = [], []
+    odd = (lax.axis_index("section") & 1) == 1
+    trader = odd != ((lax.axis_index("expert") & 1) == 1)
     for weight in weights.values():
-        first.append(moved(weight, lambda s, i: (s, i) if s % 2 == i % 2 else (s ^ 1, i ^ 1)))
+        got = moved(weight, lambda s, i: (s, i) if s % 2 == i % 2 else (s ^ 1, i ^ 1))
+        first.append(jnp.where(trader, got, weight))
         second.append(across_cores(first[-1]))
+    proj = ringed(block)
     outgoing = pack_pages(page_map, histories[0], devices)
     arrived = exchanged(outgoing, devices)
     theirs = across_cores(mine)
@@ -452,7 +462,8 @@
     result = exchanged(served, devices)
     own, other = combine(lanes, share, other_share, resid, result)
     own = moved(own, lambda s, i: (s + 1, i))
-    other = moved(other, lambda s, i: (s, i) if s % 2 else (s + 2, i))
+    got = moved(other, lambda s, i: (s, i) if s % 2 else (s + 2, i))
+    other = jnp.where(odd, other, got)
     return (own.astype(F32) + other.astype(F32)).astype(BF16)[None]
 
 

time: 267 us -> 243 us (0.910)
  starting transfers between devices: 106 us -> 89.9 us
  waiting for transfers between devices: 128 us -> 115 us
  other arithmetic: 0.77 us -> 4.94 us
    ppermute x11, starting transfers between devices: 36.6 us -> 23.7 us  [moved(): return lax.ppermute(shard, ('section', 'expert'), route)]
    ppermute x7, waiting for transfers between devices: 67.9 us -> 60.5 us  [shifted(): lax.ppermute(shard, 'expert', [(i, (i + apart) % size) for i in range(siz...]
    select_n x0 -> x3, other arithmetic: none -> 4.12 us  [shards(): first.append(jnp.where(trader, got, weight))]
    all_to_all x3, waiting for transfers between devices: 46 us -> 42.2 us  [exchanged(): lax.all_to_all(sent, 'expert', split_axis=0, concat_axis=0, tiled=True)]
    all_to_all x3, starting transfers between devices: 37.1 us -> 34 us  [exchanged(): lax.all_to_all(sent, 'expert', split_axis=0, concat_axis=0, tiled=True)]
    unnamed x30 -> x38, local copies, waits for them, and re-layouts: 6.64 us -> 7.6 us
  transfers between devices with their start and end apart: 22 -> 22, of which waited for: 14 -> 11; matrix products, arithmetic and copies ran while one was open for 0% -> 2% of each run, Pallas kernels for 3% -> 5%
where the time goes in v4:
time: 243 us; the launch traced here: 241 us
  waiting for transfers between devices  115 us (47%)
  starting transfers between devices  89.9 us (37%)
  Pallas kernels  21.5 us (9%)
  local copies, waits for them, and re-layouts  9.09 us (4%)
  other arithmetic  4.94 us (2%)
    ppermute x7, waiting for transfers between devices, shifted(): lax.ppermute(shard, 'expert', [(i, (i + apart) % size) for i in range(siz...  60.5 us
    all_to_all x3, waiting for transfers between devices, exchanged(): lax.all_to_all(sent, 'expert', split_axis=0, concat_axis=0, tiled=True)  42.2 us
    all_to_all x3, starting transfers between devices, exchanged(): lax.all_to_all(sent, 'expert', split_axis=0, concat_axis=0, tiled=True)  34 us
    ppermute x11, starting transfers between devices, moved(): return lax.ppermute(shard, ('section', 'expert'), route)  23.7 us
    ppermute x7, starting transfers between devices, shifted(): lax.ppermute(shard, 'expert', [(i, (i + apart) % size) for i in range(siz...  23.1 us
    all_to_all x1, starting transfers between devices, column_block(): lax.all_to_all(copies, 'expert', split_axis=0, concat_axis=0, tiled=True,...  9.11 us
    ppermute x11, waiting for transfers between devices, moved(): return lax.ppermute(shard, ('section', 'expert'), route)  8.93 us
    pallas_call x1, Pallas kernels, expert_stage(): pl.pallas_call(expert_body, name='expert_stage', in_specs=[whole(pl.ANY)]...  8.53 us
  transfers between devices with their start and end apart: 22, of which 11 were waited for; matrix products, arithmetic and copies ran while one was open for 2% of the time, Pallas kernels for 5%

profile of v4, /device:TPU:8, one launch (start us, length us, event | category | flops | bytes accessed | tf_op | source)
XLA Modules:
  0.0 241.3 jit_solution(7775774627214216846)
XLA Ops:
  1.5 9.1 %all-to-all-start.1 = ((bf16[8,16,1024]{2,1,0:T(8,128)(2,1)}), bf16[8,16,1024]{2,1,0:T(8,128)(2,1)S(1)}, u32[]{:S(2)}, u32[]{:S(2)}) async-start(bf16[8,16,1024]{2,1,0:T(8,128)(2,1)} %broadcast_in_dim.11), calls=%async_computation.1 | async-start | bytes 524288 | tf_op jit(solution)/shard_map/all_to_all | solution.py:416
  10.6 5.2 %pack_pages.1 = bf16[512,2560]{1,0:T(8,128)(2,1)} custom-call(s32[1,2,32]{2,1,0:T(2,128)} %map_ref.3, bf16[128,5120]{1,0:T(8,128)(2,1)} %bitcast.40), custom_call_target="tpu_custom_call" | custom-call | flops 1073741824 | bytes 4194304 | tf_op jit(solution)/shard_map/pack_pages/pallas_call | solution.py:62
  15.8 3.8 %all-to-all-done.1 = bf16[8,16,1024]{2,1,0:T(8,128)(2,1)S(1)} async-done(((bf16[8,16,1024]{2,1,0:T(8,128)(2,1)}), bf16[8,16,1024]{2,1,0:T(8,128)(2,1)S(1)}, u32[]{:S(2)}, u32[]{:S(2)}) %all-to-all-start.1) | async-done | bytes 262176 | tf_op jit(solution)/shard_map/all_to_all | solution.py:416
  19.7 12.3 %all-to-all-start = ((bf16[64,8,2560]{2,1,0:T(8,128)(2,1)}), bf16[64,8,2560]{2,1,0:T(8,128)(2,1)S(1)}, u32[]{:S(2)}, u32[]{:S(2)}) async-start(bf16[64,8,2560]{2,1,0:T(8,128)(2,1)} %bitcast.32), calls=%async_computation | async-start | bytes 5242880 | tf_op jit(solution)/shard_map/all_to_all | solution.py:403
  32.0 3.4 %collective-permute-start.1 = (bf16[128,1024]{1,0:T(8,128)(2,1)S(1)}, bf16[128,1024]{1,0:T(8,128)(2,1)S(1)}, u32[]{:S(2)}, u32[]{:S(2)}) collective-permute-start(bf16[128,1024]{1,0:T(8,128)(2,1)S(1)} %bitcast.25), channel_id=1, source_target_pairs={{0,8},{1,9},{2,10},{3,11},{4,12},{5,13},{6,14},{7,15},{8,16},{9,17... | collective-permute-start | bytes 786440 | tf_op jit(solution)/shard_map/ppermute | solution.py:408
  35.3 3.7 %collective-permute-start.5 = (bf16[128,1024]{1,0:T(8,128)(2,1)S(1)}, bf16[128,1024]{1,0:T(8,128)(2,1)S(1)}, u32[]{:S(2)}, u32[]{:S(2)}) collective-permute-start(bf16[128,1024]{1,0:T(8,128)(2,1)S(1)} %bitcast.26), channel_id=1, source_target_pairs={{0,56},{1,57},{2,58},{3,59},{4,60},{5,61},{6,62},{7,63},{8,0},{9,1... | collective-permute-start | bytes 786440 | tf_op jit(solution)/shard_map/ppermute | solution.py:408
  39.0 57.2 %collective-permute-done.1.refs_1_ = bf16[128,1024]{1,0:T(8,128)(2,1)S(1)} collective-permute-done((bf16[128,1024]{1,0:T(8,128)(2,1)S(1)}, bf16[128,1024]{1,0:T(8,128)(2,1)S(1)}, u32[]{:S(2)}, u32[]{:S(2)}) %collective-permute-start.1) | collective-permute-done | bytes 262176 | tf_op jit(solution)/shard_map/ppermute | solution.py:408
  98.2 5.1 %collective-permute-start.6 = (bf16[128,1024]{1,0:T(8,128)(2,1)S(1)}, bf16[128,1024]{1,0:T(8,128)(2,1)}, u32[]{:S(2)}, u32[]{:S(2)}) collective-permute-start(bf16[128,1024]{1,0:T(8,128)(2,1)S(1)} %collective-permute-done.5.refs_5_), channel_id=1, source_target_pairs={{0,56},{1,57},{2,58},{3,59},{4,60},{5,61},{6,62},{7,63},{8,0},{9,1... | collective-permute-start | bytes 786440 | tf_op jit(solution)/shard_map/ppermute | solution.py:408
  110.3 5.1 %collective-permute-start.7 = (bf16[128,1024]{1,0:T(8,128)(2,1)}, bf16[128,1024]{1,0:T(8,128)(2,1)S(1)}, u32[]{:S(2)}, u32[]{:S(2)}) collective-permute-start(bf16[128,1024]{1,0:T(8,128)(2,1)} %collective-permute-done.6.refs_6_), channel_id=1, source_target_pairs={{0,56},{1,57},{2,58},{3,59},{4,60},{5,61},{6,62},{7,63},{8,0},{9,1... | collective-permute-start | bytes 786440 | tf_op jit(solution)/shard_map/ppermute | solution.py:408
  117.4 3.4 %collective-permute-start.11 = (bf16[1024,512]{1,0:T(8,128)(2,1)}, bf16[1024,512]{1,0:T(8,128)(2,1)}, u32[]{:S(2)}, u32[]{:S(2)}) collective-permute-start(bf16[1024,512]{1,0:T(8,128)(2,1)} %bitcast.35), channel_id=1, source_target_pairs={{1,64},{3,66},{5,68},{7,70},{9,72},{11,74},{13,76},{15,78},{17,80}... | collective-permute-start | bytes 3145736 | tf_op jit(solution)/shard_map/ppermute | solution.py:393
  120.7 2.2 collective-permute-start.12
  128.1 4.7 %token_stage.1 = (bf16[128,1024]{1,0:T(8,128)(2,1)S(1)}, bf16[128,1024]{1,0:T(8,128)(2,1)S(1)}, f32[8,128]{1,0:T(8,128)S(1)}) custom-call(s32[1,1,4]{2,1,0:T(1,128)S(1)} %copy-done.9, s32[1,1,4]{2,1,0:T(1,128)S(1)} %copy-done.10, s32[1,2,32]{2,1,0:T(2,128)S(1)} %copy-done.7, s32[2,128]{1,0:T(2,128)S(1)} %bitcast.29, bf16[32,1024]{1,0:T(8,128)(2,1)S(1)} %bitcast.28, ...), custom_call_target="tpu_custom_call" | custom-call | flops 2147483648 | bytes 6291456 | tf_op jit(solution)/shard_map/token_stage/pallas_call | solution.py:198
  133.6 2.0 collective-permute-start.9
  135.6 2.4 collective-permute-start
  140.7 14.5 %all-to-all-start.2 = ((bf16[64,8,1024]{2,1,0:T(8,128)(2,1)}), bf16[64,8,1024]{2,1,0:T(8,128)(2,1)S(1)}, u32[]{:S(2)}, u32[]{:S(2)}) async-start(bf16[64,8,1024]{2,1,0:T(8,128)(2,1)} %bitcast.12), calls=%async_computation.2 | async-start | bytes 2097152 | tf_op jit(solution)/shard_map/all_to_all | solution.py:403
  159.9 2.4 collective-permute-start.14
  163.7 2.1 collective-permute-start.15
  168.4 16.5 %all-to-all-done.2 = bf16[64,8,1024]{2,1,0:T(8,128)(2,1)S(1)} async-done(((bf16[64,8,1024]{2,1,0:T(8,128)(2,1)}), bf16[64,8,1024]{2,1,0:T(8,128)(2,1)S(1)}, u32[]{:S(2)}, u32[]{:S(2)}) %all-to-all-start.2) | async-done | bytes 1048608 | tf_op jit(solution)/shard_map/all_to_all | solution.py:403
  184.9 8.5 %expert_stage.1 = bf16[512,1024]{1,0:T(8,128)(2,1)} custom-call(bf16[512,1024]{1,0:T(8,128)(2,1)S(1)} %bitcast.23, bf16[1024,512]{1,0:T(8,128)(2,1)S(1)} %broadcast_select_fusion.2.refs_0_, bf16[1024,512]{1,0:T(8,128)(2,1)} %copy-done.15, bf16[512,1024]{1,0:T(8,128)(2,1)} %copy-done.16, bf16[1024,512]{1,0:T(8,128)(2,1)} %copy-done.17, ...), custom_call_target="tpu_custom_call" | custom-call | flops 4294967296 | bytes 8388608 | tf_op jit(solution)/shard_map/expert_stage/pallas_call | solution.py:325
  193.4 7.3 %all-to-all-start.3 = ((bf16[64,8,1024]{2,1,0:T(8,128)(2,1)}), bf16[64,8,1024]{2,1,0:T(8,128)(2,1)S(1)}, u32[]{:S(2)}, u32[]{:S(2)}) async-start(bf16[64,8,1024]{2,1,0:T(8,128)(2,1)} %bitcast.17), calls=%async_computation.3 | async-start | bytes 2097152 | tf_op jit(solution)/shard_map/all_to_all | solution.py:403
  203.8 25.7 %all-to-all-done.3 = bf16[64,8,1024]{2,1,0:T(8,128)(2,1)S(1)} async-done(((bf16[64,8,1024]{2,1,0:T(8,128)(2,1)}), bf16[64,8,1024]{2,1,0:T(8,128)(2,1)S(1)}, u32[]{:S(2)}, u32[]{:S(2)}) %all-to-all-start.3) | async-done | bytes 1048608 | tf_op jit(solution)/shard_map/all_to_all | solution.py:403
  230.6 3.4 %collective-permute-start.17 = (bf16[128,1024]{1,0:T(8,128)(2,1)S(1)}, bf16[128,1024]{1,0:T(8,128)(2,1)S(1)}, u32[]{:S(2)}, u32[]{:S(2)}) collective-permute-start(bf16[128,1024]{1,0:T(8,128)(2,1)S(1)} %get-tuple-element.24), channel_id=1, source_target_pairs={{0,128},{1,129},{2,130},{3,131},{4,132},{5,133},{6,134},{7,135},{8... | collective-permute-start | bytes 786440 | tf_op jit(solution)/shard_map/ppermute | solution.py:393
  234.0 3.9 %collective-permute-done.16 = bf16[128,1024]{1,0:T(8,128)(2,1)S(1)} collective-permute-done((bf16[128,1024]{1,0:T(8,128)(2,1)S(1)}, bf16[128,1024]{1,0:T(8,128)(2,1)S(1)}, u32[]{:S(2)}, u32[]{:S(2)}) %collective-permute-start.16) | collective-permute-done | bytes 262176 | tf_op jit(solution)/shard_map/ppermute | solution.py:393
  238.0 2.5 %collective-permute-done.17 = bf16[128,1024]{1,0:T(8,128)(2,1)S(1)} collective-permute-done((bf16[128,1024]{1,0:T(8,128)(2,1)S(1)}, bf16[128,1024]{1,0:T(8,128)(2,1)S(1)}, u32[]{:S(2)}, u32[]{:S(2)}) %collective-permute-start.17) | collective-permute-done | bytes 262176 | tf_op jit(solution)/shard_map/ppermute | solution.py:393
  (69 shorter events, 34.3 us)
Async XLA Ops:
  1.5 18.2 %all-to-all-start.1 = ((bf16[8,16,1024]{2,1,0:T(8,128)(2,1)}), bf16[8,16,1024]{2,1,0:T(8,128)(2,1)S(1)}, u32[]{:S(2)}, u32[]{:S(2)}) async-start(bf16[8,16,1024]{2,1,0:T(8,128)(2,1)} %broadcast_in_dim.11), calls=%async_computation.1 | async-start | bytes 524288 | tf_op jit(solution)/shard_map/all_to_all | solution.py:416
  19.7 105.6 %copy-start.9 = (s32[1,1,4]{2,1,0:T(1,128)S(1)}, s32[1,1,4]{2,1,0:T(1,128)}, u32[]{:S(2)}) copy-start(s32[1,1,4]{2,1,0:T(1,128)} %pages_ref.1) | copy-start | bytes 52
  19.7 105.6 %copy-start.10 = (s32[1,1,4]{2,1,0:T(1,128)S(1)}, s32[1,1,4]{2,1,0:T(1,128)}, u32[]{:S(2)}) copy-start(s32[1,1,4]{2,1,0:T(1,128)} %tails_ref.1) | copy-start | bytes 52
  19.7 105.6 %all-to-all-start = ((bf16[64,8,2560]{2,1,0:T(8,128)(2,1)}), bf16[64,8,2560]{2,1,0:T(8,128)(2,1)S(1)}, u32[]{:S(2)}, u32[]{:S(2)}) async-start(bf16[64,8,2560]{2,1,0:T(8,128)(2,1)} %bitcast.32), calls=%async_computation | async-start | bytes 5242880 | tf_op jit(solution)/shard_map/all_to_all | solution.py:403
  32.0 64.3 %collective-permute-start.1 = (bf16[128,1024]{1,0:T(8,128)(2,1)S(1)}, bf16[128,1024]{1,0:T(8,128)(2,1)S(1)}, u32[]{:S(2)}, u32[]{:S(2)}) collective-permute-start(bf16[128,1024]{1,0:T(8,128)(2,1)S(1)} %bitcast.25), channel_id=1, source_target_pairs={{0,8},{1,9},{2,10},{3,11},{4,12},{5,13},{6,14},{7,15},{8,16},{9,17... | collective-permute-start | bytes 786440 | tf_op jit(solution)/shard_map/ppermute | solution.py:408
  35.3 62.8 %collective-permute-start.5 = (bf16[128,1024]{1,0:T(8,128)(2,1)S(1)}, bf16[128,1024]{1,0:T(8,128)(2,1)S(1)}, u32[]{:S(2)}, u32[]{:S(2)}) collective-permute-start(bf16[128,1024]{1,0:T(8,128)(2,1)S(1)} %bitcast.26), channel_id=1, source_target_pairs={{0,56},{1,57},{2,58},{3,59},{4,60},{5,61},{6,62},{7,63},{8,0},{9,1... | collective-permute-start | bytes 786440 | tf_op jit(solution)/shard_map/ppermute | solution.py:408
  96.3 9.5 %collective-permute-start.2 = (bf16[128,1024]{1,0:T(8,128)(2,1)S(1)}, bf16[128,1024]{1,0:T(8,128)(2,1)S(1)}, u32[]{:S(2)}, u32[]{:S(2)}) collective-permute-start(bf16[128,1024]{1,0:T(8,128)(2,1)S(1)} %collective-permute-done.1.refs_1_), channel_id=1, source_target_pairs={{0,8},{1,9},{2,10},{3,11},{4,12},{5,13},{6,14},{7,15},{8,16},{9,17... | collective-permute-start | bytes 786440 | tf_op jit(solution)/shard_map/ppermute | solution.py:408
  98.2 12.1 %collective-permute-start.6 = (bf16[128,1024]{1,0:T(8,128)(2,1)S(1)}, bf16[128,1024]{1,0:T(8,128)(2,1)}, u32[]{:S(2)}, u32[]{:S(2)}) collective-permute-start(bf16[128,1024]{1,0:T(8,128)(2,1)S(1)} %collective-permute-done.5.refs_5_), channel_id=1, source_target_pairs={{0,56},{1,57},{2,58},{3,59},{4,60},{5,61},{6,62},{7,63},{8,0},{9,1... | collective-permute-start | bytes 786440 | tf_op jit(solution)/shard_map/ppermute | solution.py:408
  105.7 9.7 %collective-permute-start.3 = (bf16[128,1024]{1,0:T(8,128)(2,1)S(1)}, bf16[128,1024]{1,0:T(8,128)(2,1)}, u32[]{:S(2)}, u32[]{:S(2)}) collective-permute-start(bf16[128,1024]{1,0:T(8,128)(2,1)S(1)} %collective-permute-done.2.refs_2_), channel_id=1, source_target_pairs={{0,8},{1,9},{2,10},{3,11},{4,12},{5,13},{6,14},{7,15},{8,16},{9,17... | collective-permute-start | bytes 786440 | tf_op jit(solution)/shard_map/ppermute | solution.py:408
  108.4 46.8 %collective-permute-start.10 = (bf16[1024,512]{1,0:T(8,128)(2,1)}, bf16[1024,512]{1,0:T(8,128)(2,1)}, u32[]{:S(2)}, u32[]{:S(2)}) collective-permute-start(bf16[1024,512]{1,0:T(8,128)(2,1)} %bitcast.33), channel_id=1, source_target_pairs={{1,64},{3,66},{5,68},{7,70},{9,72},{11,74},{13,76},{15,78},{17,80}... | collective-permute-start | bytes 3145736 | tf_op jit(solution)/shard_map/ppermute | solution.py:393
  110.3 12.7 %collective-permute-start.7 = (bf16[128,1024]{1,0:T(8,128)(2,1)}, bf16[128,1024]{1,0:T(8,128)(2,1)S(1)}, u32[]{:S(2)}, u32[]{:S(2)}) collective-permute-start(bf16[128,1024]{1,0:T(8,128)(2,1)} %collective-permute-done.6.refs_6_), channel_id=1, source_target_pairs={{0,56},{1,57},{2,58},{3,59},{4,60},{5,61},{6,62},{7,63},{8,0},{9,1... | collective-permute-start | bytes 786440 | tf_op jit(solution)/shard_map/ppermute | solution.py:408
  115.4 9.8 %collective-permute-start.4 = (bf16[128,1024]{1,0:T(8,128)(2,1)}, bf16[128,1024]{1,0:T(8,128)(2,1)}, u32[]{:S(2)}, u32[]{:S(2)}) collective-permute-start(bf16[128,1024]{1,0:T(8,128)(2,1)} %collective-permute-done.3.refs_3_), channel_id=1, source_target_pairs={{0,8},{1,9},{2,10},{3,11},{4,12},{5,13},{6,14},{7,15},{8,16},{9,17... | collective-permute-start | bytes 786440 | tf_op jit(solution)/shard_map/ppermute | solution.py:408
  117.4 41.2 %collective-permute-start.11 = (bf16[1024,512]{1,0:T(8,128)(2,1)}, bf16[1024,512]{1,0:T(8,128)(2,1)}, u32[]{:S(2)}, u32[]{:S(2)}) collective-permute-start(bf16[1024,512]{1,0:T(8,128)(2,1)} %bitcast.35), channel_id=1, source_target_pairs={{1,64},{3,66},{5,68},{7,70},{9,72},{11,74},{13,76},{15,78},{17,80}... | collective-permute-start | bytes 3145736 | tf_op jit(solution)/shard_map/ppermute | solution.py:393
  120.7 41.6 %collective-permute-start.12 = (bf16[512,1024]{1,0:T(8,128)(2,1)}, bf16[512,1024]{1,0:T(8,128)(2,1)}, u32[]{:S(2)}, u32[]{:S(2)}) collective-permute-start(bf16[512,1024]{1,0:T(8,128)(2,1)} %bitcast.37), channel_id=1, source_target_pairs={{1,64},{3,66},{5,68},{7,70},{9,72},{11,74},{13,76},{15,78},{17,80}... | collective-permute-start | bytes 3145736 | tf_op jit(solution)/shard_map/ppermute | solution.py:393
  133.6 5.6 %collective-permute-start.9 = (bf16[128,1024]{1,0:T(8,128)(2,1)S(1)}, bf16[128,1024]{1,0:T(8,128)(2,1)S(1)}, u32[]{:S(2)}, u32[]{:S(2)}) collective-permute-start(bf16[128,1024]{1,0:T(8,128)(2,1)S(1)} %get-tuple-element.19.mine_ref), channel_id=1, source_target_pairs={{0,64},{1,65},{2,66},{3,67},{4,68},{5,69},{6,70},{7,71},{8,72},{9,... | collective-permute-start | bytes 786440 | tf_op jit(solution)/shard_map/ppermute | solution.py:393
  135.6 3.2 %collective-permute-start = (s32[2,128]{1,0:T(2,128)S(1)}, s32[2,128]{1,0:T(2,128)S(1)}, u32[]{:S(2)}, u32[]{:S(2)}) collective-permute-start(s32[2,128]{1,0:T(2,128)S(1)} %bitcast.30), channel_id=1, source_target_pairs={{0,64},{1,65},{2,66},{3,67},{4,68},{5,69},{6,70},{7,71},{8,72},{9,... | collective-permute-start | bytes 3080 | tf_op jit(solution)/shard_map/ppermute | solution.py:393
  140.7 44.2 %all-to-all-start.2 = ((bf16[64,8,1024]{2,1,0:T(8,128)(2,1)}), bf16[64,8,1024]{2,1,0:T(8,128)(2,1)S(1)}, u32[]{:S(2)}, u32[]{:S(2)}) async-start(bf16[64,8,1024]{2,1,0:T(8,128)(2,1)} %bitcast.12), calls=%async_computation.2 | async-start | bytes 2097152 | tf_op jit(solution)/shard_map/all_to_all | solution.py:403
  156.6 9.2 %collective-permute-start.13 = (bf16[1024,512]{1,0:T(8,128)(2,1)S(1)}, bf16[1024,512]{1,0:T(8,128)(2,1)S(1)}, u32[]{:S(2)}, u32[]{:S(2)}) collective-permute-start(bf16[1024,512]{1,0:T(8,128)(2,1)S(1)} %broadcast_select_fusion.2.refs_0_), channel_id=1, source_target_pairs={{0,64},{1,65},{2,66},{3,67},{4,68},{5,69},{6,70},{7,71},{8,72},{9,... | collective-permute-start | bytes 3145736 | tf_op jit(solution)/shard_map/ppermute | solution.py:393
  159.9 5.9 %collective-permute-start.14 = (bf16[1024,512]{1,0:T(8,128)(2,1)S(1)}, bf16[1024,512]{1,0:T(8,128)(2,1)S(1)}, u32[]{:S(2)}, u32[]{:S(2)}) collective-permute-start(bf16[1024,512]{1,0:T(8,128)(2,1)S(1)} %broadcast_select_fusion.1.refs_1_), channel_id=1, source_target_pairs={{0,64},{1,65},{2,66},{3,67},{4,68},{5,69},{6,70},{7,71},{8,72},{9,... | collective-permute-start | bytes 3145736 | tf_op jit(solution)/shard_map/ppermute | solution.py:393
  163.7 4.7 %collective-permute-start.15 = (bf16[512,1024]{1,0:T(8,128)(2,1)S(1)}, bf16[512,1024]{1,0:T(8,128)(2,1)}, u32[]{:S(2)}, u32[]{:S(2)}) collective-permute-start(bf16[512,1024]{1,0:T(8,128)(2,1)S(1)} %broadcast_select_fusion.refs_2_), channel_id=1, source_target_pairs={{0,64},{1,65},{2,66},{3,67},{4,68},{5,69},{6,70},{7,71},{8,72},{9,... | collective-permute-start | bytes 3145736 | tf_op jit(solution)/shard_map/ppermute | solution.py:393
  193.4 36.0 %all-to-all-start.3 = ((bf16[64,8,1024]{2,1,0:T(8,128)(2,1)}), bf16[64,8,1024]{2,1,0:T(8,128)(2,1)S(1)}, u32[]{:S(2)}, u32[]{:S(2)}) async-start(bf16[64,8,1024]{2,1,0:T(8,128)(2,1)} %bitcast.17), calls=%async_computation.3 | async-start | bytes 2097152 | tf_op jit(solution)/shard_map/all_to_all | solution.py:403
  200.7 3.1 %collective-permute-start.8 = (f32[8,128]{1,0:T(8,128)S(1)}, f32[8,128]{1,0:T(8,128)S(1)}, u32[]{:S(2)}, u32[]{:S(2)}) collective-permute-start(f32[8,128]{1,0:T(8,128)S(1)} %get-tuple-element.16.mine_ref), channel_id=1, source_target_pairs={{0,64},{1,65},{2,66},{3,67},{4,68},{5,69},{6,70},{7,71},{8,72},{9,... | collective-permute-start | bytes 12296 | tf_op jit(solution)/shard_map/ppermute | solution.py:393
  230.6 7.3 %collective-permute-start.16 = (bf16[128,1024]{1,0:T(8,128)(2,1)S(1)}, bf16[128,1024]{1,0:T(8,128)(2,1)S(1)}, u32[]{:S(2)}, u32[]{:S(2)}) collective-permute-start(bf16[128,1024]{1,0:T(8,128)(2,1)S(1)} %get-tuple-element.23), channel_id=1, source_target_pairs={{0,64},{1,65},{2,66},{3,67},{4,68},{5,69},{6,70},{7,71},{8,72},{9,... | collective-permute-start | bytes 786440 | tf_op jit(solution)/shard_map/ppermute | solution.py:393
  230.6 9.8 %collective-permute-start.17 = (bf16[128,1024]{1,0:T(8,128)(2,1)S(1)}, bf16[128,1024]{1,0:T(8,128)(2,1)S(1)}, u32[]{:S(2)}, u32[]{:S(2)}) collective-permute-start(bf16[128,1024]{1,0:T(8,128)(2,1)S(1)} %get-tuple-element.24), channel_id=1, source_target_pairs={{0,128},{1,129},{2,130},{3,131},{4,132},{5,133},{6,134},{7,135},{8... | collective-permute-start | bytes 786440 | tf_op jit(solution)/shard_map/ppermute | solution.py:393
  (17 other events, 424.9 us)

commit v5 on v4

--- a/solution.py
+++ b/solution.py
@@ -36,42 +36,75 @@
     return pl.BlockSpec(memory_space=space)
 
 
-def pack_pages_body(map_ref, rows_ref, out_ref, pick_ref):
-    @pl.when(pl.program_id(0) == 0)
-    def _():
-        device = lax.shift_right_logical(map_ref[0, 0:1, :], 5).astype(F32)
-        pages = device.shape[1]
-        rows = pages * 4
-        spread = flag(iota((pages, rows), 0) == lax.shift_right_logical(iota((pages, rows), 1), 2))
-        target = dot(jnp.broadcast_to(device, (8, pages)).astype(BF16), spread)[0:1]
-        slot = iota((pick_ref.shape[0], rows), 0)
-        row = iota((pick_ref.shape[0], rows), 1)
-        hit = (lax.shift_right_logical(slot, 3) == target.astype(jnp.int32)) & ((slot & 3) == (row & 3))
-        pick_ref[:, :rows] = flag(hit & ((slot & 4) == 0))
-        pick_ref[:, rows:] = flag(hit & ((slot & 4) == 4))
-
-    half = rows_ref.shape[1] // 2
-    both = jnp.concatenate([rows_ref[:, :half], rows_ref[:, half:]], axis=0)
-    out_ref[...] = dot(pick_ref[...], both).astype(BF16)
-
-
-def pack_pages(page_map, rows, devices):
+def pack_pages_body(map_ref, proj_ref, rows_hbm, out_hbm, rows_ref, out_ref, pick_ref, sems):
+    count, width = rows_ref.shape
+    block = width // 5
+    half = block // 2
+    slots = out_ref.shape[0]
+    side = len(RING)
+    incoming = []
+    for index in range(5):
+        part = pl.ds(index * block, block)
+        incoming.append(
+            pltpu.make_async_copy(rows_hbm.at[:, part], rows_ref.at[:, part], sems.at[index])
+        )
+        incoming[-1].start()
+    lanes = proj_ref.shape[1] // side
+    for place in range(side):
+        columns = slice(place * lanes, (place + 1) * lanes)
+        for part in range(2):
+            piece = proj_ref[8 * part : 8 * part + 8, columns].astype(F32)
+            tall = jnp.concatenate([piece] * side, axis=0).astype(BF16)
+            start = 5 * half + part * lanes
+            out_ref[place * 8 * side : (place + 1) * 8 * side, start : start + lanes] = tall
+    outgoing = []
+
+    def send(start, size):
+        part = pl.ds(start, size)
+        sem = sems.at[5 + len(outgoing)]
+        outgoing.append(pltpu.make_async_copy(out_ref.at[:, part], out_hbm.at[:, part], sem))
+        outgoing[-1].start()
+
+    send(5 * half, 2 * lanes)
+    device = lax.shift_right_logical(map_ref[0, 0:1, :], 5).astype(F32)
+    pages = device.shape[1]
+    spread = flag(iota((pages, count), 0) == lax.shift_right_logical(iota((pages, count), 1), 2))
+    target = dot(jnp.broadcast_to(device, (8, pages)).astype(BF16), spread)[0:1]
+    slot = iota((slots, count), 0)
+    row = iota((slots, count), 1)
+    hit = (lax.shift_right_logical(slot, 3) == target.astype(jnp.int32)) & ((slot & 3) == (row & 3))
+    pick_ref[:, :count] = flag(hit & ((slot & 4) == 0))
+    pick_ref[:, count:] = flag(hit & ((slot & 4) == 4))
+    for index in range(5):
+        incoming[index].wait()
+        start = index * block
+        both = jnp.concatenate(
+            [rows_ref[:, start : start + half], rows_ref[:, start + half : start + block]], axis=0
+        )
+        out_ref[:, index * half : (index + 1) * half] = dot(pick_ref[...], both).astype(BF16)
+        send(index * half, half)
+    for copy in outgoing:
+        copy.wait()
+
+
+def pack_pages(page_map, proj, rows, devices):
     count, width = rows.shape
-    block = width // 5
     slots = devices * 8
+    wide = width // 2 + 2 * (proj.shape[1] // len(RING))
     return pl.pallas_call(
         pack_pages_body,
         name="pack_pages",
-        grid=(5,),
-        in_specs=[
-            whole(),
-            pl.BlockSpec((count, block), lambda b: (0, b)),
+        in_specs=[whole(), whole(), whole(pl.ANY)],
+        out_specs=whole(pl.ANY),
+        out_shape=jax.ShapeDtypeStruct((slots, wide), BF16),
+        scratch_shapes=[
+            pltpu.VMEM((count, width), BF16),
+            pltpu.VMEM((slots, wide), BF16),
+            pltpu.VMEM((slots, 2 * count), BF16),
+            pltpu.SemaphoreType.DMA((11,)),
         ],
-        out_specs=pl.BlockSpec((slots, block // 2), lambda b: (0, b)),
-        out_shape=jax.ShapeDtypeStruct((slots, width // 2), BF16),
-        scratch_shapes=[pltpu.VMEM((slots, 2 * count), BF16)],
         cost_estimate=pl.CostEstimate(flops=1 << 30, bytes_accessed=4 << 20, transcendentals=0),
-    )(page_map, rows)
+    )(page_map, proj, rows)
 
 
 def user_layout(index, pages_ref, tails_ref):
@@ -103,7 +136,7 @@
     normed_ref, resid_ref, share_ref, arrived_ref, proj_ref, mixed_ref, sems = refs[len(RING) :]
     count, model_width = resid_ref.shape
     slots = arrived_ref.shape[0]
-    half = arrived_ref.shape[1] // 5
+    half = model_width // 2
     pages = map_ref.shape[2]
     head_dim = model_width // HEADS
     copies = []
@@ -113,10 +146,13 @@
             pltpu.make_async_copy(arrived_hbm.at[:, part], arrived_ref.at[:, part], sems.at[index])
         )
     for index, shift in enumerate(RING):
-        rows = proj_hbm[index].shape[0]
-        start = pl.multiple_of(((place_ref[0] - shift) & (len(RING) - 1)) * rows, rows)
-        target = proj_ref.at[pl.ds(start, rows)]
-        copies.append(pltpu.make_async_copy(proj_hbm[index], target, sems.at[5 + index]))
+        lanes = proj_hbm[index].shape[1] // 2
+        start = pl.multiple_of(((place_ref[0] - shift) & (len(RING) - 1)) * lanes, lanes)
+        for part in range(2):
+            origin = proj_hbm[index].at[:, pl.ds(part * lanes, lanes)]
+            target = proj_ref.at[pl.ds(part * slots, slots), pl.ds(start, lanes)]
+            sem = sems.at[5 + 2 * index + part]
+            copies.append(pltpu.make_async_copy(origin, target, sem))
     for copy in copies:
         copy.start()
 
@@ -154,13 +190,23 @@
     squares = functools.reduce(jnp.add, [part * part for part in attended])
     variance = jnp.sum(squares, axis=1, keepdims=True) * (1.0 / model_width)
     scale = lax.rsqrt(variance + 1e-05)
+    wide = 2 * head_dim
+    come, go = iota((wide, wide), 0), iota((wide, wide), 1)
+    order = (come >> 4) * 8 + (come & 7) + ((come >> 3) & 1) * head_dim
+    order = flag(order == go)
     for side in range(2):
         gating = block(3, side)
-        for head in range(HEADS // 2):
-            part = slice(head * head_dim, (head + 1) * head_dim)
-            index = side * (HEADS // 2) + head
-            mixed = attended[index] * scale * gating[:, part]
-            mixed_ref[:, index * head_dim : (index + 1) * head_dim] = mixed.astype(BF16)
+        for pair in range(HEADS // 4):
+            heads = []
+            for head in (2 * pair, 2 * pair + 1):
+                part = slice(head * head_dim, (head + 1) * head_dim)
+                mixed = attended[side * (HEADS // 2) + head] * scale * gating[:, part]
+                heads.append(mixed.astype(BF16))
+            sorted_pair = dot(jnp.concatenate(heads, axis=1), order).astype(BF16)
+            start = (side * (HEADS // 4) + pair) * head_dim
+            mixed_ref[:, start : start + head_dim] = sorted_pair[:, :head_dim]
+            start += half
+            mixed_ref[:, start : start + head_dim] = sorted_pair[:, head_dim:]
 
     squares = jnp.zeros((count, 1), F32)
     chunk = half // 2
@@ -194,7 +240,8 @@
 
 
 def token_stage(user_pages, tails, page_map, routes, router, place, arrived, proj, count):
-    depth, width = proj[0].shape
+    slots, wide = proj[0].shape
+    width = wide // 2 * len(RING)
     return pl.pallas_call(
         token_body,
         name="token_stage",
@@ -206,10 +253,10 @@
             jax.ShapeDtypeStruct((8, count), F32),
         ],
         scratch_shapes=[
-            pltpu.VMEM(arrived.shape, BF16),
-            pltpu.VMEM((depth * len(RING), width), BF16),
+            pltpu.VMEM((slots, 5 * width // 2), BF16),
+            pltpu.VMEM((2 * slots, width), BF16),
             pltpu.VMEM((count, width), BF16),
-            pltpu.SemaphoreType.DMA((5 + len(RING),)),
+            pltpu.SemaphoreType.DMA((5 + 2 * len(RING),)),
         ],
         compiler_params=pltpu.CompilerParams(vmem_limit_bytes=40 << 20),
         cost_estimate=pl.CostEstimate(flops=2 << 30, bytes_accessed=6 << 20, transcendentals=0),
@@ -282,7 +329,7 @@
 
 def expert_body(rows_hbm, *refs):
     weights_hbm = (refs[0:3], refs[3:6])
-    out_ref, rows_ref, gate_ref, up_ref, down_ref, hidden_ref, sems = refs[6:]
+    out_hbm, out_ref, rows_ref, gate_ref, up_ref, down_ref, hidden_ref, sems = refs[6:]
     units = hidden_ref.shape[1]
     chunk = units // 2
     width = out_ref.shape[1]
@@ -298,10 +345,13 @@
                 copies.append(pltpu.make_async_copy(hbm.at[:, part], ref.at[half, :, part], sem))
         sem = sems.at[1 + len(copies)]
         copies.append(pltpu.make_async_copy(down_hbm, down_ref.at[half], sem))
-    for copy in copies:
+    copies[0].start()
+    copies[1].start()
+    rows_copy.wait()
+    for copy in copies[2:]:
         copy.start()
-    rows_copy.wait()
     pending = iter(copies)
+    sent = []
     for half in range(2):
         for piece in range(2):
             part = slice(piece * chunk, (piece + 1) * chunk)
@@ -317,6 +367,13 @@
             if half == 1:
                 result = (out_ref[:, part].astype(F32) + result.astype(F32)).astype(BF16)
             out_ref[:, part] = result
+            if half == 1:
+                part = pl.ds(quarter * width // 4, width // 4)
+                sem = sems.at[11 + quarter]
+                sent.append(pltpu.make_async_copy(out_ref.at[:, part], out_hbm.at[:, part], sem))
+                sent[-1].start()
+    for copy in sent:
+        copy.wait()
 
 
 def expert_stage(rows, first, second):
@@ -326,15 +383,16 @@
         expert_body,
         name="expert_stage",
         in_specs=[whole(pl.ANY)] * 7,
-        out_specs=whole(),
+        out_specs=whole(pl.ANY),
         out_shape=jax.ShapeDtypeStruct((count, width), BF16),
         scratch_shapes=[
+            pltpu.VMEM((count, width), BF16),
             pltpu.VMEM((count, width), BF16),
             pltpu.VMEM((2, width, units), BF16),
             pltpu.VMEM((2, width, units), BF16),
             pltpu.VMEM((2, units, width), BF16),
             pltpu.VMEM((count, units), BF16),
-            pltpu.SemaphoreType.DMA((11,)),
+            pltpu.SemaphoreType.DMA((15,)),
         ],
         compiler_params=pltpu.CompilerParams(vmem_limit_bytes=50 << 20),
         cost_estimate=pl.CostEstimate(flops=4 << 30, bytes_accessed=8 << 20, transcendentals=0),
@@ -408,17 +466,6 @@
     return lax.ppermute(shard, "expert", [(i, (i + apart) % size) for i in range(size)])
 
 
-def column_block(piece):
-    side = len(RING)
-    devices = lax.axis_size("expert")
-    groups = [list(range(start, start + side)) for start in range(0, devices, side)]
-    copies = jnp.broadcast_to(piece[None], (side,) + piece.shape)
-    block = lax.all_to_all(
-        copies, "expert", split_axis=0, concat_axis=0, tiled=True, axis_index_groups=groups
-    )
-    return block.reshape(-1, piece.shape[1])
-
-
 def ringed(block):
     side = len(RING)
     blocks = {0: block}
@@ -435,7 +482,9 @@
     experts = router.shape[2]
     weights = dict(gate=w_gate[0], up=w_up[0], down=w_down[0])
     mine = routes[0].T
-    block = column_block(out_proj[0])
+    outgoing = pack_pages(page_map, out_proj[0], histories[0], devices)
+    arrived = exchanged(outgoing, devices)
+    block = arrived[:, histories.shape[2] // 2 :]
     weights = dict(zip(weights, lax.optimization_barrier((*weights.values(), block))))
     first, second = [], []
     odd = (lax.axis_index("section") & 1) == 1
@@ -445,8 +494,6 @@
         first.append(jnp.where(trader, got, weight))
         second.append(across_cores(first[-1]))
     proj = ringed(block)
-    outgoing = pack_pages(page_map, histories[0], devices)
-    arrived = exchanged(outgoing, devices)
     theirs = across_cores(mine)
     core = (lax.axis_index("section") & 1).astype(jnp.int32).reshape(1)
     place = lax.shift_right_logical(lax.axis_index("expert"), 3).astype(jnp.int32).reshape(1)

time: 243 us -> 244 us (level)
  blocking collectives: 0 us -> 86.3 us
  waiting for transfers between devices: 115 us -> 56.1 us
  starting transfers between devices: 89.9 us -> 64.6 us
    all_to_all x0 -> x1, blocking collectives: none -> 86.3 us  [exchanged(): lax.all_to_all(sent, 'expert', split_axis=0, concat_axis=0, tiled=True)]
    ppermute x7, waiting for transfers between devices: 60.5 us -> 4.77 us  [shifted(): lax.ppermute(shard, 'expert', [(i, (i + apart) % size) for i in range(siz...]
    all_to_all x3 -> x2, starting transfers between devices: 34 us -> 18.2 us  [exchanged(): lax.all_to_all(sent, 'expert', split_axis=0, concat_axis=0, tiled=True)]
    all_to_all x1 -> x0, starting transfers between devices: 9.11 us -> none  [column_block(): lax.all_to_all(copies, 'expert', split_axis=0, concat_axis=0, tiled=True,...]
    all_to_all x1 -> x0, waiting for transfers between devices: 3.81 us -> none  [column_block(): lax.all_to_all(copies, 'expert', split_axis=0, concat_axis=0, tiled=True,...]
    unnamed x38 -> x40, local copies, waits for them, and re-layouts: 7.6 us -> 9.3 us
    all_to_all x3 -> x2, waiting for transfers between devices: 42.2 us -> 42.2 us  [exchanged(): lax.all_to_all(sent, 'expert', split_axis=0, concat_axis=0, tiled=True)]
  transfers between devices with their start and end apart: 22 -> 20, of which waited for: 11 -> 10; matrix products, arithmetic and copies ran while one was open for 2% -> 2% of each run, Pallas kernels for 5% -> 3%
where the time goes in v5:
time: 244 us; the launch traced here: 243 us
  blocking collectives  86.3 us (35%)
  starting transfers between devices  64.6 us (26%)
  waiting for transfers between devices  56.1 us (23%)
  Pallas kernels  21 us (9%)
  local copies, waits for them, and re-layouts  9.32 us (4%)
  other arithmetic  4.95 us (2%)
    all_to_all x1, blocking collectives, exchanged(): lax.all_to_all(sent, 'expert', split_axis=0, concat_axis=0, tiled=True)  86.3 us
    all_to_all x2, waiting for transfers between devices, exchanged(): lax.all_to_all(sent, 'expert', split_axis=0, concat_axis=0, tiled=True)  42.2 us
    ppermute x11, starting transfers between devices, moved(): return lax.ppermute(shard, ('section', 'expert'), route)  23.3 us
    ppermute x7, starting transfers between devices, shifted(): lax.ppermute(shard, 'expert', [(i, (i + apart) % size) for i in range(siz...  23 us
    all_to_all x2, starting transfers between devices, exchanged(): lax.all_to_all(sent, 'expert', split_axis=0, concat_axis=0, tiled=True)  18.2 us
    unnamed x40, local copies, waits for them, and re-layouts  9.3 us
    ppermute x11, waiting for transfers between devices, moved(): return lax.ppermute(shard, ('section', 'expert'), route)  9.19 us
    pallas_call x1, Pallas kernels, expert_stage(): pl.pallas_call(expert_body, name='expert_stage', in_specs=[whole(pl.ANY)]...  8.4 us
  transfers between devices with their start and end apart: 20, of which 10 were waited for; matrix products, arithmetic and copies ran while one was open for 2% of the time, Pallas kernels for 3%

profile of v5, /device:TPU:8, one launch (start us, length us, event | category | flops | bytes accessed | tf_op | source)
XLA Modules:
  0.0 242.7 jit_solution(15862608912314458765)
XLA Ops:
  0.0 4.3 %pack_pages.1 = bf16[512,2816]{1,0:T(8,128)(2,1)} custom-call(s32[1,2,32]{2,1,0:T(2,128)} %map_ref.3, bf16[16,1024]{1,0:T(8,128)(2,1)} %bitcast.33, bf16[128,5120]{1,0:T(8,128)(2,1)} %bitcast.30), custom_call_target="tpu_custom_call" | custom-call | flops 1073741824 | bytes 4194304 | tf_op jit(solution)/shard_map/pack_pages/pallas_call | solution.py:94
  4.4 86.3 %all_to_all.15 = bf16[64,8,2816]{2,1,0:T(8,128)(2,1)S(1)} all-to-all(bf16[64,8,2816]{2,1,0:T(8,128)(2,1)} %bitcast.29), channel_id=1, replica_groups=mesh['section'=8,'expert'=64] {'expert'}, dimensions={0} | all-to-all | bytes 5767168 | tf_op jit(solution)/shard_map/all_to_all | solution.py:461
  90.7 2.6 %collective-permute-start.1 = (bf16[512,256]{1,0:T(8,128)(2,1)S(1)}, bf16[512,256]{1,0:T(8,128)(2,1)S(1)}, u32[]{:S(2)}, u32[]{:S(2)}) collective-permute-start(bf16[512,256]{1,0:T(8,128)(2,1)S(1)} %slice.4.refs_0_), channel_id=1, source_target_pairs={{0,8},{1,9},{2,10},{3,11},{4,12},{5,13},{6,14},{7,15},{8,16},{9,17... | collective-permute-start | bytes 786440 | tf_op jit(solution)/shard_map/ppermute | solution.py:466
  93.3 4.4 %collective-permute-start.5 = (bf16[512,256]{1,0:T(8,128)(2,1)S(1)}, bf16[512,256]{1,0:T(8,128)(2,1)S(1)}, u32[]{:S(2)}, u32[]{:S(2)}) collective-permute-start(bf16[512,256]{1,0:T(8,128)(2,1)S(1)} %slice.4.refs_0_), channel_id=1, source_target_pairs={{0,56},{1,57},{2,58},{3,59},{4,60},{5,61},{6,62},{7,63},{8,0},{9,1... | collective-permute-start | bytes 786440 | tf_op jit(solution)/shard_map/ppermute | solution.py:466
  97.7 2.4 collective-permute-done.1.refs_1_
  100.2 2.1 collective-permute-start.2
  103.0 4.9 %collective-permute-start.6 = (bf16[512,256]{1,0:T(8,128)(2,1)S(1)}, bf16[512,256]{1,0:T(8,128)(2,1)}, u32[]{:S(2)}, u32[]{:S(2)}) collective-permute-start(bf16[512,256]{1,0:T(8,128)(2,1)S(1)} %collective-permute-done.5.refs_5_), channel_id=1, source_target_pairs={{0,56},{1,57},{2,58},{3,59},{4,60},{5,61},{6,62},{7,63},{8,0},{9,1... | collective-permute-start | bytes 786440 | tf_op jit(solution)/shard_map/ppermute | solution.py:466
  114.2 5.1 %collective-permute-start.7 = (bf16[512,256]{1,0:T(8,128)(2,1)}, bf16[512,256]{1,0:T(8,128)(2,1)}, u32[]{:S(2)}, u32[]{:S(2)}) collective-permute-start(bf16[512,256]{1,0:T(8,128)(2,1)} %collective-permute-done.6.refs_6_), channel_id=1, source_target_pairs={{0,56},{1,57},{2,58},{3,59},{4,60},{5,61},{6,62},{7,63},{8,0},{9,1... | collective-permute-start | bytes 786440 | tf_op jit(solution)/shard_map/ppermute | solution.py:466
  119.3 1.9 collective-permute-start.4
  122.0 3.4 %collective-permute-start.11 = (bf16[1024,512]{1,0:T(8,128)(2,1)}, bf16[1024,512]{1,0:T(8,128)(2,1)}, u32[]{:S(2)}, u32[]{:S(2)}) collective-permute-start(bf16[1024,512]{1,0:T(8,128)(2,1)} %bitcast.14), channel_id=1, source_target_pairs={{1,64},{3,66},{5,68},{7,70},{9,72},{11,74},{13,76},{15,78},{17,80}... | collective-permute-start | bytes 3145736 | tf_op jit(solution)/shard_map/ppermute | solution.py:451
  125.3 2.2 collective-permute-start.12
  132.7 5.4 %token_stage.1 = (bf16[128,1024]{1,0:T(8,128)(2,1)S(1)}, bf16[128,1024]{1,0:T(8,128)(2,1)S(1)}, f32[8,128]{1,0:T(8,128)S(1)}) custom-call(s32[1,1,4]{2,1,0:T(1,128)S(1)} %copy-done.11, s32[1,1,4]{2,1,0:T(1,128)S(1)} %copy-done.12, s32[1,2,32]{2,1,0:T(2,128)S(1)} %copy-done, s32[2,128]{1,0:T(2,128)S(1)} %bitcast.26, bf16[32,1024]{1,0:T(8,128)(2,1)S(1)} %bitcast.25, ...), custom_call_target="tpu_custom_call" | custom-call | flops 2147483648 | bytes 6291456 | tf_op jit(solution)/shard_map/token_stage/pallas_call | solution.py:245
  140.8 2.4 collective-permute-start
  145.8 10.9 %all-to-all-start.1 = ((bf16[64,8,1024]{2,1,0:T(8,128)(2,1)}), bf16[64,8,1024]{2,1,0:T(8,128)(2,1)S(1)}, u32[]{:S(2)}, u32[]{:S(2)}) async-start(bf16[64,8,1024]{2,1,0:T(8,128)(2,1)} %bitcast.11), calls=%async_computation.1 | async-start | bytes 2097152 | tf_op jit(solution)/shard_map/all_to_all | solution.py:461
  161.5 2.4 collective-permute-start.14
  165.3 2.1 collective-permute-start.15
  170.0 16.5 %all-to-all-done.1 = bf16[64,8,1024]{2,1,0:T(8,128)(2,1)S(1)} async-done(((bf16[64,8,1024]{2,1,0:T(8,128)(2,1)}), bf16[64,8,1024]{2,1,0:T(8,128)(2,1)S(1)}, u32[]{:S(2)}, u32[]{:S(2)}) %all-to-all-start.1) | async-done | bytes 1048608 | tf_op jit(solution)/shard_map/all_to_all | solution.py:461
  186.5 8.4 %expert_stage.1 = bf16[512,1024]{1,0:T(8,128)(2,1)} custom-call(bf16[512,1024]{1,0:T(8,128)(2,1)S(1)} %bitcast.23, bf16[1024,512]{1,0:T(8,128)(2,1)S(1)} %broadcast_select_fusion.2.refs_0_, bf16[1024,512]{1,0:T(8,128)(2,1)} %copy-done.16, bf16[512,1024]{1,0:T(8,128)(2,1)} %copy-done.17, bf16[1024,512]{1,0:T(8,128)(2,1)} %copy-done.18, ...), custom_call_target="tpu_custom_call" | custom-call | flops 4294967296 | bytes 8388608 | tf_op jit(solution)/shard_map/expert_stage/pallas_call | solution.py:382
  194.9 7.3 %all-to-all-start.2 = ((bf16[64,8,1024]{2,1,0:T(8,128)(2,1)}), bf16[64,8,1024]{2,1,0:T(8,128)(2,1)S(1)}, u32[]{:S(2)}, u32[]{:S(2)}) async-start(bf16[64,8,1024]{2,1,0:T(8,128)(2,1)} %bitcast.16), calls=%async_computation.2 | async-start | bytes 2097152 | tf_op jit(solution)/shard_map/all_to_all | solution.py:461
  202.2 1.9 collective-permute-start.8
  205.3 25.7 %all-to-all-done.2 = bf16[64,8,1024]{2,1,0:T(8,128)(2,1)S(1)} async-done(((bf16[64,8,1024]{2,1,0:T(8,128)(2,1)}), bf16[64,8,1024]{2,1,0:T(8,128)(2,1)S(1)}, u32[]{:S(2)}, u32[]{:S(2)}) %all-to-all-start.2) | async-done | bytes 1048608 | tf_op jit(solution)/shard_map/all_to_all | solution.py:461
  232.1 3.1 %collective-permute-start.17 = (bf16[128,1024]{1,0:T(8,128)(2,1)S(1)}, bf16[128,1024]{1,0:T(8,128)(2,1)S(1)}, u32[]{:S(2)}, u32[]{:S(2)}) collective-permute-start(bf16[128,1024]{1,0:T(8,128)(2,1)S(1)} %get-tuple-element.24), channel_id=1, source_target_pairs={{0,128},{1,129},{2,130},{3,131},{4,132},{5,133},{6,134},{7,135},{8... | collective-permute-start | bytes 786440 | tf_op jit(solution)/shard_map/ppermute | solution.py:451
  235.2 4.2 %collective-permute-done.16 = bf16[128,1024]{1,0:T(8,128)(2,1)S(1)} collective-permute-done((bf16[128,1024]{1,0:T(8,128)(2,1)S(1)}, bf16[128,1024]{1,0:T(8,128)(2,1)S(1)}, u32[]{:S(2)}, u32[]{:S(2)}) %collective-permute-start.16) | collective-permute-done | bytes 262176 | tf_op jit(solution)/shard_map/ppermute | solution.py:451
  239.4 2.5 %collective-permute-done.17 = bf16[128,1024]{1,0:T(8,128)(2,1)S(1)} collective-permute-done((bf16[128,1024]{1,0:T(8,128)(2,1)S(1)}, bf16[128,1024]{1,0:T(8,128)(2,1)S(1)}, u32[]{:S(2)}, u32[]{:S(2)}) %collective-permute-start.17) | collective-permute-done | bytes 262176 | tf_op jit(solution)/shard_map/ppermute | solution.py:451
  (68 shorter events, 29.7 us)
Async XLA Ops:
  4.3 124.6 %copy-start = (s32[1,2,32]{2,1,0:T(2,128)S(1)}, s32[1,2,32]{2,1,0:T(2,128)}, u32[]{:S(2)}) copy-start(s32[1,2,32]{2,1,0:T(2,128)} %map_ref.3) | copy-start | bytes 772
  4.3 124.6 %copy-start.9 = (bf16[1,1024,32]{1,2,0:T(8,128)(2,1)S(1)}, bf16[1,1024,32]{1,2,0:T(8,128)(2,1)}, u32[]{:S(2)}) copy-start(bf16[1,1024,32]{1,2,0:T(8,128)(2,1)} %param.16) | copy-start | bytes 196612
  4.3 124.6 %copy-start.10 = (s32[1,128,2]{1,2,0:T(2,128)S(1)}, s32[1,128,2]{1,2,0:T(2,128)}, u32[]{:S(2)}) copy-start(s32[1,128,2]{1,2,0:T(2,128)} %param.14) | copy-start | bytes 3076
  4.3 124.6 %copy-start.11 = (s32[1,1,4]{2,1,0:T(1,128)S(1)}, s32[1,1,4]{2,1,0:T(1,128)}, u32[]{:S(2)}) copy-start(s32[1,1,4]{2,1,0:T(1,128)} %pages_ref.1) | copy-start | bytes 52
  90.7 9.5 %collective-permute-start.1 = (bf16[512,256]{1,0:T(8,128)(2,1)S(1)}, bf16[512,256]{1,0:T(8,128)(2,1)S(1)}, u32[]{:S(2)}, u32[]{:S(2)}) collective-permute-start(bf16[512,256]{1,0:T(8,128)(2,1)S(1)} %slice.4.refs_0_), channel_id=1, source_target_pairs={{0,8},{1,9},{2,10},{3,11},{4,12},{5,13},{6,14},{7,15},{8,16},{9,17... | collective-permute-start | bytes 786440 | tf_op jit(solution)/shard_map/ppermute | solution.py:466
  93.3 9.7 %collective-permute-start.5 = (bf16[512,256]{1,0:T(8,128)(2,1)S(1)}, bf16[512,256]{1,0:T(8,128)(2,1)S(1)}, u32[]{:S(2)}, u32[]{:S(2)}) collective-permute-start(bf16[512,256]{1,0:T(8,128)(2,1)S(1)} %slice.4.refs_0_), channel_id=1, source_target_pairs={{0,56},{1,57},{2,58},{3,59},{4,60},{5,61},{6,62},{7,63},{8,0},{9,1... | collective-permute-start | bytes 786440 | tf_op jit(solution)/shard_map/ppermute | solution.py:466
  100.2 9.5 %collective-permute-start.2 = (bf16[512,256]{1,0:T(8,128)(2,1)S(1)}, bf16[512,256]{1,0:T(8,128)(2,1)S(1)}, u32[]{:S(2)}, u32[]{:S(2)}) collective-permute-start(bf16[512,256]{1,0:T(8,128)(2,1)S(1)} %collective-permute-done.1.refs_1_), channel_id=1, source_target_pairs={{0,8},{1,9},{2,10},{3,11},{4,12},{5,13},{6,14},{7,15},{8,16},{9,17... | collective-permute-start | bytes 786440 | tf_op jit(solution)/shard_map/ppermute | solution.py:466
  103.0 11.2 %collective-permute-start.6 = (bf16[512,256]{1,0:T(8,128)(2,1)S(1)}, bf16[512,256]{1,0:T(8,128)(2,1)}, u32[]{:S(2)}, u32[]{:S(2)}) collective-permute-start(bf16[512,256]{1,0:T(8,128)(2,1)S(1)} %collective-permute-done.5.refs_5_), channel_id=1, source_target_pairs={{0,56},{1,57},{2,58},{3,59},{4,60},{5,61},{6,62},{7,63},{8,0},{9,1... | collective-permute-start | bytes 786440 | tf_op jit(solution)/shard_map/ppermute | solution.py:466
  109.6 9.7 %collective-permute-start.3 = (bf16[512,256]{1,0:T(8,128)(2,1)S(1)}, bf16[512,256]{1,0:T(8,128)(2,1)S(1)}, u32[]{:S(2)}, u32[]{:S(2)}) collective-permute-start(bf16[512,256]{1,0:T(8,128)(2,1)S(1)} %collective-permute-done.2.refs_2_), channel_id=1, source_target_pairs={{0,8},{1,9},{2,10},{3,11},{4,12},{5,13},{6,14},{7,15},{8,16},{9,17... | collective-permute-start | bytes 786440 | tf_op jit(solution)/shard_map/ppermute | solution.py:466
  112.2 44.5 %collective-permute-start.10 = (bf16[1024,512]{1,0:T(8,128)(2,1)}, bf16[1024,512]{1,0:T(8,128)(2,1)}, u32[]{:S(2)}, u32[]{:S(2)}) collective-permute-start(bf16[1024,512]{1,0:T(8,128)(2,1)} %bitcast.13), channel_id=1, source_target_pairs={{1,64},{3,66},{5,68},{7,70},{9,72},{11,74},{13,76},{15,78},{17,80}... | collective-permute-start | bytes 3145736 | tf_op jit(solution)/shard_map/ppermute | solution.py:451
  114.2 13.4 %collective-permute-start.7 = (bf16[512,256]{1,0:T(8,128)(2,1)}, bf16[512,256]{1,0:T(8,128)(2,1)}, u32[]{:S(2)}, u32[]{:S(2)}) collective-permute-start(bf16[512,256]{1,0:T(8,128)(2,1)} %collective-permute-done.6.refs_6_), channel_id=1, source_target_pairs={{0,56},{1,57},{2,58},{3,59},{4,60},{5,61},{6,62},{7,63},{8,0},{9,1... | collective-permute-start | bytes 786440 | tf_op jit(solution)/shard_map/ppermute | solution.py:466
  119.3 9.6 %collective-permute-start.4 = (bf16[512,256]{1,0:T(8,128)(2,1)S(1)}, bf16[512,256]{1,0:T(8,128)(2,1)}, u32[]{:S(2)}, u32[]{:S(2)}) collective-permute-start(bf16[512,256]{1,0:T(8,128)(2,1)S(1)} %collective-permute-done.3.refs_3_), channel_id=1, source_target_pairs={{0,8},{1,9},{2,10},{3,11},{4,12},{5,13},{6,14},{7,15},{8,16},{9,17... | collective-permute-start | bytes 786440 | tf_op jit(solution)/shard_map/ppermute | solution.py:466
  122.0 38.2 %collective-permute-start.11 = (bf16[1024,512]{1,0:T(8,128)(2,1)}, bf16[1024,512]{1,0:T(8,128)(2,1)}, u32[]{:S(2)}, u32[]{:S(2)}) collective-permute-start(bf16[1024,512]{1,0:T(8,128)(2,1)} %bitcast.14), channel_id=1, source_target_pairs={{1,64},{3,66},{5,68},{7,70},{9,72},{11,74},{13,76},{15,78},{17,80}... | collective-permute-start | bytes 3145736 | tf_op jit(solution)/shard_map/ppermute | solution.py:451
  125.3 38.6 %collective-permute-start.12 = (bf16[512,1024]{1,0:T(8,128)(2,1)}, bf16[512,1024]{1,0:T(8,128)(2,1)}, u32[]{:S(2)}, u32[]{:S(2)}) collective-permute-start(bf16[512,1024]{1,0:T(8,128)(2,1)} %bitcast.31), channel_id=1, source_target_pairs={{1,64},{3,66},{5,68},{7,70},{9,72},{11,74},{13,76},{15,78},{17,80}... | collective-permute-start | bytes 3145736 | tf_op jit(solution)/shard_map/ppermute | solution.py:451
  138.9 5.5 %collective-permute-start.9 = (bf16[128,1024]{1,0:T(8,128)(2,1)S(1)}, bf16[128,1024]{1,0:T(8,128)(2,1)S(1)}, u32[]{:S(2)}, u32[]{:S(2)}) collective-permute-start(bf16[128,1024]{1,0:T(8,128)(2,1)S(1)} %get-tuple-element.19.mine_ref), channel_id=1, source_target_pairs={{0,64},{1,65},{2,66},{3,67},{4,68},{5,69},{6,70},{7,71},{8,72},{9,... | collective-permute-start | bytes 786440 | tf_op jit(solution)/shard_map/ppermute | solution.py:451
  140.8 3.2 %collective-permute-start = (s32[2,128]{1,0:T(2,128)S(1)}, s32[2,128]{1,0:T(2,128)S(1)}, u32[]{:S(2)}, u32[]{:S(2)}) collective-permute-start(s32[2,128]{1,0:T(2,128)S(1)} %bitcast.27), channel_id=1, source_target_pairs={{0,64},{1,65},{2,66},{3,67},{4,68},{5,69},{6,70},{7,71},{8,72},{9,... | collective-permute-start | bytes 3080 | tf_op jit(solution)/shard_map/ppermute | solution.py:451
  145.8 40.7 %all-to-all-start.1 = ((bf16[64,8,1024]{2,1,0:T(8,128)(2,1)}), bf16[64,8,1024]{2,1,0:T(8,128)(2,1)S(1)}, u32[]{:S(2)}, u32[]{:S(2)}) async-start(bf16[64,8,1024]{2,1,0:T(8,128)(2,1)} %bitcast.11), calls=%async_computation.1 | async-start | bytes 2097152 | tf_op jit(solution)/shard_map/all_to_all | solution.py:461
  158.2 9.2 %collective-permute-start.13 = (bf16[1024,512]{1,0:T(8,128)(2,1)S(1)}, bf16[1024,512]{1,0:T(8,128)(2,1)S(1)}, u32[]{:S(2)}, u32[]{:S(2)}) collective-permute-start(bf16[1024,512]{1,0:T(8,128)(2,1)S(1)} %broadcast_select_fusion.2.refs_0_), channel_id=1, source_target_pairs={{0,64},{1,65},{2,66},{3,67},{4,68},{5,69},{6,70},{7,71},{8,72},{9,... | collective-permute-start | bytes 3145736 | tf_op jit(solution)/shard_map/ppermute | solution.py:451
  161.5 5.9 %collective-permute-start.14 = (bf16[1024,512]{1,0:T(8,128)(2,1)S(1)}, bf16[1024,512]{1,0:T(8,128)(2,1)S(1)}, u32[]{:S(2)}, u32[]{:S(2)}) collective-permute-start(bf16[1024,512]{1,0:T(8,128)(2,1)S(1)} %broadcast_select_fusion.1.refs_1_), channel_id=1, source_target_pairs={{0,64},{1,65},{2,66},{3,67},{4,68},{5,69},{6,70},{7,71},{8,72},{9,... | collective-permute-start | bytes 3145736 | tf_op jit(solution)/shard_map/ppermute | solution.py:451
  165.3 4.7 %collective-permute-start.15 = (bf16[512,1024]{1,0:T(8,128)(2,1)S(1)}, bf16[512,1024]{1,0:T(8,128)(2,1)}, u32[]{:S(2)}, u32[]{:S(2)}) collective-permute-start(bf16[512,1024]{1,0:T(8,128)(2,1)S(1)} %broadcast_select_fusion.refs_2_), channel_id=1, source_target_pairs={{0,64},{1,65},{2,66},{3,67},{4,68},{5,69},{6,70},{7,71},{8,72},{9,... | collective-permute-start | bytes 3145736 | tf_op jit(solution)/shard_map/ppermute | solution.py:451
  194.9 36.0 %all-to-all-start.2 = ((bf16[64,8,1024]{2,1,0:T(8,128)(2,1)}), bf16[64,8,1024]{2,1,0:T(8,128)(2,1)S(1)}, u32[]{:S(2)}, u32[]{:S(2)}) async-start(bf16[64,8,1024]{2,1,0:T(8,128)(2,1)} %bitcast.16), calls=%async_computation.2 | async-start | bytes 2097152 | tf_op jit(solution)/shard_map/all_to_all | solution.py:461
  202.2 3.1 %collective-permute-start.8 = (f32[8,128]{1,0:T(8,128)S(1)}, f32[8,128]{1,0:T(8,128)S(1)}, u32[]{:S(2)}, u32[]{:S(2)}) collective-permute-start(f32[8,128]{1,0:T(8,128)S(1)} %get-tuple-element.16.mine_ref), channel_id=1, source_target_pairs={{0,64},{1,65},{2,66},{3,67},{4,68},{5,69},{6,70},{7,71},{8,72},{9,... | collective-permute-start | bytes 12296 | tf_op jit(solution)/shard_map/ppermute | solution.py:451
  232.1 7.3 %collective-permute-start.16 = (bf16[128,1024]{1,0:T(8,128)(2,1)S(1)}, bf16[128,1024]{1,0:T(8,128)(2,1)S(1)}, u32[]{:S(2)}, u32[]{:S(2)}) collective-permute-start(bf16[128,1024]{1,0:T(8,128)(2,1)S(1)} %get-tuple-element.23), channel_id=1, source_target_pairs={{0,64},{1,65},{2,66},{3,67},{4,68},{5,69},{6,70},{7,71},{8,72},{9,... | collective-permute-start | bytes 786440 | tf_op jit(solution)/shard_map/ppermute | solution.py:451
  232.1 9.8 %collective-permute-start.17 = (bf16[128,1024]{1,0:T(8,128)(2,1)S(1)}, bf16[128,1024]{1,0:T(8,128)(2,1)S(1)}, u32[]{:S(2)}, u32[]{:S(2)}) collective-permute-start(bf16[128,1024]{1,0:T(8,128)(2,1)S(1)} %get-tuple-element.24), channel_id=1, source_target_pairs={{0,128},{1,129},{2,130},{3,131},{4,132},{5,133},{6,134},{7,135},{8... | collective-permute-start | bytes 786440 | tf_op jit(solution)/shard_map/ppermute | solution.py:451
  (16 other events, 212.7 us)

commit v6 on v4

--- a/solution.py
+++ b/solution.py
@@ -36,40 +36,58 @@
     return pl.BlockSpec(memory_space=space)
 
 
-def pack_pages_body(map_ref, rows_ref, out_ref, pick_ref):
-    @pl.when(pl.program_id(0) == 0)
-    def _():
-        device = lax.shift_right_logical(map_ref[0, 0:1, :], 5).astype(F32)
-        pages = device.shape[1]
-        rows = pages * 4
-        spread = flag(iota((pages, rows), 0) == lax.shift_right_logical(iota((pages, rows), 1), 2))
-        target = dot(jnp.broadcast_to(device, (8, pages)).astype(BF16), spread)[0:1]
-        slot = iota((pick_ref.shape[0], rows), 0)
-        row = iota((pick_ref.shape[0], rows), 1)
-        hit = (lax.shift_right_logical(slot, 3) == target.astype(jnp.int32)) & ((slot & 3) == (row & 3))
-        pick_ref[:, :rows] = flag(hit & ((slot & 4) == 0))
-        pick_ref[:, rows:] = flag(hit & ((slot & 4) == 4))
-
-    half = rows_ref.shape[1] // 2
-    both = jnp.concatenate([rows_ref[:, :half], rows_ref[:, half:]], axis=0)
-    out_ref[...] = dot(pick_ref[...], both).astype(BF16)
+def pack_pages_body(map_ref, rows_hbm, out_hbm, rows_ref, out_ref, pick_ref, sems):
+    count, width = rows_ref.shape
+    block = width // 5
+    half = block // 2
+    slots = out_ref.shape[0]
+    incoming, outgoing = [], []
+    for index in range(5):
+        part = pl.ds(index * block, block)
+        incoming.append(
+            pltpu.make_async_copy(rows_hbm.at[:, part], rows_ref.at[:, part], sems.at[index])
+        )
+        incoming[-1].start()
+    device = lax.shift_right_logical(map_ref[0, 0:1, :], 5).astype(F32)
+    pages = device.shape[1]
+    spread = flag(iota((pages, count), 0) == lax.shift_right_logical(iota((pages, count), 1), 2))
+    target = dot(jnp.broadcast_to(device, (8, pages)).astype(BF16), spread)[0:1]
+    slot = iota((slots, count), 0)
+    row = iota((slots, count), 1)
+    hit = (lax.shift_right_logical(slot, 3) == target.astype(jnp.int32)) & ((slot & 3) == (row & 3))
+    pick_ref[:, :count] = flag(hit & ((slot & 4) == 0))
+    pick_ref[:, count:] = flag(hit & ((slot & 4) == 4))
+    for index in range(5):
+        incoming[index].wait()
+        start = index * block
+        both = jnp.concatenate(
+            [rows_ref[:, start : start + half], rows_ref[:, start + half : start + block]], axis=0
+        )
+        out_ref[:, index * half : (index + 1) * half] = dot(pick_ref[...], both).astype(BF16)
+        part = pl.ds(index * half, half)
+        outgoing.append(
+            pltpu.make_async_copy(out_ref.at[:, part], out_hbm.at[:, part], sems.at[5 + index])
+        )
+        outgoing[-1].start()
+    for copy in outgoing:
+        copy.wait()
 
 
 def pack_pages(page_map, rows, devices):
     count, width = rows.shape
-    block = width // 5
     slots = devices * 8
     return pl.pallas_call(
         pack_pages_body,
         name="pack_pages",
-        grid=(5,),
-        in_specs=[
-            whole(),
-            pl.BlockSpec((count, block), lambda b: (0, b)),
+        in_specs=[whole(), whole(pl.ANY)],
+        out_specs=whole(pl.ANY),
+        out_shape=jax.ShapeDtypeStruct((slots, width // 2), BF16),
+        scratch_shapes=[
+            pltpu.VMEM((count, width), BF16),
+            pltpu.VMEM((slots, width // 2), BF16),
+            pltpu.VMEM((slots, 2 * count), BF16),
+            pltpu.SemaphoreType.DMA((10,)),
         ],
-        out_specs=pl.BlockSpec((slots, block // 2), lambda b: (0, b)),
-        out_shape=jax.ShapeDtypeStruct((slots, width // 2), BF16),
-        scratch_shapes=[pltpu.VMEM((slots, 2 * count), BF16)],
         cost_estimate=pl.CostEstimate(flops=1 << 30, bytes_accessed=4 << 20, transcendentals=0),
     )(page_map, rows)
 
@@ -282,7 +300,7 @@
 
 def expert_body(rows_hbm, *refs):
     weights_hbm = (refs[0:3], refs[3:6])
-    out_ref, rows_ref, gate_ref, up_ref, down_ref, hidden_ref, sems = refs[6:]
+    out_hbm, out_ref, rows_ref, gate_ref, up_ref, down_ref, hidden_ref, sems = refs[6:]
     units = hidden_ref.shape[1]
     chunk = units // 2
     width = out_ref.shape[1]
@@ -298,10 +316,13 @@
                 copies.append(pltpu.make_async_copy(hbm.at[:, part], ref.at[half, :, part], sem))
         sem = sems.at[1 + len(copies)]
         copies.append(pltpu.make_async_copy(down_hbm, down_ref.at[half], sem))
-    for copy in copies:
+    copies[0].start()
+    copies[1].start()
+    rows_copy.wait()
+    for copy in copies[2:]:
         copy.start()
-    rows_copy.wait()
     pending = iter(copies)
+    sent = []
     for half in range(2):
         for piece in range(2):
             part = slice(piece * chunk, (piece + 1) * chunk)
@@ -317,6 +338,13 @@
             if half == 1:
                 result = (out_ref[:, part].astype(F32) + result.astype(F32)).astype(BF16)
             out_ref[:, part] = result
+            if half == 1:
+                part = pl.ds(quarter * width // 4, width // 4)
+                sem = sems.at[11 + quarter]
+                sent.append(pltpu.make_async_copy(out_ref.at[:, part], out_hbm.at[:, part], sem))
+                sent[-1].start()
+    for copy in sent:
+        copy.wait()
 
 
 def expert_stage(rows, first, second):
@@ -326,15 +354,16 @@
         expert_body,
         name="expert_stage",
         in_specs=[whole(pl.ANY)] * 7,
-        out_specs=whole(),
+        out_specs=whole(pl.ANY),
         out_shape=jax.ShapeDtypeStruct((count, width), BF16),
         scratch_shapes=[
+            pltpu.VMEM((count, width), BF16),
             pltpu.VMEM((count, width), BF16),
             pltpu.VMEM((2, width, units), BF16),
             pltpu.VMEM((2, width, units), BF16),
             pltpu.VMEM((2, units, width), BF16),
             pltpu.VMEM((count, units), BF16),
-            pltpu.SemaphoreType.DMA((11,)),
+            pltpu.SemaphoreType.DMA((15,)),
         ],
         compiler_params=pltpu.CompilerParams(vmem_limit_bytes=50 << 20),
         cost_estimate=pl.CostEstimate(flops=4 << 30, bytes_accessed=8 << 20, transcendentals=0),

time: 243 us -> 242 us (level)
  transfers between devices with their start and end apart: 22 -> 22, of which waited for: 11 -> 11; matrix products, arithmetic and copies ran while one was open for 2% -> 2% of each run, Pallas kernels for 5% -> 4%
where the time goes in v6:
time: 242 us; the launch traced here: 241 us
  waiting for transfers between devices  117 us (48%)
  starting transfers between devices  89.9 us (37%)
  Pallas kernels  20.2 us (8%)
  local copies, waits for them, and re-layouts  9.09 us (4%)
  other arithmetic  4.94 us (2%)
    ppermute x7, waiting for transfers between devices, shifted(): lax.ppermute(shard, 'expert', [(i, (i + apart) % size) for i in range(siz...  60.5 us
    all_to_all x3, waiting for transfers between devices, exchanged(): lax.all_to_all(sent, 'expert', split_axis=0, concat_axis=0, tiled=True)  42.2 us
    all_to_all x3, starting transfers between devices, exchanged(): lax.all_to_all(sent, 'expert', split_axis=0, concat_axis=0, tiled=True)  34 us
    ppermute x11, starting transfers between devices, moved(): return lax.ppermute(shard, ('section', 'expert'), route)  23.7 us
    ppermute x7, starting transfers between devices, shifted(): lax.ppermute(shard, 'expert', [(i, (i + apart) % size) for i in range(siz...  23.1 us
    all_to_all x1, starting transfers between devices, column_block(): lax.all_to_all(copies, 'expert', split_axis=0, concat_axis=0, tiled=True,...  9.11 us
    ppermute x11, waiting for transfers between devices, moved(): return lax.ppermute(shard, ('section', 'expert'), route)  8.93 us
    pallas_call x1, Pallas kernels, expert_stage(): pl.pallas_call(expert_body, name='expert_stage', in_specs=[whole(pl.ANY)]...  8.46 us
  transfers between devices with their start and end apart: 22, of which 11 were waited for; matrix products, arithmetic and copies ran while one was open for 2% of the time, Pallas kernels for 4%

profile of v6, /device:TPU:8, one launch (start us, length us, event | category | flops | bytes accessed | tf_op | source)
XLA Modules:
  0.0 241.2 jit_solution(1532643188462892328)
XLA Ops:
  1.5 9.1 %all-to-all-start.1 = ((bf16[8,16,1024]{2,1,0:T(8,128)(2,1)}), bf16[8,16,1024]{2,1,0:T(8,128)(2,1)S(1)}, u32[]{:S(2)}, u32[]{:S(2)}) async-start(bf16[8,16,1024]{2,1,0:T(8,128)(2,1)} %broadcast_in_dim.11), calls=%async_computation.1 | async-start | bytes 524288 | tf_op jit(solution)/shard_map/all_to_all | solution.py:445
  10.6 4.0 %pack_pages.1 = bf16[512,2560]{1,0:T(8,128)(2,1)} custom-call(s32[1,2,32]{2,1,0:T(2,128)} %map_ref.3, bf16[128,5120]{1,0:T(8,128)(2,1)} %bitcast.40), custom_call_target="tpu_custom_call" | custom-call | flops 1073741824 | bytes 4194304 | tf_op jit(solution)/shard_map/pack_pages/pallas_call | solution.py:79
  14.6 5.0 %all-to-all-done.1 = bf16[8,16,1024]{2,1,0:T(8,128)(2,1)S(1)} async-done(((bf16[8,16,1024]{2,1,0:T(8,128)(2,1)}), bf16[8,16,1024]{2,1,0:T(8,128)(2,1)S(1)}, u32[]{:S(2)}, u32[]{:S(2)}) %all-to-all-start.1) | async-done | bytes 262176 | tf_op jit(solution)/shard_map/all_to_all | solution.py:445
  19.7 12.3 %all-to-all-start = ((bf16[64,8,2560]{2,1,0:T(8,128)(2,1)}), bf16[64,8,2560]{2,1,0:T(8,128)(2,1)S(1)}, u32[]{:S(2)}, u32[]{:S(2)}) async-start(bf16[64,8,2560]{2,1,0:T(8,128)(2,1)} %bitcast.32), calls=%async_computation | async-start | bytes 5242880 | tf_op jit(solution)/shard_map/all_to_all | solution.py:432
  32.0 3.4 %collective-permute-start.1 = (bf16[128,1024]{1,0:T(8,128)(2,1)S(1)}, bf16[128,1024]{1,0:T(8,128)(2,1)S(1)}, u32[]{:S(2)}, u32[]{:S(2)}) collective-permute-start(bf16[128,1024]{1,0:T(8,128)(2,1)S(1)} %bitcast.25), channel_id=1, source_target_pairs={{0,8},{1,9},{2,10},{3,11},{4,12},{5,13},{6,14},{7,15},{8,16},{9,17... | collective-permute-start | bytes 786440 | tf_op jit(solution)/shard_map/ppermute | solution.py:437
  35.3 3.7 %collective-permute-start.5 = (bf16[128,1024]{1,0:T(8,128)(2,1)S(1)}, bf16[128,1024]{1,0:T(8,128)(2,1)S(1)}, u32[]{:S(2)}, u32[]{:S(2)}) collective-permute-start(bf16[128,1024]{1,0:T(8,128)(2,1)S(1)} %bitcast.26), channel_id=1, source_target_pairs={{0,56},{1,57},{2,58},{3,59},{4,60},{5,61},{6,62},{7,63},{8,0},{9,1... | collective-permute-start | bytes 786440 | tf_op jit(solution)/shard_map/ppermute | solution.py:437
  39.0 57.2 %collective-permute-done.1.refs_1_ = bf16[128,1024]{1,0:T(8,128)(2,1)S(1)} collective-permute-done((bf16[128,1024]{1,0:T(8,128)(2,1)S(1)}, bf16[128,1024]{1,0:T(8,128)(2,1)S(1)}, u32[]{:S(2)}, u32[]{:S(2)}) %collective-permute-start.1) | collective-permute-done | bytes 262176 | tf_op jit(solution)/shard_map/ppermute | solution.py:437
  98.2 5.1 %collective-permute-start.6 = (bf16[128,1024]{1,0:T(8,128)(2,1)S(1)}, bf16[128,1024]{1,0:T(8,128)(2,1)}, u32[]{:S(2)}, u32[]{:S(2)}) collective-permute-start(bf16[128,1024]{1,0:T(8,128)(2,1)S(1)} %collective-permute-done.5.refs_5_), channel_id=1, source_target_pairs={{0,56},{1,57},{2,58},{3,59},{4,60},{5,61},{6,62},{7,63},{8,0},{9,1... | collective-permute-start | bytes 786440 | tf_op jit(solution)/shard_map/ppermute | solution.py:437
  110.3 5.1 %collective-permute-start.7 = (bf16[128,1024]{1,0:T(8,128)(2,1)}, bf16[128,1024]{1,0:T(8,128)(2,1)S(1)}, u32[]{:S(2)}, u32[]{:S(2)}) collective-permute-start(bf16[128,1024]{1,0:T(8,128)(2,1)} %collective-permute-done.6.refs_6_), channel_id=1, source_target_pairs={{0,56},{1,57},{2,58},{3,59},{4,60},{5,61},{6,62},{7,63},{8,0},{9,1... | collective-permute-start | bytes 786440 | tf_op jit(solution)/shard_map/ppermute | solution.py:437
  117.4 3.4 %collective-permute-start.11 = (bf16[1024,512]{1,0:T(8,128)(2,1)}, bf16[1024,512]{1,0:T(8,128)(2,1)}, u32[]{:S(2)}, u32[]{:S(2)}) collective-permute-start(bf16[1024,512]{1,0:T(8,128)(2,1)} %bitcast.35), channel_id=1, source_target_pairs={{1,64},{3,66},{5,68},{7,70},{9,72},{11,74},{13,76},{15,78},{17,80}... | collective-permute-start | bytes 3145736 | tf_op jit(solution)/shard_map/ppermute | solution.py:422
  120.7 2.2 collective-permute-start.12
  128.1 4.7 %token_stage.1 = (bf16[128,1024]{1,0:T(8,128)(2,1)S(1)}, bf16[128,1024]{1,0:T(8,128)(2,1)S(1)}, f32[8,128]{1,0:T(8,128)S(1)}) custom-call(s32[1,1,4]{2,1,0:T(1,128)S(1)} %copy-done.9, s32[1,1,4]{2,1,0:T(1,128)S(1)} %copy-done.10, s32[1,2,32]{2,1,0:T(2,128)S(1)} %copy-done.7, s32[2,128]{1,0:T(2,128)S(1)} %bitcast.29, bf16[32,1024]{1,0:T(8,128)(2,1)S(1)} %bitcast.28, ...), custom_call_target="tpu_custom_call" | custom-call | flops 2147483648 | bytes 6291456 | tf_op jit(solution)/shard_map/token_stage/pallas_call | solution.py:216
  133.6 2.0 collective-permute-start.9
  135.6 2.4 collective-permute-start
  140.7 14.5 %all-to-all-start.2 = ((bf16[64,8,1024]{2,1,0:T(8,128)(2,1)}), bf16[64,8,1024]{2,1,0:T(8,128)(2,1)S(1)}, u32[]{:S(2)}, u32[]{:S(2)}) async-start(bf16[64,8,1024]{2,1,0:T(8,128)(2,1)} %bitcast.12), calls=%async_computation.2 | async-start | bytes 2097152 | tf_op jit(solution)/shard_map/all_to_all | solution.py:432
  159.9 2.4 collective-permute-start.14
  163.7 2.1 collective-permute-start.15
  168.4 16.5 %all-to-all-done.2 = bf16[64,8,1024]{2,1,0:T(8,128)(2,1)S(1)} async-done(((bf16[64,8,1024]{2,1,0:T(8,128)(2,1)}), bf16[64,8,1024]{2,1,0:T(8,128)(2,1)S(1)}, u32[]{:S(2)}, u32[]{:S(2)}) %all-to-all-start.2) | async-done | bytes 1048608 | tf_op jit(solution)/shard_map/all_to_all | solution.py:432
  184.9 8.5 %expert_stage.1 = bf16[512,1024]{1,0:T(8,128)(2,1)} custom-call(bf16[512,1024]{1,0:T(8,128)(2,1)S(1)} %bitcast.23, bf16[1024,512]{1,0:T(8,128)(2,1)S(1)} %broadcast_select_fusion.2.refs_0_, bf16[1024,512]{1,0:T(8,128)(2,1)} %copy-done.15, bf16[512,1024]{1,0:T(8,128)(2,1)} %copy-done.16, bf16[1024,512]{1,0:T(8,128)(2,1)} %copy-done.17, ...), custom_call_target="tpu_custom_call" | custom-call | flops 4294967296 | bytes 8388608 | tf_op jit(solution)/shard_map/expert_stage/pallas_call | solution.py:353
  193.4 7.3 %all-to-all-start.3 = ((bf16[64,8,1024]{2,1,0:T(8,128)(2,1)}), bf16[64,8,1024]{2,1,0:T(8,128)(2,1)S(1)}, u32[]{:S(2)}, u32[]{:S(2)}) async-start(bf16[64,8,1024]{2,1,0:T(8,128)(2,1)} %bitcast.17), calls=%async_computation.3 | async-start | bytes 2097152 | tf_op jit(solution)/shard_map/all_to_all | solution.py:432
  203.7 25.7 %all-to-all-done.3 = bf16[64,8,1024]{2,1,0:T(8,128)(2,1)S(1)} async-done(((bf16[64,8,1024]{2,1,0:T(8,128)(2,1)}), bf16[64,8,1024]{2,1,0:T(8,128)(2,1)S(1)}, u32[]{:S(2)}, u32[]{:S(2)}) %all-to-all-start.3) | async-done | bytes 1048608 | tf_op jit(solution)/shard_map/all_to_all | solution.py:432
  230.6 3.4 %collective-permute-start.17 = (bf16[128,1024]{1,0:T(8,128)(2,1)S(1)}, bf16[128,1024]{1,0:T(8,128)(2,1)S(1)}, u32[]{:S(2)}, u32[]{:S(2)}) collective-permute-start(bf16[128,1024]{1,0:T(8,128)(2,1)S(1)} %get-tuple-element.24), channel_id=1, source_target_pairs={{0,128},{1,129},{2,130},{3,131},{4,132},{5,133},{6,134},{7,135},{8... | collective-permute-start | bytes 786440 | tf_op jit(solution)/shard_map/ppermute | solution.py:422
  234.0 3.9 %collective-permute-done.16 = bf16[128,1024]{1,0:T(8,128)(2,1)S(1)} collective-permute-done((bf16[128,1024]{1,0:T(8,128)(2,1)S(1)}, bf16[128,1024]{1,0:T(8,128)(2,1)S(1)}, u32[]{:S(2)}, u32[]{:S(2)}) %collective-permute-start.16) | collective-permute-done | bytes 262176 | tf_op jit(solution)/shard_map/ppermute | solution.py:422
  237.9 2.5 %collective-permute-done.17 = bf16[128,1024]{1,0:T(8,128)(2,1)S(1)} collective-permute-done((bf16[128,1024]{1,0:T(8,128)(2,1)S(1)}, bf16[128,1024]{1,0:T(8,128)(2,1)S(1)}, u32[]{:S(2)}, u32[]{:S(2)}) %collective-permute-start.17) | collective-permute-done | bytes 262176 | tf_op jit(solution)/shard_map/ppermute | solution.py:422
  (69 shorter events, 34.3 us)
Async XLA Ops:
  1.5 18.2 %all-to-all-start.1 = ((bf16[8,16,1024]{2,1,0:T(8,128)(2,1)}), bf16[8,16,1024]{2,1,0:T(8,128)(2,1)S(1)}, u32[]{:S(2)}, u32[]{:S(2)}) async-start(bf16[8,16,1024]{2,1,0:T(8,128)(2,1)} %broadcast_in_dim.11), calls=%async_computation.1 | async-start | bytes 524288 | tf_op jit(solution)/shard_map/all_to_all | solution.py:445
  19.7 105.6 %copy-start.9 = (s32[1,1,4]{2,1,0:T(1,128)S(1)}, s32[1,1,4]{2,1,0:T(1,128)}, u32[]{:S(2)}) copy-start(s32[1,1,4]{2,1,0:T(1,128)} %pages_ref.1) | copy-start | bytes 52
  19.7 105.6 %copy-start.10 = (s32[1,1,4]{2,1,0:T(1,128)S(1)}, s32[1,1,4]{2,1,0:T(1,128)}, u32[]{:S(2)}) copy-start(s32[1,1,4]{2,1,0:T(1,128)} %tails_ref.1) | copy-start | bytes 52
  19.7 105.6 %all-to-all-start = ((bf16[64,8,2560]{2,1,0:T(8,128)(2,1)}), bf16[64,8,2560]{2,1,0:T(8,128)(2,1)S(1)}, u32[]{:S(2)}, u32[]{:S(2)}) async-start(bf16[64,8,2560]{2,1,0:T(8,128)(2,1)} %bitcast.32), calls=%async_computation | async-start | bytes 5242880 | tf_op jit(solution)/shard_map/all_to_all | solution.py:432
  32.0 64.3 %collective-permute-start.1 = (bf16[128,1024]{1,0:T(8,128)(2,1)S(1)}, bf16[128,1024]{1,0:T(8,128)(2,1)S(1)}, u32[]{:S(2)}, u32[]{:S(2)}) collective-permute-start(bf16[128,1024]{1,0:T(8,128)(2,1)S(1)} %bitcast.25), channel_id=1, source_target_pairs={{0,8},{1,9},{2,10},{3,11},{4,12},{5,13},{6,14},{7,15},{8,16},{9,17... | collective-permute-start | bytes 786440 | tf_op jit(solution)/shard_map/ppermute | solution.py:437
  35.3 62.8 %collective-permute-start.5 = (bf16[128,1024]{1,0:T(8,128)(2,1)S(1)}, bf16[128,1024]{1,0:T(8,128)(2,1)S(1)}, u32[]{:S(2)}, u32[]{:S(2)}) collective-permute-start(bf16[128,1024]{1,0:T(8,128)(2,1)S(1)} %bitcast.26), channel_id=1, source_target_pairs={{0,56},{1,57},{2,58},{3,59},{4,60},{5,61},{6,62},{7,63},{8,0},{9,1... | collective-permute-start | bytes 786440 | tf_op jit(solution)/shard_map/ppermute | solution.py:437
  96.3 9.5 %collective-permute-start.2 = (bf16[128,1024]{1,0:T(8,128)(2,1)S(1)}, bf16[128,1024]{1,0:T(8,128)(2,1)S(1)}, u32[]{:S(2)}, u32[]{:S(2)}) collective-permute-start(bf16[128,1024]{1,0:T(8,128)(2,1)S(1)} %collective-permute-done.1.refs_1_), channel_id=1, source_target_pairs={{0,8},{1,9},{2,10},{3,11},{4,12},{5,13},{6,14},{7,15},{8,16},{9,17... | collective-permute-start | bytes 786440 | tf_op jit(solution)/shard_map/ppermute | solution.py:437
  98.2 12.1 %collective-permute-start.6 = (bf16[128,1024]{1,0:T(8,128)(2,1)S(1)}, bf16[128,1024]{1,0:T(8,128)(2,1)}, u32[]{:S(2)}, u32[]{:S(2)}) collective-permute-start(bf16[128,1024]{1,0:T(8,128)(2,1)S(1)} %collective-permute-done.5.refs_5_), channel_id=1, source_target_pairs={{0,56},{1,57},{2,58},{3,59},{4,60},{5,61},{6,62},{7,63},{8,0},{9,1... | collective-permute-start | bytes 786440 | tf_op jit(solution)/shard_map/ppermute | solution.py:437
  105.7 9.7 %collective-permute-start.3 = (bf16[128,1024]{1,0:T(8,128)(2,1)S(1)}, bf16[128,1024]{1,0:T(8,128)(2,1)}, u32[]{:S(2)}, u32[]{:S(2)}) collective-permute-start(bf16[128,1024]{1,0:T(8,128)(2,1)S(1)} %collective-permute-done.2.refs_2_), channel_id=1, source_target_pairs={{0,8},{1,9},{2,10},{3,11},{4,12},{5,13},{6,14},{7,15},{8,16},{9,17... | collective-permute-start | bytes 786440 | tf_op jit(solution)/shard_map/ppermute | solution.py:437
  108.4 46.8 %collective-permute-start.10 = (bf16[1024,512]{1,0:T(8,128)(2,1)}, bf16[1024,512]{1,0:T(8,128)(2,1)}, u32[]{:S(2)}, u32[]{:S(2)}) collective-permute-start(bf16[1024,512]{1,0:T(8,128)(2,1)} %bitcast.33), channel_id=1, source_target_pairs={{1,64},{3,66},{5,68},{7,70},{9,72},{11,74},{13,76},{15,78},{17,80}... | collective-permute-start | bytes 3145736 | tf_op jit(solution)/shard_map/ppermute | solution.py:422
  110.3 12.7 %collective-permute-start.7 = (bf16[128,1024]{1,0:T(8,128)(2,1)}, bf16[128,1024]{1,0:T(8,128)(2,1)S(1)}, u32[]{:S(2)}, u32[]{:S(2)}) collective-permute-start(bf16[128,1024]{1,0:T(8,128)(2,1)} %collective-permute-done.6.refs_6_), channel_id=1, source_target_pairs={{0,56},{1,57},{2,58},{3,59},{4,60},{5,61},{6,62},{7,63},{8,0},{9,1... | collective-permute-start | bytes 786440 | tf_op jit(solution)/shard_map/ppermute | solution.py:437
  115.4 9.8 %collective-permute-start.4 = (bf16[128,1024]{1,0:T(8,128)(2,1)}, bf16[128,1024]{1,0:T(8,128)(2,1)}, u32[]{:S(2)}, u32[]{:S(2)}) collective-permute-start(bf16[128,1024]{1,0:T(8,128)(2,1)} %collective-permute-done.3.refs_3_), channel_id=1, source_target_pairs={{0,8},{1,9},{2,10},{3,11},{4,12},{5,13},{6,14},{7,15},{8,16},{9,17... | collective-permute-start | bytes 786440 | tf_op jit(solution)/shard_map/ppermute | solution.py:437
  117.4 41.2 %collective-permute-start.11 = (bf16[1024,512]{1,0:T(8,128)(2,1)}, bf16[1024,512]{1,0:T(8,128)(2,1)}, u32[]{:S(2)}, u32[]{:S(2)}) collective-permute-start(bf16[1024,512]{1,0:T(8,128)(2,1)} %bitcast.35), channel_id=1, source_target_pairs={{1,64},{3,66},{5,68},{7,70},{9,72},{11,74},{13,76},{15,78},{17,80}... | collective-permute-start | bytes 3145736 | tf_op jit(solution)/shard_map/ppermute | solution.py:422
  120.7 41.6 %collective-permute-start.12 = (bf16[512,1024]{1,0:T(8,128)(2,1)}, bf16[512,1024]{1,0:T(8,128)(2,1)}, u32[]{:S(2)}, u32[]{:S(2)}) collective-permute-start(bf16[512,1024]{1,0:T(8,128)(2,1)} %bitcast.37), channel_id=1, source_target_pairs={{1,64},{3,66},{5,68},{7,70},{9,72},{11,74},{13,76},{15,78},{17,80}... | collective-permute-start | bytes 3145736 | tf_op jit(solution)/shard_map/ppermute | solution.py:422
  133.6 5.6 %collective-permute-start.9 = (bf16[128,1024]{1,0:T(8,128)(2,1)S(1)}, bf16[128,1024]{1,0:T(8,128)(2,1)S(1)}, u32[]{:S(2)}, u32[]{:S(2)}) collective-permute-start(bf16[128,1024]{1,0:T(8,128)(2,1)S(1)} %get-tuple-element.19.mine_ref), channel_id=1, source_target_pairs={{0,64},{1,65},{2,66},{3,67},{4,68},{5,69},{6,70},{7,71},{8,72},{9,... | collective-permute-start | bytes 786440 | tf_op jit(solution)/shard_map/ppermute | solution.py:422
  135.6 3.2 %collective-permute-start = (s32[2,128]{1,0:T(2,128)S(1)}, s32[2,128]{1,0:T(2,128)S(1)}, u32[]{:S(2)}, u32[]{:S(2)}) collective-permute-start(s32[2,128]{1,0:T(2,128)S(1)} %bitcast.30), channel_id=1, source_target_pairs={{0,64},{1,65},{2,66},{3,67},{4,68},{5,69},{6,70},{7,71},{8,72},{9,... | collective-permute-start | bytes 3080 | tf_op jit(solution)/shard_map/ppermute | solution.py:422
  140.7 44.2 %all-to-all-start.2 = ((bf16[64,8,1024]{2,1,0:T(8,128)(2,1)}), bf16[64,8,1024]{2,1,0:T(8,128)(2,1)S(1)}, u32[]{:S(2)}, u32[]{:S(2)}) async-start(bf16[64,8,1024]{2,1,0:T(8,128)(2,1)} %bitcast.12), calls=%async_computation.2 | async-start | bytes 2097152 | tf_op jit(solution)/shard_map/all_to_all | solution.py:432
  156.6 9.2 %collective-permute-start.13 = (bf16[1024,512]{1,0:T(8,128)(2,1)S(1)}, bf16[1024,512]{1,0:T(8,128)(2,1)S(1)}, u32[]{:S(2)}, u32[]{:S(2)}) collective-permute-start(bf16[1024,512]{1,0:T(8,128)(2,1)S(1)} %broadcast_select_fusion.2.refs_0_), channel_id=1, source_target_pairs={{0,64},{1,65},{2,66},{3,67},{4,68},{5,69},{6,70},{7,71},{8,72},{9,... | collective-permute-start | bytes 3145736 | tf_op jit(solution)/shard_map/ppermute | solution.py:422
  159.9 5.9 %collective-permute-start.14 = (bf16[1024,512]{1,0:T(8,128)(2,1)S(1)}, bf16[1024,512]{1,0:T(8,128)(2,1)S(1)}, u32[]{:S(2)}, u32[]{:S(2)}) collective-permute-start(bf16[1024,512]{1,0:T(8,128)(2,1)S(1)} %broadcast_select_fusion.1.refs_1_), channel_id=1, source_target_pairs={{0,64},{1,65},{2,66},{3,67},{4,68},{5,69},{6,70},{7,71},{8,72},{9,... | collective-permute-start | bytes 3145736 | tf_op jit(solution)/shard_map/ppermute | solution.py:422
  163.7 4.7 %collective-permute-start.15 = (bf16[512,1024]{1,0:T(8,128)(2,1)S(1)}, bf16[512,1024]{1,0:T(8,128)(2,1)}, u32[]{:S(2)}, u32[]{:S(2)}) collective-permute-start(bf16[512,1024]{1,0:T(8,128)(2,1)S(1)} %broadcast_select_fusion.refs_2_), channel_id=1, source_target_pairs={{0,64},{1,65},{2,66},{3,67},{4,68},{5,69},{6,70},{7,71},{8,72},{9,... | collective-permute-start | bytes 3145736 | tf_op jit(solution)/shard_map/ppermute | solution.py:422
  193.4 36.0 %all-to-all-start.3 = ((bf16[64,8,1024]{2,1,0:T(8,128)(2,1)}), bf16[64,8,1024]{2,1,0:T(8,128)(2,1)S(1)}, u32[]{:S(2)}, u32[]{:S(2)}) async-start(bf16[64,8,1024]{2,1,0:T(8,128)(2,1)} %bitcast.17), calls=%async_computation.3 | async-start | bytes 2097152 | tf_op jit(solution)/shard_map/all_to_all | solution.py:432
  200.7 3.1 %collective-permute-start.8 = (f32[8,128]{1,0:T(8,128)S(1)}, f32[8,128]{1,0:T(8,128)S(1)}, u32[]{:S(2)}, u32[]{:S(2)}) collective-permute-start(f32[8,128]{1,0:T(8,128)S(1)} %get-tuple-element.16.mine_ref), channel_id=1, source_target_pairs={{0,64},{1,65},{2,66},{3,67},{4,68},{5,69},{6,70},{7,71},{8,72},{9,... | collective-permute-start | bytes 12296 | tf_op jit(solution)/shard_map/ppermute | solution.py:422
  230.6 7.3 %collective-permute-start.16 = (bf16[128,1024]{1,0:T(8,128)(2,1)S(1)}, bf16[128,1024]{1,0:T(8,128)(2,1)S(1)}, u32[]{:S(2)}, u32[]{:S(2)}) collective-permute-start(bf16[128,1024]{1,0:T(8,128)(2,1)S(1)} %get-tuple-element.23), channel_id=1, source_target_pairs={{0,64},{1,65},{2,66},{3,67},{4,68},{5,69},{6,70},{7,71},{8,72},{9,... | collective-permute-start | bytes 786440 | tf_op jit(solution)/shard_map/ppermute | solution.py:422
  230.6 9.8 %collective-permute-start.17 = (bf16[128,1024]{1,0:T(8,128)(2,1)S(1)}, bf16[128,1024]{1,0:T(8,128)(2,1)S(1)}, u32[]{:S(2)}, u32[]{:S(2)}) collective-permute-start(bf16[128,1024]{1,0:T(8,128)(2,1)S(1)} %get-tuple-element.24), channel_id=1, source_target_pairs={{0,128},{1,129},{2,130},{3,131},{4,132},{5,133},{6,134},{7,135},{8... | collective-permute-start | bytes 786440 | tf_op jit(solution)/shard_map/ppermute | solution.py:422
  (17 other events, 424.8 us)
